TPU v7x, 32 devices: a whole 2x2x4 slice. The times are simulated.
32 devices in a mesh: row: 16 (over z, y, x), col: 2 (over core).
Axes of the slice: x: 2, y: 2, z: 4, core: 2. Of those that a mesh axis runs over, the one named last changes fastest.
Arguments:
- hidden_in: bfloat16 [8192, 1536], P(('row', 'col')), may hold values from -6 to 6
- segments: int32 [16, 512], P('row'), may hold values from 0 to 3, never falling along the last dimension, each value on 1 to 256 neighbouring positions
- routes: int32 [8192, 4], P('row'), may hold values from 0 to 31, all different within a row; in each aligned block of 512 rows (0 to 511, 512 to 1023, ...) at most 96 rows name the same one
- attention_gain: bfloat16 [1536], P('row'), may hold values from 0.099609375 to 1.8984375
- query_weight: bfloat16 [1536, 1536], P('row', 'col'), may hold values from -0.15625 to 0.15625
- key_matrix: bfloat16 [1536, 256], P('row', 'col'), may hold values from -0.15625 to 0.15625
- value_matrix: bfloat16 [1536, 256], P('row', 'col'), may hold values from -0.15625 to 0.15625
- output_weight: bfloat16 [1536, 1536], P('col', 'row'), may hold values from -1.5 to 1.5
- expert_gain: bfloat16 [1536], P('row'), may hold values from 0.099609375 to 1.8984375
- router_weight: bfloat16 [1536, 32], P('row'), may hold values from -0.078125 to 0.078125
- gate_weight: bfloat16 [32, 1536, 768], P(None, 'row', 'col'), may hold values from -0.15625 to 0.15625
- up_weight: bfloat16 [32, 1536, 768], P(None, 'row', 'col'), may hold values from -0.15625 to 0.15625
- down_weight: bfloat16 [32, 768, 1536], P(None, 'col', 'row'), may hold values from -0.4375 to 0.4375
- cotangent: bfloat16 [8192, 1536], P(('row', 'col')), may hold values from -6 to 6
Outputs:
- block_out: bfloat16 [8192, 1536], P(('row', 'col'))
- input_grad: float32 [8192, 1536], P(('row', 'col'))
- attention_gain_grad: float32 [1536], P('row')
- query_weight_grad: float32 [1536, 1536], P('row', 'col')
- key_weight_grad: float32 [1536, 256], P('row', 'col')
- value_weight_grad: float32 [1536, 256], P('row', 'col')
- output_weight_grad: float32 [1536, 1536], P('col', 'row')
- expert_gain_grad: float32 [1536], P('row')
- router_weight_grad: float32 [1536, 32], P('row')
- gate_weight_grad: float32 [32, 1536, 768], P(None, 'row', 'col')
- up_weight_grad: float32 [32, 1536, 768], P(None, 'row', 'col')
- down_weight_grad: float32 [32, 768, 1536], P(None, 'col', 'row')
Inputs may be any that keep to these rules, and one draw needn't show every extreme that they name: Each row of segments numbers the documents of one packed sequence from 0 without falling; a document is one run of positions of at most 256. `routes`: each row names 4 different experts. Among the 512 rows of one sequence no expert is named more than 96 times, a bound that some block reaches.
All inputs are finite; a program needn't handle non-finite values.
Results may differ from a plain program's by a relative error of at most 0.02.
Values may be sent and summed in bfloat16 or wider, within the bound.
No kernel may reach another device: no remote copies, remote signals or barrier semaphores. Data moves between devices by JAX's collectives and lax.ppermute only.
A program may use at most 448 MiB of HBM per device.

v0:
```python
import jax
import jax.numpy as jnp
from jax import lax
from jax.sharding import PartitionSpec as P

MODEL_WIDTH = 1536
QUERY_HEADS = 12
KEY_VALUE_HEADS = 2
HEAD_SIZE = 128
E = 32
TOPK = 4


EPSILON = 1e-06
ROPE_BASE = 1000000.0
MASKED = -1e30


def positions(segment_ids):
    total_length = segment_ids.shape[0]
    token_index = jnp.arange(total_length, dtype=jnp.int32)
    change = jnp.concatenate([jnp.ones((1,), jnp.bool_), segment_ids[1:] != segment_ids[:-1]])
    first_index = lax.cummax(jnp.where(change, token_index, 0), axis=0)
    return token_index - first_index


def apply_rotary(values, places, direction):
    half_size = values.shape[-1] // 2
    frequency = ROPE_BASE ** (-2.0 * jnp.arange(half_size, dtype=jnp.float32) / values.shape[-1])
    angles = places.astype(jnp.float32)[:, None] * frequency[None, :]
    cosine_part = jnp.cos(angles)[:, None, :]
    sine_part = direction * jnp.sin(angles)[:, None, :]
    first_half = values[..., :half_size]
    second_half = values[..., half_size:]
    return jnp.concatenate(
        [
            first_half * cosine_part - second_half * sine_part,
            second_half * cosine_part + first_half * sine_part,
        ],
        axis=-1,
    )


def slot_tables(route_ids, experts, capacity):
    flat_ids = route_ids.reshape(-1)
    expert_ids = jnp.arange(experts, dtype=jnp.int32)
    onehot = (flat_ids[:, None] == expert_ids[None, :]).astype(jnp.int32)
    rank_ids = jnp.sum(
        (jnp.cumsum(onehot, axis=0, dtype=jnp.int32) - 1) * onehot, axis=1, dtype=jnp.int32
    )
    pair_slot = flat_ids * capacity + rank_ids
    owners = jnp.arange(flat_ids.shape[0], dtype=jnp.int32) // route_ids.shape[1]
    token_of = jnp.zeros((experts * capacity,), jnp.int32).at[pair_slot].set(owners)
    filled = jnp.zeros((experts * capacity,), jnp.int32).at[pair_slot].set(1)
    return (pair_slot, token_of, filled)


def masked_scores(queries, key_row_block, allowed, scaling):
    scores = (
        jnp.einsum("gqd,kd->gqk", queries, key_row_block, preferred_element_type=jnp.float32)
        * scaling
    )
    return jnp.where(allowed[None], scores, MASKED)


def attend_group(operands, allowed, scaling):
    queries, key_row_block, value_row_block = operands
    scores = masked_scores(queries, key_row_block, allowed, scaling)
    highest = jnp.max(scores, axis=-1, keepdims=True)
    exponent = jnp.exp(scores - highest)
    summed = jnp.sum(exponent, axis=-1, keepdims=True)
    weights_low = (exponent / summed).astype(jnp.bfloat16)
    result = jnp.einsum(
        "gqk,kd->gqd", weights_low, value_row_block, preferred_element_type=jnp.float32
    )
    return (result, highest + jnp.log(summed))


def attend_back(operands, allowed, scaling):
    queries, key_row_block, value_row_block, log_total, grad_result = operands
    scores = masked_scores(queries, key_row_block, allowed, scaling)
    weights_full = jnp.where(allowed[None], jnp.exp(scores - log_total), 0.0)
    weights_low = weights_full.astype(jnp.bfloat16)
    grad_values = jnp.einsum(
        "gqk,gqd->kd", weights_low, grad_result, preferred_element_type=jnp.float32
    )
    grad_weights = jnp.einsum(
        "gqd,kd->gqk", grad_result, value_row_block, preferred_element_type=jnp.float32
    )
    centre = jnp.sum(weights_full * grad_weights, axis=-1, keepdims=True)
    grad_scores = (weights_full * (grad_weights - centre)).astype(jnp.bfloat16)
    grad_queries = (
        jnp.einsum("gqk,kd->gqd", grad_scores, key_row_block, preferred_element_type=jnp.float32)
        * scaling
    )
    grad_keys = (
        jnp.einsum("gqk,gqd->kd", grad_scores, queries, preferred_element_type=jnp.float32)
        * scaling
    )
    return (grad_queries, grad_keys, grad_values)


def per_device(
    hidden_in,
    segments,
    routes,
    attention_gain,
    query_weight,
    key_matrix,
    value_matrix,
    output_weight,
    expert_gain,
    router_weight,
    gate_weight,
    up_weight,
    down_weight,
    cotangent,
):
    gain_first, query_cols, key_cols, value_cols, output_rows = (
        lax.all_gather(attention_gain, "row", axis=0, tiled=True),
        lax.all_gather(query_weight, "row", axis=0, tiled=True),
        lax.all_gather(key_matrix, "row", axis=0, tiled=True),
        lax.all_gather(value_matrix, "row", axis=0, tiled=True),
        lax.all_gather(output_weight, "row", axis=1, tiled=True),
    )
    query_full, gathered_keys, gathered_values, output_full = (
        lax.all_gather(query_cols, "col", axis=1, tiled=True),
        lax.all_gather(key_cols, "col", axis=1, tiled=True),
        lax.all_gather(value_cols, "col", axis=1, tiled=True),
        lax.all_gather(output_rows, "col", axis=0, tiled=True),
    )
    gain_second, router_full, gate_full, up_full, down_full = (
        lax.all_gather(expert_gain, "row", axis=0, tiled=True),
        lax.all_gather(router_weight, "row", axis=0, tiled=True),
        lax.all_gather(gate_weight, "row", axis=1, tiled=True),
        lax.all_gather(up_weight, "row", axis=1, tiled=True),
        lax.all_gather(down_weight, "row", axis=2, tiled=True),
    )
    local_row_block = hidden_in.shape[0]
    sequence_span_length = segments.shape[1]
    first_row = lax.axis_index("col") * local_row_block
    segment_ids = segments[0]
    places_all = positions(segment_ids)
    local_positions = lax.dynamic_slice_in_dim(places_all, first_row, local_row_block)
    own_segments = lax.dynamic_slice_in_dim(segment_ids, first_row, local_row_block)
    query_index = first_row + jnp.arange(local_row_block, dtype=jnp.int32)
    key_index = jnp.arange(sequence_span_length, dtype=jnp.int32)
    allowed = (own_segments[:, None] == segment_ids[None, :]) & (
        key_index[None, :] <= query_index[:, None]
    )
    tokens_in = hidden_in.astype(jnp.float32)
    scale_first = lax.rsqrt(jnp.mean(tokens_in * tokens_in, axis=-1, keepdims=True) + EPSILON)
    unit_first = tokens_in * scale_first
    normed_first = (unit_first * gain_first.astype(jnp.float32)).astype(jnp.bfloat16)
    query_raw = jnp.dot(normed_first, query_full, preferred_element_type=jnp.float32).reshape(
        local_row_block, QUERY_HEADS, HEAD_SIZE
    )
    unrotated_keys = jnp.dot(
        normed_first, gathered_keys, preferred_element_type=jnp.float32
    ).reshape(local_row_block, KEY_VALUE_HEADS, HEAD_SIZE)
    values_reduced = jnp.dot(
        normed_first, gathered_values, preferred_element_type=jnp.float32
    ).astype(jnp.bfloat16)
    rotated_queries = apply_rotary(query_raw, local_positions, 1.0).astype(jnp.bfloat16)
    rotated_keys = (
        apply_rotary(unrotated_keys, local_positions, 1.0)
        .astype(jnp.bfloat16)
        .reshape(local_row_block, KEY_VALUE_HEADS * HEAD_SIZE)
    )
    key_row_block, value_row_block = (
        lax.all_gather(rotated_keys, "col", axis=0, tiled=True),
        lax.all_gather(values_reduced, "col", axis=0, tiled=True),
    )
    heads_per_group = QUERY_HEADS // KEY_VALUE_HEADS
    scaling = HEAD_SIZE ** (-0.5)
    grouped_queries = rotated_queries.reshape(
        local_row_block, KEY_VALUE_HEADS, heads_per_group, HEAD_SIZE
    ).transpose(1, 2, 0, 3)
    grouped_keys = key_row_block.reshape(
        sequence_span_length, KEY_VALUE_HEADS, HEAD_SIZE
    ).transpose(1, 0, 2)
    grouped_values = value_row_block.reshape(
        sequence_span_length, KEY_VALUE_HEADS, HEAD_SIZE
    ).transpose(1, 0, 2)
    attended, log_total = lax.map(
        lambda operands: attend_group(operands, allowed, scaling),
        (grouped_queries, grouped_keys, grouped_values),
    )
    attended_low = (
        attended.transpose(2, 0, 1, 3)
        .reshape(local_row_block, QUERY_HEADS * HEAD_SIZE)
        .astype(jnp.bfloat16)
    )
    branch = jnp.dot(attended_low, output_full, preferred_element_type=jnp.float32)
    hidden_mid = tokens_in + branch
    scale_second = lax.rsqrt(jnp.mean(hidden_mid * hidden_mid, axis=-1, keepdims=True) + EPSILON)
    unit_second = hidden_mid * scale_second
    normed_second = (unit_second * gain_second.astype(jnp.float32)).astype(jnp.bfloat16)
    normed_all, upstream_all = (
        lax.all_gather(normed_second, "col", axis=0, tiled=True),
        lax.all_gather(cotangent, "col", axis=0, tiled=True),
    )
    logits = jnp.dot(normed_all, router_full, preferred_element_type=jnp.float32)
    expert_ids = jnp.arange(E, dtype=jnp.int32)
    chosen_mask = routes[:, :, None] == expert_ids[None, None, :]
    chosen = jnp.sum(jnp.where(chosen_mask, logits[:, None, :], 0.0), axis=-1)
    exponent = jnp.exp(chosen - jnp.max(chosen, axis=-1, keepdims=True))
    route_gates = exponent / jnp.sum(exponent, axis=-1, keepdims=True)
    group_width = 4
    capacity = max(2, 3 * sequence_span_length * TOPK // (2 * E))
    pair_slot, token_of, filled = slot_tables(routes, E, capacity)
    slot_gate = jnp.zeros((E * capacity,), jnp.float32).at[pair_slot].set(route_gates.reshape(-1))
    group_rows = group_width * capacity

    def expert_step(accumulated, group_index):
        mixture_sum, input_sum = accumulated
        offset = group_index * group_rows
        row_ids = lax.dynamic_slice_in_dim(token_of, offset, group_rows)
        occupied = lax.dynamic_slice_in_dim(filled, offset, group_rows) > 0
        slot_weight = lax.dynamic_slice_in_dim(slot_gate, offset, group_rows)
        first_expert = group_index * group_width
        gate_block = lax.dynamic_slice_in_dim(gate_full, first_expert, group_width, 0)
        up_block = lax.dynamic_slice_in_dim(up_full, first_expert, group_width, 0)
        down_block = lax.dynamic_slice_in_dim(down_full, first_expert, group_width, 0)
        inputs = jnp.where(
            occupied[:, None], normed_all[row_ids], jnp.zeros((), jnp.bfloat16)
        ).reshape(group_width, capacity, MODEL_WIDTH)
        upstream = upstream_all[row_ids].astype(jnp.float32)
        gate_value = jnp.einsum(
            "ecd,edf->ecf", inputs, gate_block, preferred_element_type=jnp.float32
        )
        up_value = jnp.einsum("ecd,edf->ecf", inputs, up_block, preferred_element_type=jnp.float32)
        sigmoid_gate = jax.nn.sigmoid(gate_value)
        silu_gate = gate_value * sigmoid_gate
        activation = (silu_gate * up_value).astype(jnp.bfloat16)
        partial_out = jnp.einsum(
            "ecf,efd->ecd", activation, down_block, preferred_element_type=jnp.float32
        ).reshape(group_rows, MODEL_WIDTH)
        mixture_sum = mixture_sum.at[row_ids].add(partial_out * slot_weight[:, None])
        slot_grad = jnp.sum(partial_out * upstream, axis=-1)
        grad_expert = (
            (upstream * slot_weight[:, None])
            .astype(jnp.bfloat16)
            .reshape(group_width, capacity, MODEL_WIDTH)
        )
        grad_act = jnp.einsum(
            "ecd,efd->ecf", grad_expert, down_block, preferred_element_type=jnp.float32
        )
        slope = sigmoid_gate * (1.0 + gate_value * (1.0 - sigmoid_gate))
        grad_gate = (grad_act * up_value * slope).astype(jnp.bfloat16)
        grad_up = (grad_act * silu_gate).astype(jnp.bfloat16)
        grad_inputs = jnp.einsum(
            "ecf,edf->ecd", grad_gate, gate_block, preferred_element_type=jnp.float32
        )
        grad_inputs = grad_inputs + jnp.einsum(
            "ecf,edf->ecd", grad_up, up_block, preferred_element_type=jnp.float32
        )
        input_sum = input_sum.at[row_ids].add(grad_inputs.reshape(group_rows, MODEL_WIDTH))
        gate_piece = jnp.einsum(
            "ecd,ecf->edf", inputs, grad_gate, preferred_element_type=jnp.float32
        )
        up_piece = jnp.einsum("ecd,ecf->edf", inputs, grad_up, preferred_element_type=jnp.float32)
        down_piece = jnp.einsum(
            "ecf,ecd->efd", activation, grad_expert, preferred_element_type=jnp.float32
        )
        return ((mixture_sum, input_sum), (slot_grad, gate_piece, up_piece, down_piece))

    initial = (
        jnp.zeros((sequence_span_length, MODEL_WIDTH), jnp.float32),
        jnp.zeros((sequence_span_length, MODEL_WIDTH), jnp.float32),
    )
    sums_out, pieces = lax.scan(expert_step, initial, jnp.arange(E // group_width, dtype=jnp.int32))
    mixture_part, input_part = sums_out
    slot_grads, gate_pieces, up_pieces, down_pieces = pieces
    hidden_cols = gate_full.shape[2]
    gate_grad = gate_pieces.reshape(E, MODEL_WIDTH, hidden_cols)
    up_grad = up_pieces.reshape(E, MODEL_WIDTH, hidden_cols)
    down_grad = down_pieces.reshape(E, hidden_cols, MODEL_WIDTH)
    pick_grads = slot_grads.reshape(-1)[pair_slot].reshape(sequence_span_length, TOPK)
    mixture_own, input_own, pick_own = (
        lax.psum_scatter(mixture_part, "col", scatter_dimension=0, tiled=True),
        lax.psum_scatter(input_part, "col", scatter_dimension=0, tiled=True),
        lax.psum_scatter(pick_grads, "col", scatter_dimension=0, tiled=True),
    )
    block_out = (hidden_mid + mixture_own).astype(jnp.bfloat16)
    own_gates = lax.dynamic_slice_in_dim(route_gates, first_row, local_row_block)
    own_mask = lax.dynamic_slice_in_dim(chosen_mask, first_row, local_row_block)
    centred = own_gates * (pick_own - jnp.sum(own_gates * pick_own, axis=-1, keepdims=True))
    grad_logits = jnp.sum(jnp.where(own_mask, centred[:, :, None], 0.0), axis=1).astype(
        jnp.bfloat16
    )
    grad_normed = input_own + jnp.dot(
        grad_logits, router_full.T, preferred_element_type=jnp.float32
    )
    router_grad = jnp.dot(normed_second.T, grad_logits, preferred_element_type=jnp.float32)
    tilted_second = grad_normed * gain_second.astype(jnp.float32)
    gain_second_grad = jnp.sum(grad_normed * unit_second, axis=0)
    grad_hidden = cotangent.astype(jnp.float32) + scale_second * (
        tilted_second - unit_second * jnp.mean(tilted_second * unit_second, axis=-1, keepdims=True)
    )
    grad_branch = grad_hidden.astype(jnp.bfloat16)
    output_grad = jnp.dot(attended_low.T, grad_branch, preferred_element_type=jnp.float32)
    attended_gradient = jnp.dot(
        grad_branch, output_full.T, preferred_element_type=jnp.float32
    ).astype(jnp.bfloat16)
    grouped_gradient = attended_gradient.reshape(
        local_row_block, KEY_VALUE_HEADS, heads_per_group, HEAD_SIZE
    ).transpose(1, 2, 0, 3)
    grad_query_groups, key_gradient_grouped, value_gradient_grouped = lax.map(
        lambda operands: attend_back(operands, allowed, scaling),
        (grouped_queries, grouped_keys, grouped_values, log_total, grouped_gradient),
    )
    grad_query_rot = grad_query_groups.transpose(2, 0, 1, 3).reshape(
        local_row_block, QUERY_HEADS, HEAD_SIZE
    )
    key_gradient_total = key_gradient_grouped.transpose(1, 0, 2).reshape(
        sequence_span_length, KEY_VALUE_HEADS * HEAD_SIZE
    )
    value_gradient_total = value_gradient_grouped.transpose(1, 0, 2).reshape(
        sequence_span_length, KEY_VALUE_HEADS * HEAD_SIZE
    )
    local_keys, value_own = (
        lax.psum_scatter(
            key_gradient_total.astype(jnp.bfloat16), "col", scatter_dimension=0, tiled=True
        ).astype(jnp.float32),
        lax.psum_scatter(
            value_gradient_total.astype(jnp.bfloat16), "col", scatter_dimension=0, tiled=True
        ).astype(jnp.float32),
    )
    grad_query_low = (
        apply_rotary(grad_query_rot, local_positions, -1.0)
        .reshape(local_row_block, QUERY_HEADS * HEAD_SIZE)
        .astype(jnp.bfloat16)
    )
    grad_key_low = (
        apply_rotary(
            local_keys.reshape(local_row_block, KEY_VALUE_HEADS, HEAD_SIZE), local_positions, -1.0
        )
        .reshape(local_row_block, KEY_VALUE_HEADS * HEAD_SIZE)
        .astype(jnp.bfloat16)
    )
    grad_value_low = value_own.astype(jnp.bfloat16)
    grad_normed_first = jnp.dot(grad_query_low, query_full.T, preferred_element_type=jnp.float32)
    grad_normed_first = grad_normed_first + jnp.dot(
        grad_key_low, gathered_keys.T, preferred_element_type=jnp.float32
    )
    grad_normed_first = grad_normed_first + jnp.dot(
        grad_value_low, gathered_values.T, preferred_element_type=jnp.float32
    )
    query_grad = jnp.dot(normed_first.T, grad_query_low, preferred_element_type=jnp.float32)
    key_grad = jnp.dot(normed_first.T, grad_key_low, preferred_element_type=jnp.float32)
    value_grad = jnp.dot(normed_first.T, grad_value_low, preferred_element_type=jnp.float32)
    tilted_first = grad_normed_first * gain_first.astype(jnp.float32)
    gain_first_grad = jnp.sum(grad_normed_first * unit_first, axis=0)
    input_grad = grad_hidden + scale_first * (
        tilted_first - unit_first * jnp.mean(tilted_first * unit_first, axis=-1, keepdims=True)
    )
    query_part, key_part, value_part, output_part = (
        lax.psum_scatter(
            query_grad.astype(jnp.bfloat16), "col", scatter_dimension=1, tiled=True
        ).astype(jnp.float32),
        lax.psum_scatter(
            key_grad.astype(jnp.bfloat16), "col", scatter_dimension=1, tiled=True
        ).astype(jnp.float32),
        lax.psum_scatter(
            value_grad.astype(jnp.bfloat16), "col", scatter_dimension=1, tiled=True
        ).astype(jnp.float32),
        lax.psum_scatter(
            output_grad.astype(jnp.bfloat16), "col", scatter_dimension=0, tiled=True
        ).astype(jnp.float32),
    )
    small_total = lax.psum((gain_first_grad, gain_second_grad, router_grad), ("row", "col"))
    query_out, key_out, value_out, output_out, gate_out, up_out, down_out = (
        lax.psum_scatter(
            query_part.astype(jnp.bfloat16), "row", scatter_dimension=0, tiled=True
        ).astype(jnp.float32),
        lax.psum_scatter(
            key_part.astype(jnp.bfloat16), "row", scatter_dimension=0, tiled=True
        ).astype(jnp.float32),
        lax.psum_scatter(
            value_part.astype(jnp.bfloat16), "row", scatter_dimension=0, tiled=True
        ).astype(jnp.float32),
        lax.psum_scatter(
            output_part.astype(jnp.bfloat16), "row", scatter_dimension=1, tiled=True
        ).astype(jnp.float32),
        lax.psum_scatter(
            gate_grad.astype(jnp.bfloat16), "row", scatter_dimension=1, tiled=True
        ).astype(jnp.float32),
        lax.psum_scatter(
            up_grad.astype(jnp.bfloat16), "row", scatter_dimension=1, tiled=True
        ).astype(jnp.float32),
        lax.psum_scatter(
            down_grad.astype(jnp.bfloat16), "row", scatter_dimension=2, tiled=True
        ).astype(jnp.float32),
    )
    row_block = attention_gain.shape[0]
    row_start = lax.axis_index("row") * row_block
    gain_first_out = lax.dynamic_slice_in_dim(small_total[0], row_start, row_block)
    gain_second_out = lax.dynamic_slice_in_dim(small_total[1], row_start, row_block)
    router_out = lax.dynamic_slice_in_dim(small_total[2], row_start, row_block, 0)
    return (
        block_out,
        input_grad,
        gain_first_out,
        query_out,
        key_out,
        value_out,
        output_out,
        gain_second_out,
        router_out,
        gate_out,
        up_out,
        down_out,
    )


def solution(mesh):
    in_specs = (
        P(("row", "col"), None),
        P("row", None),
        P("row", None),
        P("row"),
        P("row", "col"),
        P("row", "col"),
        P("row", "col"),
        P("col", "row"),
        P("row"),
        P("row", None),
        P(None, "row", "col"),
        P(None, "row", "col"),
        P(None, "col", "row"),
        P(("row", "col"), None),
    )
    out_specs = (
        P(("row", "col"), None),
        P(("row", "col"), None),
        P("row"),
        P("row", "col"),
        P("row", "col"),
        P("row", "col"),
        P("col", "row"),
        P("row"),
        P("row", None),
        P(None, "row", "col"),
        P(None, "row", "col"),
        P(None, "col", "row"),
    )
    return jax.shard_map(
        per_device, mesh=mesh, in_specs=in_specs, out_specs=out_specs, check_vma=False
    )
```

profile of v0, /device:TPU:0, one launch (start us, length us, event | category | flops | bytes accessed | tf_op | source)
XLA Modules:
  0.0 4592.0 jit_solution(17435384423934884050)
XLA Ops:
  8.8 67.1 %all-gather.11.cloned.1.call-done = bf16[1536,768]{1,0:T(8,128)(2,1)} async-done(((bf16[96,768]{1,0:T(8,128)(2,1)}), bf16[1536,768]{1,0:T(8,128)(2,1)}) %all-gather.11.cloned.1.call-update) | async-done | bytes 2359312 | tf_op jit(solution)/shard_map/all_gather | solution.py:121
  78.3 40.4 all-reduce.3
  119.3 38.5 all_gather.57
  161.8 40.4 all_gather.60
  217.4 11.5 while.49
  241.1 36.3 all-gather
  277.6 9.1 reduce-window.19
  315.2 333.8 %all-gather.25.cloned.1.call-done = bf16[32,384,1536]{1,0,2:T(8,128)(2,1)} async-done(((bf16[32,384,96]{1,0,2:T(8,128)(2,1)}), bf16[32,384,1536]{1,0,2:T(8,128)(2,1)}) %all-gather.25.cloned.1.call-update) | async-done | bytes 37748752 | tf_op jit(solution)/shard_map/all_gather | solution.py:137
  649.0 391.4 %all-gather.21.cloned.1.call-done = bf16[32,1536,384]{2,1,0:T(8,128)(2,1)} async-done(((bf16[32,96,384]{2,1,0:T(8,128)(2,1)}), bf16[32,1536,384]{2,1,0:T(8,128)(2,1)}) %all-gather.21.cloned.1.call-update) | async-done | bytes 37748752 | tf_op jit(solution)/shard_map/all_gather | solution.py:135
  1040.4 391.4 %all-gather.23.cloned.1.call-done = bf16[32,1536,384]{2,1,0:T(8,128)(2,1)} async-done(((bf16[32,96,384]{2,1,0:T(8,128)(2,1)}), bf16[32,1536,384]{2,1,0:T(8,128)(2,1)}) %all-gather.23.cloned.1.call-update) | async-done | bytes 37748752 | tf_op jit(solution)/shard_map/all_gather | solution.py:136
  1434.2 690.8 %while.48 = (s32[]{:T(128)}, f32[512,1536]{1,0:T(8,128)S(1)}, f32[512,1536]{1,0:T(8,128)}, f32[8,384]{1,0:T(8,128)S(1)}, bf16[8,4,1536,384]{3,2,1,0:T(8,128)(2,1...) while((s32[]{:T(128)}, f32[512,1536]{1,0:T(8,128)S(1)}, ...), condition=%wide.region_21.22_spmd, body=%wide.region_17.21_spmd.sunk | while | flops 4089104384 | bytes 133634576 | solution.py:272
  1596.3 8.9 scatter_fusion.1
  1681.0 8.9 scatter_fusion.1
  1765.6 8.9 scatter_fusion.1
  1850.1 8.9 scatter_fusion.1
  1934.7 8.9 scatter_fusion.1
  2125.1 11.8 gather_fusion.2
  2145.0 13.9 reduce-scatter.27.cloned.1.call-done
  2161.6 12.1 reduce-scatter.25.cloned.1.call-done
  2182.8 24.4 while.50
  2252.8 14.6 reduce-scatter.41.cloned.1.call-done
  2271.8 12.2 reduce-scatter.33.cloned.1.call-done
  2284.1 48.7 %copy.143 = bf16[8,4,384,1536]{2,3,1,0:T(8,128)(2,1)} copy(bf16[8,4,384,1536]{3,2,1,0:T(8,128)(2,1)} %get-tuple-element.201) | data formatting | bytes 75497472 | tf_op jit(solution)/shard_map/convert_element_type | solution.py:393
  2334.1 81.1 %all-reduce.6.cloned.1.call-done = f32[1536,32]{0,1:T(8,128)} async-done(((f32[1536,32]{0,1:T(8,128)}), f32[1536,32]{0,1:T(8,128)}) %all-reduce.6.cloned.1.call-update) | async-done | bytes 196624 | tf_op jit(solution)/shard_map/psum | solution.py:372
  2423.6 41.5 all-reduce.2
  2469.2 74.2 %reduce-scatter.37.cloned.1.call-done = bf16[96,128]{1,0:T(8,128)(2,1)} async-done(((bf16[1536,128]{1,0:T(8,128)(2,1)}), bf16[96,128]{1,0:T(8,128)(2,1)}) %reduce-scatter.37.cloned.1.call-update) | async-done | bytes 24592 | tf_op jit(solution)/shard_map/reduce_scatter | solution.py:377
  2544.7 124.0 %reduce-scatter.39.cloned.1.call-done = bf16[96,128]{1,0:T(8,128)(2,1)} async-done(((bf16[1536,128]{1,0:T(8,128)(2,1)}), bf16[96,128]{1,0:T(8,128)(2,1)}) %reduce-scatter.39.cloned.1.call-update) | async-done | bytes 24592 | tf_op jit(solution)/shard_map/reduce_scatter | solution.py:380
  2670.1 131.6 %reduce-scatter.55.cloned.1.call-done = bf16[96,768]{1,0:T(8,128)(2,1)} async-done(((bf16[1536,768]{1,0:T(8,128)(2,1)}), bf16[96,768]{1,0:T(8,128)(2,1)}) %reduce-scatter.55.cloned.1.call-update) | async-done | bytes 147472
  2803.6 130.5 %reduce-scatter.35.cloned.1.call-done = bf16[96,768]{1,0:T(8,128)(2,1)} async-done(((bf16[1536,768]{1,0:T(8,128)(2,1)}), bf16[96,768]{1,0:T(8,128)(2,1)}) %reduce-scatter.35.cloned.1.call-update) | async-done | bytes 147472 | tf_op jit(solution)/shard_map/reduce_scatter | solution.py:374
  2935.7 547.2 %reduce-scatter.47.cloned.1.call-done = bf16[32,384,96]{1,2,0:T(8,128)(2,1)} async-done(((bf16[32,384,1536]{1,2,0:T(8,128)(2,1)}), bf16[32,384,96]{1,2,0:T(8,128)(2,1)}) %reduce-scatter.47.cloned.1.call-update) | async-done | bytes 2359312 | tf_op jit(solution)/shard_map/reduce_scatter | solution.py:392
  3487.3 544.6 %reduce-scatter.43.cloned.1.call-done = bf16[32,96,384]{2,1,0:T(8,128)(2,1)} async-done(((bf16[32,1536,384]{2,1,0:T(8,128)(2,1)}), bf16[32,96,384]{2,1,0:T(8,128)(2,1)}) %reduce-scatter.43.cloned.1.call-update) | async-done | bytes 2359312 | tf_op jit(solution)/shard_map/reduce_scatter | solution.py:386
  4036.4 544.5 %reduce-scatter.45.cloned.1.call-done = bf16[32,96,384]{2,1,0:T(8,128)(2,1)} async-done(((bf16[32,1536,384]{2,1,0:T(8,128)(2,1)}), bf16[32,96,384]{2,1,0:T(8,128)(2,1)}) %reduce-scatter.45.cloned.1.call-update) | async-done | bytes 2359312 | tf_op jit(solution)/shard_map/reduce_scatter | solution.py:389
  (585 shorter events, 825.3 us)
Async XLA Ops:
  7.2 70.9 %copy-start.59 = (bf16[96]{0:T(256)(128)(2,1)S(1)}, bf16[96]{0:T(256)(128)(2,1)}, u32[]{:S(2)}) copy-start(bf16[96]{0:T(256)(128)(2,1)} %param.28) | copy-start | bytes 580
  7.2 111.8 %copy-start.3 = (bf16[256,1536]{1,0:T(8,128)(2,1)S(1)}, bf16[256,1536]{1,0:T(8,128)(2,1)}, u32[]{:S(2)}) copy-start(bf16[256,1536]{1,0:T(8,128)(2,1)} %param.20) | copy-start | bytes 2359300
  7.2 68.7 %all-gather.11.cloned.1.call-start = ((), (), s32[]{:S(2)}) async-start(), calls=%async_computation.16 | async-start | bytes 2506752 | tf_op jit(solution)/shard_map/all_gather | solution.py:121
  8.0 197.9 %all-gather.15.cloned.1.call-start = ((), (), s32[]{:S(2)}) async-start(), calls=%async_computation.18 | async-start | bytes 2506752 | tf_op jit(solution)/shard_map/all_gather | solution.py:124
  8.7 202.2 %all-gather.13.cloned.1.call-start = ((), (), s32[]{:S(2)}) async-start(), calls=%async_computation.17 | async-start | bytes 7077888 | tf_op jit(solution)/shard_map/all_gather | solution.py:127
  75.9 153.0 %all-gather.17.cloned.1.call-start = ((), (), s32[]{:S(2)}) async-start(), calls=%async_computation.19 | async-start | bytes 7077888 | tf_op jit(solution)/shard_map/all_gather | solution.py:130
  118.7 92.2 %copy-start.34 = (f32[1536]{0:T(1024)}, f32[1536]{0:T(1024)S(1)}, u32[]{:S(2)}) copy-start(f32[1536]{0:T(1024)S(1)} %convert_element_type.181) | copy-start | bytes 18436
  205.9 98.7 %all-gather.19.cloned.1.call-start = ((), (), s32[]{:S(2)}) async-start(), calls=%async_computation.20 | async-start | bytes 2359296 | tf_op jit(solution)/shard_map/all_gather | solution.py:200
  235.7 79.5 %all-gather.27.cloned.1.call-start = ((), (), s32[]{:S(2)}) async-start(), calls=%async_computation.24 | async-start | bytes 2359296 | tf_op jit(solution)/shard_map/all_gather | solution.py:201
  236.3 412.7 %all-gather.25.cloned.1.call-start = ((), (), s32[]{:S(2)}) async-start(), calls=%async_computation.23 | async-start | bytes 40108032 | tf_op jit(solution)/shard_map/all_gather | solution.py:137
  239.0 801.4 %all-gather.21.cloned.1.call-start = ((), (), s32[]{:S(2)}) async-start(), calls=%async_computation.21 | async-start | bytes 40108032 | tf_op jit(solution)/shard_map/all_gather | solution.py:135
  239.7 1192.1 %all-gather.23.cloned.1.call-start = ((), (), s32[]{:S(2)}) async-start(), calls=%async_computation.22 | async-start | bytes 40108032 | tf_op jit(solution)/shard_map/all_gather | solution.py:136
  240.5 1903.4 %reduce-scatter.49.cloned.1.call-start = ((), (), s32[]{:S(2)}) async-start(), calls=%async_computation.38 | async-start | bytes 393216
  306.7 1125.1 %copy-start.47 = (f32[512,4]{0,1:T(4,128)}, f32[512,4]{0,1:T(4,128)S(1)}, u32[]{:S(2)}) copy-start(f32[512,4]{0,1:T(4,128)S(1)} %fusion.105) | copy-start | bytes 24580
  1434.2 690.8 %copy-start.50 = (s32[2048]{0:T(1024)S(1)}, s32[2048]{0:T(1024)}, u32[]{:S(2)}) copy-start(s32[2048]{0:T(1024)} %broadcast_clamp_fusion) | copy-start | bytes 24580
  2137.9 21.0 reduce-scatter.27.cloned.1.call-start
  2138.6 35.0 reduce-scatter.25.cloned.1.call-start
  2139.2 77.0 %reduce-scatter.29.cloned.1.call-start = ((), (), s32[]{:S(2)}) async-start(), calls=%async_computation.27 | async-start | bytes 393216 | tf_op jit(solution)/shard_map/reduce_scatter | solution.py:323
  2207.2 19.9 reduce-scatter.31.cloned.1.call-start
  2207.8 39.7 reduce-scatter.51.cloned.1.call-start
  2219.7 31.1 reduce-scatter.53.cloned.1.call-start
  2231.9 35.6 reduce-scatter.41.cloned.1.call-start
  2235.5 48.5 %reduce-scatter.33.cloned.1.call-start = ((), (), s32[]{:S(2)}) async-start(), calls=%async_computation.29 | async-start | bytes 7077888 | tf_op jit(solution)/shard_map/reduce_scatter | solution.py:359
  2245.4 169.8 %all-reduce.6.cloned.1.call-start = ((), (), s32[]{:S(2)}) async-start(), calls=%async_computation.34 | async-start | bytes 393216 | tf_op jit(solution)/shard_map/psum | solution.py:372
  2247.4 295.9 %reduce-scatter.37.cloned.1.call-start = ((), (), s32[]{:S(2)}) async-start(), calls=%async_computation.31 | async-start | bytes 417792 | tf_op jit(solution)/shard_map/reduce_scatter | solution.py:377
  2249.5 419.2 %reduce-scatter.39.cloned.1.call-start = ((), (), s32[]{:S(2)}) async-start(), calls=%async_computation.32 | async-start | bytes 417792 | tf_op jit(solution)/shard_map/reduce_scatter | solution.py:380
  2252.8 548.9 %reduce-scatter.55.cloned.1.call-start = ((), (), s32[]{:S(2)}) async-start(), calls=%async_computation.41 | async-start | bytes 2506752
  2271.7 662.4 %reduce-scatter.35.cloned.1.call-start = ((), (), s32[]{:S(2)}) async-start(), calls=%async_computation.30 | async-start | bytes 2506752 | tf_op jit(solution)/shard_map/reduce_scatter | solution.py:374
  2284.0 1198.9 %reduce-scatter.47.cloned.1.call-start = ((), (), s32[]{:S(2)}) async-start(), calls=%async_computation.37 | async-start | bytes 40108032 | tf_op jit(solution)/shard_map/reduce_scatter | solution.py:392
  2332.8 1699.2 %reduce-scatter.43.cloned.1.call-start = ((), (), s32[]{:S(2)}) async-start(), calls=%async_computation.35 | async-start | bytes 40108032 | tf_op jit(solution)/shard_map/reduce_scatter | solution.py:386
  2333.5 2247.4 %reduce-scatter.45.cloned.1.call-start = ((), (), s32[]{:S(2)}) async-start(), calls=%async_computation.36 | async-start | bytes 40108032 | tf_op jit(solution)/shard_map/reduce_scatter | solution.py:389
  2333.6 83.1 %copy-start.16 = (bf16[256,12,128]{0,2,1:T(8,128)(2,1)S(1)}, bf16[256,12,128]{0,2,1:T(8,128)(2,1)}, u32[]{:S(2)}) copy-start(bf16[256,12,128]{0,2,1:T(8,128)(2,1)} %copy-done.15) | copy-start | bytes 2359300
  (81 other events, 725.2 us)
Sparse Core Ops, SparseCore 0:
  10.9 64.9 all-gather.10
  78.7 63.1 all-gather.14
  143.5 13.7 all-gather.12
  206.1 10.3 all-gather.16
  235.8 5.6 all-gather.18
  242.9 10.9 all-gather.26
  257.3 391.6 all-gather.24
  651.7 388.6 all-gather.20
  1043.1 388.6 all-gather.22
  2138.0 5.8 reduce-scatter.48
  2146.8 12.0 reduce-scatter.26
  2161.6 12.0 reduce-scatter.24
  2207.3 8.8 reduce-scatter.28
  2218.2 8.8 reduce-scatter.30
  2229.9 9.3 reduce-scatter.50
  2241.4 9.3 reduce-scatter.52
  2253.6 13.7 reduce-scatter.40
  2270.2 13.7 reduce-scatter.32
  2291.0 124.1 all-reduce.5
  2421.0 122.2 reduce-scatter.36
  2548.0 120.6 reduce-scatter.38
  2674.9 126.6 reduce-scatter.54
  2806.6 127.4 reduce-scatter.34
  2941.0 541.8 reduce-scatter.46
  3489.9 541.9 reduce-scatter.42
  4038.8 542.0 reduce-scatter.44
where the time goes:
time: 4610 us; the launch traced here: 4590 us
  waiting for transfers between devices  3440 us (75%)
  local copies, waits for them, and re-layouts  369 us (8%)
  matrix products  348 us (8%)
  blocking collectives  206 us (4%)
  other arithmetic  184 us (4%)
    reduce_scatter x1, waiting for transfers between devices, per_device(): lax.psum_scatter(down_grad.astype(jnp.bfloat16), 'row', scatter_dimension...  547 us
    reduce_scatter x1, waiting for transfers between devices, per_device(): lax.psum_scatter(gate_grad.astype(jnp.bfloat16), 'row', scatter_dimension...  545 us
    reduce_scatter x1, waiting for transfers between devices, per_device(): lax.psum_scatter(up_grad.astype(jnp.bfloat16), 'row', scatter_dimension=1...  545 us
    all_gather x1, waiting for transfers between devices, per_device(): lax.all_gather(up_weight, 'row', axis=1, tiled=True)  391 us
    all_gather x1, waiting for transfers between devices, per_device(): lax.all_gather(gate_weight, 'row', axis=1, tiled=True)  391 us
    all_gather x1, waiting for transfers between devices, per_device(): lax.all_gather(down_weight, 'row', axis=2, tiled=True)  334 us
    unnamed x30, waiting for transfers between devices  144 us
    dynamic_slice x16, local copies, waits for them, and re-layouts, expert_step(): lax.dynamic_slice_in_dim(down_full, first_expert, group_width, 0)  134 us
  transfers between devices with their start and end apart: 26, of which 20 were waited for; matrix products, arithmetic and copies ran while one was open for 4% of the time, Pallas kernels for 0%

commit v1 on v0

--- a/solution.py
+++ b/solution.py
@@ -19,9 +19,10 @@
 def positions(segment_ids):
     total_length = segment_ids.shape[0]
     token_index = jnp.arange(total_length, dtype=jnp.int32)
-    change = jnp.concatenate([jnp.ones((1,), jnp.bool_), segment_ids[1:] != segment_ids[:-1]])
-    first_index = lax.cummax(jnp.where(change, token_index, 0), axis=0)
-    return token_index - first_index
+    earlier = (segment_ids[:, None] == segment_ids[None, :]) & (
+        token_index[None, :] < token_index[:, None]
+    )
+    return jnp.sum(earlier.astype(jnp.int32), axis=1)
 
 
 def apply_rotary(values, places, direction):
@@ -41,13 +42,27 @@
     )
 
 
+def slot_ranks(route_ids):
+    total_length = route_ids.shape[0]
+    token_index = jnp.arange(total_length, dtype=jnp.int32)
+    expert_ids = jnp.arange(E, dtype=jnp.int32)
+    named = jnp.any(route_ids[:, :, None] == expert_ids[None, None, :], axis=1)
+    before = (token_index[None, :] < token_index[:, None]).astype(jnp.bfloat16)
+    counts = jnp.dot(before, named.astype(jnp.bfloat16), preferred_element_type=jnp.float32)
+    return (named, counts.astype(jnp.int32))
+
+
 def slot_tables(route_ids, experts, capacity):
     flat_ids = route_ids.reshape(-1)
-    expert_ids = jnp.arange(experts, dtype=jnp.int32)
-    onehot = (flat_ids[:, None] == expert_ids[None, :]).astype(jnp.int32)
+    named, counts = slot_ranks(route_ids)
     rank_ids = jnp.sum(
-        (jnp.cumsum(onehot, axis=0, dtype=jnp.int32) - 1) * onehot, axis=1, dtype=jnp.int32
-    )
+        jnp.where(
+            route_ids[:, :, None] == jnp.arange(experts, dtype=jnp.int32)[None, None, :],
+            counts[:, None, :],
+            0,
+        ),
+        axis=-1,
+    ).reshape(-1)
     pair_slot = flat_ids * capacity + rank_ids
     owners = jnp.arange(flat_ids.shape[0], dtype=jnp.int32) // route_ids.shape[1]
     token_of = jnp.zeros((experts * capacity,), jnp.int32).at[pair_slot].set(owners)
@@ -100,7 +115,7 @@
     return (grad_queries, grad_keys, grad_values)
 
 
-def per_device(
+def weights_move(
     hidden_in,
     segments,
     routes,
@@ -414,6 +429,244 @@
     )
 
 
+GRID = ("row", "col")
+
+
+def swap_cores(block):
+    return lax.ppermute(block, "col", [(0, 1), (1, 0)])
+
+
+def both_cores(own, core):
+    other = swap_cores(own)
+    return jnp.where(
+        core == 0,
+        jnp.concatenate([own, other], axis=0),
+        jnp.concatenate([other, own], axis=0),
+    )
+
+
+def sum_cores(partial, core):
+    half = partial.shape[0] // 2
+    away = lax.dynamic_slice_in_dim(partial, (1 - core) * half, half)
+    kept = lax.dynamic_slice_in_dim(partial, core * half, half)
+    return kept + swap_cores(away)
+
+
+def exchange(block):
+    return lax.all_to_all(block, GRID, split_axis=0, concat_axis=0, tiled=True)
+
+
+def tokens_move(
+    hidden_in,
+    segments,
+    routes,
+    attention_gain,
+    query_weight,
+    key_matrix,
+    value_matrix,
+    output_weight,
+    expert_gain,
+    router_weight,
+    gate_weight,
+    up_weight,
+    down_weight,
+    cotangent,
+):
+    bf16, f32 = jnp.bfloat16, jnp.float32
+    core = lax.axis_index("col")
+    local = hidden_in.shape[0]
+    span = segments.shape[1]
+    rows = MODEL_WIDTH // query_weight.shape[0]
+    row_block = query_weight.shape[0]
+    hidden_block = gate_weight.shape[2]
+    ffe = 2 * hidden_block
+    capacity = max(2, 3 * span * TOPK // (2 * E))
+    share = capacity // 2
+    head_cols = query_weight.shape[1]
+    kv_cols = key_matrix.shape[1]
+    heads = head_cols // HEAD_SIZE
+
+    packed = jnp.concatenate(
+        [
+            query_weight,
+            key_matrix,
+            value_matrix,
+            output_weight.T,
+            router_weight,
+            attention_gain[:, None],
+            expert_gain[:, None],
+            jnp.zeros((row_block, 128 - E - 2), bf16),
+        ],
+        axis=1,
+    )
+    packed_full = lax.all_gather(packed, "row", axis=0, tiled=True)
+    o0 = head_cols + 2 * kv_cols
+    o1 = o0 + head_cols
+    query_cols = packed_full[:, :head_cols]
+    qkv_cols = packed_full[:, :o0]
+    output_t = packed_full[:, o0:o1]
+    router_full = packed_full[:, o1 : o1 + E]
+    gain_first = packed_full[:, o1 + E].astype(f32)
+    gain_second = packed_full[:, o1 + E + 1].astype(f32)
+
+    named, counts = slot_ranks(routes)
+    slot_of = jnp.where(named, counts, -1).T
+    share_slots = core * share + jnp.arange(share, dtype=jnp.int32)
+    pick = (slot_of[:, None, :] == share_slots[None, :, None]).astype(bf16)
+    pick = pick.reshape(E * share, span)
+
+    cotangent_all = both_cores(cotangent, core)
+    cot_share = jnp.dot(pick, cotangent_all, preferred_element_type=f32).astype(bf16)
+    upstream = exchange(cot_share)
+    gate_e = exchange(gate_weight)
+    up_e = exchange(up_weight)
+    down_e = exchange(down_weight.transpose(0, 2, 1))
+
+    def whole_weight(blocks):
+        return (
+            blocks.reshape(rows, 2, row_block, hidden_block)
+            .transpose(0, 2, 1, 3)
+            .reshape(MODEL_WIDTH, ffe)
+        )
+
+    hidden_all = both_cores(hidden_in, core)
+    tokens_all = hidden_all.astype(f32)
+    scale_all = lax.rsqrt(jnp.mean(tokens_all * tokens_all, axis=-1, keepdims=True) + EPSILON)
+    normed_all = (tokens_all * scale_all * gain_first).astype(bf16)
+    segment_ids = segments[0]
+    places = positions(segment_ids)
+    token_index = jnp.arange(span, dtype=jnp.int32)
+    allowed = (segment_ids[:, None] == segment_ids[None, :]) & (
+        token_index[None, :] <= token_index[:, None]
+    )
+    raw = jnp.dot(normed_all, qkv_cols, preferred_element_type=f32)
+    queries = apply_rotary(raw[:, :head_cols].reshape(span, heads, HEAD_SIZE), places, 1.0)
+    queries = queries.astype(bf16).transpose(1, 0, 2)
+    keys = apply_rotary(
+        raw[:, head_cols : head_cols + kv_cols].reshape(span, 1, HEAD_SIZE), places, 1.0
+    ).astype(bf16)[:, 0]
+    values = raw[:, head_cols + kv_cols :].astype(bf16)
+    scaling = HEAD_SIZE ** (-0.5)
+    attended, log_total = attend_group((queries, keys, values), allowed, scaling)
+    attended_low = attended.transpose(1, 0, 2).reshape(span, head_cols).astype(bf16)
+    branch_part = lax.dot_general(
+        attended_low, output_t, (((1,), (1,)), ((), ())), preferred_element_type=f32
+    )
+    tokens_in = hidden_in.astype(f32)
+    hidden_mid = tokens_in + sum_cores(branch_part, core)
+    scale_second = lax.rsqrt(jnp.mean(hidden_mid * hidden_mid, axis=-1, keepdims=True) + EPSILON)
+    unit_second = hidden_mid * scale_second
+    normed_second = (unit_second * gain_second).astype(bf16)
+    second_all = both_cores(normed_second, core)
+
+    logits = jnp.dot(second_all, router_full, preferred_element_type=f32)
+    masked = jnp.where(named, logits, MASKED)
+    exponent = jnp.where(named, jnp.exp(masked - jnp.max(masked, axis=-1, keepdims=True)), 0.0)
+    gates = exponent / jnp.sum(exponent, axis=-1, keepdims=True)
+
+    expert_in = exchange(jnp.dot(pick, second_all, preferred_element_type=f32).astype(bf16))
+    pick3 = pick.reshape(E, share, span)
+    slot_gate = jnp.sum(pick3.astype(f32) * gates.T[:, None, :], axis=-1)
+    slot_gate = exchange(slot_gate).reshape(-1, 1)
+
+    gate_w, up_w, down_t = whole_weight(gate_e), whole_weight(up_e), whole_weight(down_e)
+    nt = (((1,), (1,)), ((), ()))
+    tn = (((0,), (0,)), ((), ()))
+    gate_value = jnp.dot(expert_in, gate_w, preferred_element_type=f32)
+    up_value = jnp.dot(expert_in, up_w, preferred_element_type=f32)
+    sigmoid_gate = jax.nn.sigmoid(gate_value)
+    silu_gate = gate_value * sigmoid_gate
+    activation = (silu_gate * up_value).astype(bf16)
+    expert_out = lax.dot_general(activation, down_t, nt, preferred_element_type=f32)
+    up32 = upstream.astype(f32)
+    slot_grad = jnp.sum(expert_out * up32, axis=-1)
+    returned = exchange((expert_out * slot_gate).astype(bf16))
+    grad_expert = (up32 * slot_gate).astype(bf16)
+    grad_act = jnp.dot(grad_expert, down_t, preferred_element_type=f32)
+    slope = sigmoid_gate * (1.0 + gate_value * (1.0 - sigmoid_gate))
+    grad_gate = (grad_act * up_value * slope).astype(bf16)
+    grad_up = (grad_act * silu_gate).astype(bf16)
+    grad_in = lax.dot_general(grad_gate, gate_w, nt, preferred_element_type=f32)
+    grad_in = grad_in + lax.dot_general(grad_up, up_w, nt, preferred_element_type=f32)
+    grad_back = exchange(grad_in.astype(bf16))
+    slot_grad = exchange(slot_grad.reshape(E, share))
+
+    def shard_grad(left, right):
+        full = lax.dot_general(left, right, tn, preferred_element_type=f32).astype(bf16)
+        blocks = full.reshape(rows, row_block, 2, hidden_block).transpose(0, 2, 1, 3)
+        return exchange(blocks.reshape(E, row_block, hidden_block)).astype(f32)
+
+    def combine(slots):
+        return sum_cores(lax.dot_general(pick, slots, tn, preferred_element_type=f32), core)
+
+    input_own = combine(grad_back.reshape(E * share, MODEL_WIDTH))
+    pick_part = jnp.sum(pick3.astype(f32) * slot_grad[:, :, None], axis=1).T
+    pick_own = sum_cores(pick_part, core)
+    own_gates = lax.dynamic_slice_in_dim(gates, core * local, local)
+    centred = own_gates * (pick_own - jnp.sum(own_gates * pick_own, axis=-1, keepdims=True))
+    grad_logits = centred.astype(bf16)
+    grad_normed = input_own + lax.dot_general(
+        grad_logits, router_full, nt, preferred_element_type=f32
+    )
+    router_grad = lax.dot_general(normed_second, grad_logits, tn, preferred_element_type=f32)
+    tilted = grad_normed * gain_second
+    gain_second_grad = jnp.sum(grad_normed * unit_second, axis=0)
+    grad_hidden = cotangent.astype(f32) + scale_second * (
+        tilted - unit_second * jnp.mean(tilted * unit_second, axis=-1, keepdims=True)
+    )
+    branch_all = both_cores(grad_hidden.astype(bf16), core)
+
+    output_t_grad = lax.dot_general(branch_all, attended_low, tn, preferred_element_type=f32)
+    grad_attended = jnp.dot(branch_all, output_t, preferred_element_type=f32).astype(bf16)
+    grad_attended = grad_attended.reshape(span, heads, HEAD_SIZE).transpose(1, 0, 2)
+    grad_queries, grad_keys, grad_values = attend_back(
+        (queries, keys, values, log_total, grad_attended), allowed, scaling
+    )
+    grad_query_low = (
+        apply_rotary(grad_queries.transpose(1, 0, 2), places, -1.0)
+        .reshape(span, head_cols)
+        .astype(bf16)
+    )
+    grad_key_low = apply_rotary(grad_keys[:, None], places, -1.0)[:, 0].astype(bf16)
+    grad_qkv = jnp.concatenate([grad_query_low, grad_key_low, grad_values.astype(bf16)], axis=1)
+    first_part = lax.dot_general(grad_qkv, qkv_cols, nt, preferred_element_type=f32)
+    qkv_grad = lax.dot_general(normed_all, grad_qkv, tn, preferred_element_type=f32)
+    grad_first = sum_cores(first_part, core)
+    scale_first = lax.dynamic_slice_in_dim(scale_all, core * local, local)
+    unit_first = tokens_in * scale_first
+    tilted_first = grad_first * gain_first
+    gain_first_grad = jnp.sum(grad_first * unit_first, axis=0)
+    input_grad = grad_hidden + scale_first * (
+        tilted_first - unit_first * jnp.mean(tilted_first * unit_first, axis=-1, keepdims=True)
+    )
+    block_out = (hidden_mid + combine(returned.reshape(E * share, MODEL_WIDTH))).astype(bf16)
+
+    gate_out = shard_grad(expert_in, grad_gate)
+    up_out = shard_grad(expert_in, grad_up)
+    down_out = shard_grad(grad_expert, activation).transpose(0, 2, 1)
+    packed_grad = jnp.concatenate([qkv_grad, output_t_grad], axis=1).astype(bf16)
+    packed_own = lax.psum_scatter(packed_grad, "row", scatter_dimension=0, tiled=True).astype(f32)
+    small = jnp.concatenate(
+        [router_grad, gain_first_grad[:, None], gain_second_grad[:, None]], axis=1
+    )
+    small = lax.psum(small, GRID)
+    small_own = lax.dynamic_slice_in_dim(small, lax.axis_index("row") * row_block, row_block)
+    return (
+        block_out,
+        input_grad,
+        small_own[:, E],
+        packed_own[:, :head_cols],
+        packed_own[:, head_cols : head_cols + kv_cols],
+        packed_own[:, head_cols + kv_cols : o0],
+        packed_own[:, o0:].T,
+        small_own[:, E + 1],
+        small_own[:, :E],
+        gate_out,
+        up_out,
+        down_out,
+    )
+
+
 def solution(mesh):
     in_specs = (
         P(("row", "col"), None),
@@ -445,6 +698,11 @@
         P(None, "row", "col"),
         P(None, "col", "row"),
     )
+    rows, cols = mesh.shape["row"], mesh.shape["col"]
+    one_each = rows * cols == E and cols == KEY_VALUE_HEADS
     return jax.shard_map(
-        per_device, mesh=mesh, in_specs=in_specs, out_specs=out_specs, check_vma=False
-    )
+        tokens_move if one_each else weights_move, mesh=mesh,
+        in_specs=in_specs,
+        out_specs=out_specs,
+        check_vma=False,
+    )

time: 4610 us -> 1100 us (0.24)
  waiting for transfers between devices: 3440 us -> 619 us
  local copies, waits for them, and re-layouts: 369 us -> 98 us
  matrix products: 348 us -> 137 us
  other arithmetic: 184 us -> 69 us
  blocking collectives: 206 us -> 98.7 us
  starting transfers between devices: 1.59 us -> 49.5 us
    reduce_scatter x12 -> x0, waiting for transfers between devices: 2030 us -> none  [the longest x1 547 us: per_device(): lax.psum_scatter(down_grad.astype(jnp.bfloat16), 'row', scatter_dimension...]
    all_gather x9 -> x1, waiting for transfers between devices: 1180 us -> 48.7 us  [tokens_move(): packed_full = lax.all_gather(packed, 'row', axis=0, tiled=True)]
    all_to_all x0 -> x10, waiting for transfers between devices: none -> 419 us  [exchange(): return lax.all_to_all(block, GRID, split_axis=0, concat_axis=0, tiled=True)]
    dot_general x87 -> x23, matrix products: 328 us -> 118 us  [the longest x3 24.4 us: shard_grad(): lax.dot_general(left, right, tn, preferred_element_type=f32).astype(bf16)]
    dynamic_slice x36 -> x6, local copies, waits for them, and re-layouts: 142 us -> 2.83 us  [the longest x5 2.19 us: sum_cores(): away = lax.dynamic_slice_in_dim(partial, (1 - core) * half, half)]
    all_gather x7 -> x0, blocking collectives: 124 us -> none  [the longest x1 40.4 us: per_device(): lax.all_gather(value_matrix, 'row', axis=0, tiled=True)]
    scatter-add x16 -> x0, other arithmetic: 123 us -> none  [the longest x8 70.9 us: expert_step(): input_sum.at[row_ids].add(grad_inputs.reshape(group_rows, MODEL_WIDTH))]
    gather x17 -> x0, local copies, waits for them, and re-layouts: 106 us -> none  [the longest x8 47.2 us: expert_step(): upstream = upstream_all[row_ids].astype(jnp.float32)]
  transfers between devices with their start and end apart: 26 -> 22, of which waited for: 20 -> 15; matrix products, arithmetic and copies ran while one was open for 4% -> 23% of each run, Pallas kernels for 0% -> 0%
where the time goes in v1:
time: 1100 us; the launch traced here: 1090 us
  waiting for transfers between devices  619 us (56%)
  matrix products  137 us (12%)
  blocking collectives  98.7 us (9%)
  local copies, waits for them, and re-layouts  98 us (9%)
  other arithmetic  69 us (6%)
  starting transfers between devices  49.5 us (4%)
  between operations  15.4 us (1%)
    all_to_all x10, waiting for transfers between devices, exchange(): return lax.all_to_all(block, GRID, split_axis=0, concat_axis=0, tiled=True)  419 us
    unnamed x4, waiting for transfers between devices  144 us
    all_to_all x2, blocking collectives, exchange(): return lax.all_to_all(block, GRID, split_axis=0, concat_axis=0, tiled=True)  98.7 us
    all_gather x1, waiting for transfers between devices, tokens_move(): packed_full = lax.all_gather(packed, 'row', axis=0, tiled=True)  48.7 us
    all_to_all x10, starting transfers between devices, exchange(): return lax.all_to_all(block, GRID, split_axis=0, concat_axis=0, tiled=True)  46.4 us
    unnamed x168, local copies, waits for them, and re-layouts  34.9 us
    dot_general x3, matrix products, shard_grad(): lax.dot_general(left, right, tn, preferred_element_type=f32).astype(bf16)  24.4 us
  transfers between devices with their start and end apart: 22, of which 15 were waited for; matrix products, arithmetic and copies ran while one was open for 23% of the time, Pallas kernels for 0%

profile of v1, /device:TPU:0, one launch (start us, length us, event | category | flops | bytes accessed | tf_op | source)
XLA Modules:
  0.0 1086.4 jit_solution(15489080651619431518)
XLA Ops:
  11.5 89.9 %all_to_all.87 = bf16[32,96,384]{2,1,0:T(8,128)(2,1)} all-to-all(bf16[32,96,384]{2,1,0:T(8,128)(2,1)} %param.24), channel_id=1, replica_groups=mesh['row'=16,'col'=2] {'row','col'}, dimensions={0} | all-to-all | bytes 4718592 | tf_op jit(solution)/shard_map/all_to_all | solution.py:456
  109.1 48.7 %all-gather.2.cloned.1.call-done = bf16[1536,1920]{1,0:T(8,128)(2,1)} async-done(((bf16[96,1920]{1,0:T(8,128)(2,1)}), bf16[1536,1920]{1,0:T(8,128)(2,1)}) %all-gather.2.cloned.1.call-update) | async-done | bytes 5898256 | tf_op jit(solution)/shard_map/all_gather | solution.py:502
  183.5 9.8 all-to-all-start.3
  211.6 6.3 convolution_convert_fusion.1
  218.0 29.8 %all-to-all-done.3 = bf16[32,96,384]{2,1,0:T(8,128)(2,1)} async-done(((bf16[32,96,384]{2,1,0:T(8,128)(2,1)}), bf16[32,96,384]{2,1,0:T(8,128)(2,1)}, u32[]{:S(2)}, u32[]{:S(2)}) %all-to-all-start.3) | async-done | bytes 2359328 | tf_op jit(solution)/shard_map/all_to_all | solution.py:456
  254.3 5.5 convolution_convert_fusion
  259.7 97.5 %all-to-all-done = bf16[32,48,1536]{2,1,0:T(8,128)(2,1)} async-done(((bf16[32,48,1536]{2,1,0:T(8,128)(2,1)}), bf16[32,48,1536]{2,1,0:T(8,128)(2,1)}, u32[]{:S(2)}, u32[]{:S(2)}) %all-to-all-start) | async-done | bytes 4718624 | tf_op jit(solution)/shard_map/all_to_all | solution.py:456
  380.6 5.7 fusion.120
  388.5 8.5 multiply_convert_fusion.4
  396.9 69.6 %all-to-all-done.6 = bf16[32,48,1536]{2,1,0:T(8,128)(2,1)} async-done(((bf16[32,48,1536]{2,1,0:T(8,128)(2,1)}), bf16[32,48,1536]{2,1,0:T(8,128)(2,1)}, u32[]{:S(2)}, u32[]{:S(2)}) %all-to-all-start.6) | async-done | bytes 4718624 | tf_op jit(solution)/shard_map/all_to_all | solution.py:456
  466.5 11.4 %fusion.1 = (f32[1536]{0:T(1024)S(1)}, f32[1536,1536]{1,0:T(8,128)}) fusion(bf16[32,48,1536]{2,1,0:T(8,128)(2,1)} %all-to-all-done.6, bf16[1536,768]{1,0:T(8,128)(2,1)} %get-tuple-element.98, bf16[1536,768]{1,0:T(8,128)(2,1)} %bitcast.185), kind=kOutput, calls=%fused_computation.4 | convolution fusion | flops 3630955008 | bytes 18880512 | tf_op jit(solution)/shard_map/dot_general | solution.py:580
  482.4 7.0 all-to-all-done.8
  490.6 8.8 all_to_all.88
  503.9 6.9 multiply_convert_fusion.2
  514.7 5.7 add_convert_fusion
  524.4 8.4 convolution_convert_fusion.6
  532.8 5.8 reshape.390
  542.1 87.7 %all-to-all-done.7 = bf16[32,48,1536]{2,1,0:T(8,128)(2,1)} async-done(((bf16[32,48,1536]{2,1,0:T(8,128)(2,1)}), bf16[32,48,1536]{2,1,0:T(8,128)(2,1)}, u32[]{:S(2)}, u32[]{:S(2)}) %all-to-all-start.7) | async-done | bytes 4718624 | tf_op jit(solution)/shard_map/all_to_all | solution.py:456
  643.1 7.5 convolution_convert_fusion.5
  654.0 5.8 reshape.392
  669.7 18.4 %all-to-all-done.9 = bf16[32,96,384]{2,1,0:T(8,128)(2,1)} async-done(((bf16[32,96,384]{2,1,0:T(8,128)(2,1)}), bf16[32,96,384]{2,1,0:T(8,128)(2,1)}, u32[]{:S(2)}, u32[]{:S(2)}) %all-to-all-start.9) | async-done | bytes 2359328 | tf_op jit(solution)/shard_map/all_to_all | solution.py:456
  692.4 11.3 %fusion.2 = (bf16[1536,1536]{1,0:T(8,128)(2,1)}, bf16[1536,1536]{1,0:T(8,128)(2,1)}) fusion(bf16[32,48,1536]{2,1,0:T(8,128)(2,1)} %all-to-all-done.6, f32[1536]{0:T(1024)S(1)} %mul.409, f32[1536,1536]{1,0:T(8,128)} %get-tuple-element.101), kind=kLoop, calls=%fused_computation.5 | loop fusion | flops 11796480 | bytes 23599104 | tf_op jit(solution)/shard_map/convert_element_type | solution.py:584
  710.9 5.6 multiply_reduce_fusion
  724.5 22.4 %all-to-all-done.10 = bf16[32,96,384]{2,1,0:T(8,128)(2,1)} async-done(((bf16[32,96,384]{2,1,0:T(8,128)(2,1)}), bf16[32,96,384]{2,1,0:T(8,128)(2,1)}, u32[]{:S(2)}, u32[]{:S(2)}) %all-to-all-start.10) | async-done | bytes 2359328 | tf_op jit(solution)/shard_map/all_to_all | solution.py:456
  779.5 5.4 pad_maximum_fusion
  784.9 8.3 copy.153
  793.2 8.4 convolution_convert_fusion.4
  801.6 5.8 reshape.394
  810.9 47.6 %all-to-all-done.5 = bf16[32,48,1536]{2,1,0:T(8,128)(2,1)} async-done(((bf16[32,48,1536]{2,1,0:T(8,128)(2,1)}), bf16[32,48,1536]{2,1,0:T(8,128)(2,1)}, u32[]{:S(2)}, u32[]{:S(2)}) %all-to-all-start.5) | async-done | bytes 4718624 | tf_op jit(solution)/shard_map/all_to_all | solution.py:456
  862.4 5.1 fusion.10
  879.6 38.6 %all-to-all-done.11 = bf16[32,96,384]{2,1,0:T(8,128)(2,1)} async-done(((bf16[32,96,384]{2,1,0:T(8,128)(2,1)}), bf16[32,96,384]{2,1,0:T(8,128)(2,1)}, u32[]{:S(2)}, u32[]{:S(2)}) %all-to-all-start.11) | async-done | bytes 2359328 | tf_op jit(solution)/shard_map/all_to_all | solution.py:456
  930.7 144.1 %reduce-scatter.4.cloned.1.call-done = bf16[96,1792]{1,0:T(8,128)(2,1)} async-done(((bf16[1536,1792]{1,0:T(8,128)(2,1)}), bf16[96,1792]{1,0:T(8,128)(2,1)}) %reduce-scatter.4.cloned.1.call-update) | async-done | bytes 344080
  (296 shorter events, 223.9 us)
Async XLA Ops:
  7.2 150.6 %all-gather.2.cloned.1.call-start = ((), (), s32[]{:S(2)}) async-start(), calls=%async_computation.13 | async-start | bytes 6266880 | tf_op jit(solution)/shard_map/all_gather | solution.py:502
  101.3 82.1 %all-to-all-start.2 = ((bf16[32,96,384]{2,1,0:T(8,128)(2,1)}), bf16[32,96,384]{2,1,0:T(8,128)(2,1)}, u32[]{:S(2)}, u32[]{:S(2)}) async-start(bf16[32,96,384]{2,1,0:T(8,128)(2,1)} %param.25), calls=%async_computation.2 | async-start | bytes 4718592 | tf_op jit(solution)/shard_map/all_to_all | solution.py:456
  106.0 2.6 collective-permute-start
  106.4 67.6 %copy-start.52 = (f32[512]{0:T(512)}, f32[512]{0:T(512)S(1)}, u32[]{:S(2)}) copy-start(f32[512]{0:T(512)S(1)} %convert_element_type.172) | copy-start | bytes 6148
  106.4 67.6 %copy-start.65 = (f32[64]{0:T(128)}, f32[64]{0:T(128)S(1)}, u32[]{:S(2)}) copy-start(f32[64]{0:T(128)S(1)} %multiply_power_fusion) | copy-start | bytes 772
  108.5 54.7 %copy-start.32 = (bf16[256,1536]{1,0:T(8,128)(2,1)}, bf16[256,1536]{1,0:T(8,128)(2,1)S(1)}, u32[]{:S(2)}) copy-start(bf16[256,1536]{1,0:T(8,128)(2,1)S(1)} %collective-permute-done) | copy-start | bytes 2359300
  109.1 54.1 %copy-start.63 = (f32[512]{0:T(512)}, f32[512]{0:T(512)S(1)}, u32[]{:S(2)}) copy-start(f32[512]{0:T(512)S(1)} %add_rsqrt_fusion) | copy-start | bytes 6148
  183.5 64.3 %all-to-all-start.3 = ((bf16[32,96,384]{2,1,0:T(8,128)(2,1)}), bf16[32,96,384]{2,1,0:T(8,128)(2,1)}, u32[]{:S(2)}, u32[]{:S(2)}) async-start(bf16[32,96,384]{2,1,0:T(8,128)(2,1)} %bitcast.180), calls=%async_computation.3 | async-start | bytes 4718592 | tf_op jit(solution)/shard_map/all_to_all | solution.py:456
  203.1 3.6 collective-permute-start.1
  209.1 168.5 %copy-start.12 = (bf16[256,1536]{1,0:T(8,128)(2,1)}, bf16[256,1536]{1,0:T(8,128)(2,1)S(1)}, u32[]{:S(2)}) copy-start(bf16[256,1536]{1,0:T(8,128)(2,1)S(1)} %multiply_convert_fusion.5) | copy-start | bytes 2359300
  209.2 2.5 collective-permute-start.2
  209.6 424.0 %copy-start.67 = (s32[48]{0:T(128)}, s32[48]{0:T(128)S(1)}, u32[]{:S(2)}) copy-start(s32[48]{0:T(128)S(1)} %iota_add_fusion) | copy-start | bytes 580
  209.7 168.0 %copy-start.44 = (pred[512,32]{0,1:T(8,128)(4,1)}, pred[512,32]{0,1:T(8,128)(4,1)S(1)}, u32[]{:S(2)}) copy-start(pred[512,32]{0,1:T(8,128)(4,1)S(1)} %fusion.88) | copy-start | bytes 49156
  247.8 109.4 %all-to-all-start = ((bf16[32,48,1536]{2,1,0:T(8,128)(2,1)}), bf16[32,48,1536]{2,1,0:T(8,128)(2,1)}, u32[]{:S(2)}, u32[]{:S(2)}) async-start(bf16[32,48,1536]{2,1,0:T(8,128)(2,1)} %bitcast.177), calls=%async_computation | async-start | bytes 9437184 | tf_op jit(solution)/shard_map/all_to_all | solution.py:456
  251.9 2.4 collective-permute-start.4
  357.2 109.3 %all-to-all-start.6 = ((bf16[32,48,1536]{2,1,0:T(8,128)(2,1)}), bf16[32,48,1536]{2,1,0:T(8,128)(2,1)}, u32[]{:S(2)}, u32[]{:S(2)}) async-start(bf16[32,48,1536]{2,1,0:T(8,128)(2,1)} %bitcast.176), calls=%async_computation.6 | async-start | bytes 9437184 | tf_op jit(solution)/shard_map/all_to_all | solution.py:456
  466.5 22.9 %copy-start.37 = (s32[32,512]{1,0:T(8,128)S(1)}, s32[32,512]{1,0:T(8,128)}, u32[]{:S(2)}) copy-start(s32[32,512]{1,0:T(8,128)} %copy-done.36) | copy-start | bytes 196612
  478.6 10.9 all-to-all-start.8
  520.4 109.3 %all-to-all-start.7 = ((bf16[32,48,1536]{2,1,0:T(8,128)(2,1)}), bf16[32,48,1536]{2,1,0:T(8,128)(2,1)}, u32[]{:S(2)}, u32[]{:S(2)}) async-start(bf16[32,48,1536]{2,1,0:T(8,128)(2,1)} %bitcast.178), calls=%async_computation.7 | async-start | bytes 9437184 | tf_op jit(solution)/shard_map/all_to_all | solution.py:456
  629.8 58.3 %all-to-all-start.9 = ((bf16[32,96,384]{2,1,0:T(8,128)(2,1)}), bf16[32,96,384]{2,1,0:T(8,128)(2,1)}, u32[]{:S(2)}, u32[]{:S(2)}) async-start(bf16[32,96,384]{2,1,0:T(8,128)(2,1)} %bitcast.167), calls=%async_computation.9 | async-start | bytes 4718592 | tf_op jit(solution)/shard_map/all_to_all | solution.py:456
  640.5 24.5 %collective-permute-start.5 = (f32[256,1536]{1,0:T(8,128)S(1)}, f32[256,1536]{1,0:T(8,128)}, u32[]{:S(2)}, u32[]{:S(2)}) collective-permute-start(f32[256,1536]{1,0:T(8,128)S(1)} %constant_dynamic-slice_fusion.2), channel_id=1, source_target_pairs={{0,1},{1,0},{2,3},{3,2},{4,5},{5,4},{6,7},{7,6},{8,9},{9,8},{10,11... | collective-permute-start | bytes 4718600 | tf_op jit(solution)/shard_map/ppermute | solution.py:436
  642.9 20.4 %collective-permute-start.6 = (f32[256,32]{0,1:T(8,128)}, f32[256,32]{0,1:T(8,128)}, u32[]{:S(2)}, u32[]{:S(2)}) collective-permute-start(f32[256,32]{0,1:T(8,128)} %dynamic-slice_bitcast_fusion), channel_id=1, source_target_pairs={{0,1},{1,0},{2,3},{3,2},{4,5},{5,4},{6,7},{7,6},{8,9},{9,8},{10,11... | collective-permute-start | bytes 98312 | tf_op jit(solution)/shard_map/ppermute | solution.py:436
  669.4 34.3 %collective-permute-start.7 = (bf16[256,1536]{1,0:T(8,128)(2,1)}, bf16[256,1536]{1,0:T(8,128)(2,1)}, u32[]{:S(2)}, u32[]{:S(2)}) collective-permute-start(bf16[256,1536]{1,0:T(8,128)(2,1)} %fusion.116), channel_id=1, source_target_pairs={{0,1},{1,0},{2,3},{3,2},{4,5},{5,4},{6,7},{7,6},{8,9},{9,8},{10,11... | collective-permute-start | bytes 2359304 | tf_op jit(solution)/shard_map/ppermute | solution.py:436
  688.1 58.8 %all-to-all-start.10 = ((bf16[32,96,384]{2,1,0:T(8,128)(2,1)}), bf16[32,96,384]{2,1,0:T(8,128)(2,1)}, u32[]{:S(2)}, u32[]{:S(2)}) async-start(bf16[32,96,384]{2,1,0:T(8,128)(2,1)} %bitcast.166), calls=%async_computation.10 | async-start | bytes 4718592 | tf_op jit(solution)/shard_map/all_to_all | solution.py:456
  746.9 111.6 %all-to-all-start.5 = ((bf16[32,48,1536]{2,1,0:T(8,128)(2,1)}), bf16[32,48,1536]{2,1,0:T(8,128)(2,1)}, u32[]{:S(2)}, u32[]{:S(2)}) async-start(bf16[32,48,1536]{2,1,0:T(8,128)(2,1)} %bitcast.164), calls=%async_computation.5 | async-start | bytes 9437184 | tf_op jit(solution)/shard_map/all_to_all | solution.py:456
  751.0 176.9 %all-reduce.2.cloned.1.call-start = ((), (), s32[]{:S(2)}) async-start(), calls=%async_computation.14 | async-start | bytes 491520 | tf_op jit(solution)/shard_map/psum | solution.py:652
  767.0 9.7 collective-permute-start.8
  779.2 295.6 %reduce-scatter.4.cloned.1.call-start = ((), (), s32[]{:S(2)}) async-start(), calls=%async_computation.15 | async-start | bytes 5849088
  858.5 59.7 %all-to-all-start.11 = ((bf16[32,96,384]{2,1,0:T(8,128)(2,1)}), bf16[32,96,384]{2,1,0:T(8,128)(2,1)}, u32[]{:S(2)}, u32[]{:S(2)}) async-start(bf16[32,96,384]{2,1,0:T(8,128)(2,1)} %bitcast.168), calls=%async_computation.11 | async-start | bytes 4718592 | tf_op jit(solution)/shard_map/all_to_all | solution.py:456
  870.5 52.3 %collective-permute-start.3 = (f32[256,1536]{1,0:T(8,128)}, f32[256,1536]{1,0:T(8,128)}, u32[]{:S(2)}, u32[]{:S(2)}) collective-permute-start(f32[256,1536]{1,0:T(8,128)} %constant_dynamic-slice_fusion.3), channel_id=1, source_target_pairs={{0,1},{1,0},{2,3},{3,2},{4,5},{5,4},{6,7},{7,6},{8,9},{9,8},{10,11... | collective-permute-start | bytes 4718600 | tf_op jit(solution)/shard_map/ppermute | solution.py:436
  879.6 43.2 %copy-start.58 = (f32[256]{0:T(256)S(1)}, f32[256]{0:T(256)}, u32[]{:S(2)}) copy-start(f32[256]{0:T(256)} %copy-done.56) | copy-start | bytes 3076
  879.6 43.2 %copy-start.60 = (f32[256]{0:T(256)S(1)}, f32[256]{0:T(256)}, u32[]{:S(2)}) copy-start(f32[256]{0:T(256)} %copy-done.59) | copy-start | bytes 3076
  (68 other events, 267.8 us)
Sparse Core Ops, SparseCore 0:
  11.6 146.1 all-gather.1
  779.3 148.5 all-reduce.1
  933.1 141.6 reduce-scatter.3

commit v2 on v1

--- a/solution.py
+++ b/solution.py
@@ -1,6 +1,8 @@
 import jax
 import jax.numpy as jnp
 from jax import lax
+from jax.experimental import pallas as pl
+from jax.experimental.pallas import tpu as pltpu
 from jax.sharding import PartitionSpec as P
 
 MODEL_WIDTH = 1536
@@ -430,30 +432,120 @@
 
 
 GRID = ("row", "col")
+PLANE = 4
+LINE = 4
+
+
+def nothing(*refs):
+    pass
+
+
+def after(block, *others):
+    anywhere = pl.BlockSpec(memory_space=pl.ANY)
+    return pl.pallas_call(
+        nothing,
+        out_shape=jax.ShapeDtypeStruct(block.shape, block.dtype),
+        in_specs=[anywhere] * (1 + len(others)),
+        out_specs=anywhere,
+        input_output_aliases={0: 0},
+        name="after",
+    )(block, *others)
 
 
 def swap_cores(block):
     return lax.ppermute(block, "col", [(0, 1), (1, 0)])
 
 
-def both_cores(own, core):
-    other = swap_cores(own)
-    return jnp.where(
-        core == 0,
-        jnp.concatenate([own, other], axis=0),
-        jnp.concatenate([other, own], axis=0),
-    )
-
-
-def sum_cores(partial, core):
+def both_cores(own):
+    return jnp.concatenate([own, swap_cores(own)], axis=0)
+
+
+def sum_cores(partial, kind):
     half = partial.shape[0] // 2
-    away = lax.dynamic_slice_in_dim(partial, (1 - core) * half, half)
-    kept = lax.dynamic_slice_in_dim(partial, core * half, half)
-    return kept + swap_cores(away)
+    away = partial[half:].astype(kind)
+    return partial[:half] + swap_cores(away).astype(partial.dtype)
+
+
+def own_first(table, core, axis):
+    half = table.shape[axis] // 2
+    mine = lax.dynamic_slice_in_dim(table, core * half, half, axis)
+    theirs = lax.dynamic_slice_in_dim(table, (1 - core) * half, half, axis)
+    return jnp.concatenate([mine, theirs], axis=axis)
 
 
 def exchange(block):
     return lax.all_to_all(block, GRID, split_axis=0, concat_axis=0, tiled=True)
+
+
+LINES = [[z * PLANE + p for z in range(LINE)] for p in range(PLANE)]
+
+
+def line_shift(block, step):
+    pairs = [
+        (s * PLANE + p, (s + step) % LINE * PLANE + p) for s in range(LINE) for p in range(PLANE)
+    ]
+    return lax.ppermute(block, "row", pairs)
+
+
+def plane_pairs(flip):
+    return [(r, r ^ flip) for r in range(PLANE * LINE)]
+
+
+def reorder(block, order, axis):
+    picked = [lax.dynamic_index_in_dim(block, i, axis, True) for i in order]
+    return jnp.concatenate(picked, axis=axis)
+
+
+def row_gather(line, level, place):
+    moved = [lax.ppermute(line, "row", plane_pairs(flip)) for flip in range(1, PLANE)]
+    whole = jnp.concatenate([line, *moved], axis=0)
+    order = [(place ^ p) * LINE + (level - z) % LINE for z in range(LINE) for p in range(PLANE)]
+    return reorder(whole, order, 0).reshape(LINE * PLANE * line.shape[1], line.shape[2])
+
+
+def row_reduce(total, flips, level, place, kind=jnp.bfloat16):
+    block = total.shape[0] // (LINE * PLANE)
+    parts = total.reshape(LINE, 2, 2, block, total.shape[1])
+    for flip in flips:
+        axis = min(3 - flip, parts.ndim - 3)
+        bit = (place // flip) % 2
+        kept = lax.dynamic_index_in_dim(parts, bit, axis, False)
+        away = lax.dynamic_index_in_dim(parts, 1 - bit, axis, False).astype(kind)
+        parts = kept + lax.ppermute(away, "row", plane_pairs(flip)).astype(jnp.float32)
+    order = [(level + step) % LINE for step in range(LINE)]
+    parts = [lax.dynamic_index_in_dim(parts, i, 0, False) for i in order]
+    moved = [line_shift(parts[step].astype(kind), step) for step in range(1, LINE)]
+    total = parts[0]
+    for part in moved:
+        total = total + part.astype(jnp.float32)
+    return total
+
+
+def line_gather(block):
+    whole = lax.all_gather(block, "row", axis=0, tiled=False, axis_index_groups=LINES)
+    return whole
+
+
+def line_reduce(parts):
+    return lax.psum_scatter(
+        parts, "row", scatter_dimension=0, tiled=False, axis_index_groups=LINES
+    )
+
+
+def plane_exchange(block, mate):
+    block = reorder(block, [mate ^ m for m in range(2 * PLANE)], 0)
+    out = [block[0]]
+    for move in range(1, 2 * PLANE):
+        pairs = [(d, d ^ move) for d in range(2 * PLANE * LINE)]
+        out.append(lax.ppermute(block[move], GRID, pairs))
+    return reorder(jnp.stack(out), [mate ^ m for m in range(2 * PLANE)], 0)
+
+
+def plane_all(block):
+    groups = [[z * 2 * PLANE + d for d in range(2 * PLANE)] for z in range(LINE)]
+    return lax.all_to_all(
+        block, GRID, split_axis=0, concat_axis=0, tiled=True, axis_index_groups=groups
+    )
 
 
 def tokens_move(
@@ -473,11 +565,12 @@
     cotangent,
 ):
     bf16, f32 = jnp.bfloat16, jnp.float32
-    core = lax.axis_index("col")
+    core, row = lax.axis_index("col"), lax.axis_index("row")
+    level, place = row // PLANE, row % PLANE
     local = hidden_in.shape[0]
     span = segments.shape[1]
-    rows = MODEL_WIDTH // query_weight.shape[0]
     row_block = query_weight.shape[0]
+    rows = MODEL_WIDTH // row_block
     hidden_block = gate_weight.shape[2]
     ffe = 2 * hidden_block
     capacity = max(2, 3 * span * TOPK // (2 * E))
@@ -485,6 +578,10 @@
     head_cols = query_weight.shape[1]
     kv_cols = key_matrix.shape[1]
     heads = head_cols // HEAD_SIZE
+    mates = 2 * PLANE
+    my_expert = row * 2 + core
+    nt = (((1,), (1,)), ((), ()))
+    tn = (((0,), (0,)), ((), ()))
 
     packed = jnp.concatenate(
         [
@@ -499,28 +596,40 @@
         ],
         axis=1,
     )
-    packed_full = lax.all_gather(packed, "row", axis=0, tiled=True)
+    packed_line = jnp.stack([packed] + [line_shift(packed, step) for step in range(1, LINE)])
+    routes_line = [routes.T] + [line_shift(routes.T, step) for step in range(1, LINE)]
+    routes_line = reorder(jnp.stack(routes_line), [(level - z) % LINE for z in range(LINE)], 0)
+    packed_line = after(packed_line, routes_line)
+    packed_full = row_gather(packed_line, level, place)
     o0 = head_cols + 2 * kv_cols
-    o1 = o0 + head_cols
-    query_cols = packed_full[:, :head_cols]
-    qkv_cols = packed_full[:, :o0]
-    output_t = packed_full[:, o0:o1]
-    router_full = packed_full[:, o1 : o1 + E]
-    gain_first = packed_full[:, o1 + E].astype(f32)
-    gain_second = packed_full[:, o1 + E + 1].astype(f32)
-
-    named, counts = slot_ranks(routes)
-    slot_of = jnp.where(named, counts, -1).T
+    qkv_cols, out_full = packed_full[:, :o0], packed_full[:, o0:]
+    output_t = out_full[:, :head_cols]
+    router_full = out_full[:, head_cols : head_cols + E]
+    gain_first = out_full[:, head_cols + E].astype(f32)
+    gain_second = out_full[:, head_cols + E + 1].astype(f32)
+
+    expert_ids = jnp.arange(E, dtype=jnp.int32)
     share_slots = core * share + jnp.arange(share, dtype=jnp.int32)
-    pick = (slot_of[:, None, :] == share_slots[None, :, None]).astype(bf16)
-    pick = pick.reshape(E * share, span)
-
-    cotangent_all = both_cores(cotangent, core)
-    cot_share = jnp.dot(pick, cotangent_all, preferred_element_type=f32).astype(bf16)
-    upstream = exchange(cot_share)
-    gate_e = exchange(gate_weight)
-    up_e = exchange(up_weight)
-    down_e = exchange(down_weight.transpose(0, 2, 1))
+    picks, masks = [], []
+    for i in range(LINE):
+        named, counts = slot_ranks(routes_line[i].T)
+        slot_of = jnp.where(named, counts, -1).T
+        slot_of = lax.dynamic_slice_in_dim(own_first(slot_of, core, 1), level * mates, mates)
+        pick = (slot_of[:, None, :] == share_slots[None, :, None]).astype(bf16)
+        picks.append(pick.reshape(mates * share, span))
+        masks.append(own_first(jnp.pad(named.astype(bf16), ((0, 0), (0, 128 - E))), core, 0))
+
+    def send_rows(tables, chunks):
+        sent = []
+        for pick, chunk in zip(tables, chunks):
+            part = jnp.dot(pick, chunk, preferred_element_type=f32).astype(bf16)
+            sent.append(part.reshape(mates, 1, share, chunk.shape[1]))
+        return jnp.concatenate(sent, axis=1)
+
+    slots = LINE * share * mates
+
+    gate_up = exchange(after(jnp.concatenate([gate_weight, up_weight], axis=2), packed_line))
+    cot_line = line_gather(after(cotangent, packed_line))
 
     def whole_weight(blocks):
         return (
@@ -529,13 +638,13 @@
             .reshape(MODEL_WIDTH, ffe)
         )
 
-    hidden_all = both_cores(hidden_in, core)
+    hidden_all = both_cores(hidden_in)
     tokens_all = hidden_all.astype(f32)
     scale_all = lax.rsqrt(jnp.mean(tokens_all * tokens_all, axis=-1, keepdims=True) + EPSILON)
     normed_all = (tokens_all * scale_all * gain_first).astype(bf16)
-    segment_ids = segments[0]
-    places = positions(segment_ids)
-    token_index = jnp.arange(span, dtype=jnp.int32)
+    places = own_first(positions(segments[0]), core, 0)
+    segment_ids = own_first(segments[0], core, 0)
+    token_index = own_first(jnp.arange(span, dtype=jnp.int32), core, 0)
     allowed = (segment_ids[:, None] == segment_ids[None, :]) & (
         token_index[None, :] <= token_index[:, None]
     )
@@ -549,72 +658,94 @@
     scaling = HEAD_SIZE ** (-0.5)
     attended, log_total = attend_group((queries, keys, values), allowed, scaling)
     attended_low = attended.transpose(1, 0, 2).reshape(span, head_cols).astype(bf16)
-    branch_part = lax.dot_general(
-        attended_low, output_t, (((1,), (1,)), ((), ())), preferred_element_type=f32
-    )
+    branch_part = lax.dot_general(attended_low, output_t, nt, preferred_element_type=f32)
     tokens_in = hidden_in.astype(f32)
-    hidden_mid = tokens_in + sum_cores(branch_part, core)
+    hidden_mid = tokens_in + sum_cores(branch_part, f32)
     scale_second = lax.rsqrt(jnp.mean(hidden_mid * hidden_mid, axis=-1, keepdims=True) + EPSILON)
     unit_second = hidden_mid * scale_second
     normed_second = (unit_second * gain_second).astype(bf16)
-    second_all = both_cores(normed_second, core)
-
-    logits = jnp.dot(second_all, router_full, preferred_element_type=f32)
-    masked = jnp.where(named, logits, MASKED)
-    exponent = jnp.where(named, jnp.exp(masked - jnp.max(masked, axis=-1, keepdims=True)), 0.0)
-    gates = exponent / jnp.sum(exponent, axis=-1, keepdims=True)
-
-    expert_in = exchange(jnp.dot(pick, second_all, preferred_element_type=f32).astype(bf16))
-    pick3 = pick.reshape(E, share, span)
-    slot_gate = jnp.sum(pick3.astype(f32) * gates.T[:, None, :], axis=-1)
-    slot_gate = exchange(slot_gate).reshape(-1, 1)
-
-    gate_w, up_w, down_t = whole_weight(gate_e), whole_weight(up_e), whole_weight(down_e)
-    nt = (((1,), (1,)), ((), ()))
-    tn = (((0,), (0,)), ((), ()))
+
+    normed_line = line_gather(after(normed_second, gate_up))
+    cot_line = after(cot_line, normed_second)
+    cot_swap = swap_cores(cot_line)
+    cot_rows = [
+        jnp.concatenate([jnp.concatenate([cot_line[i], cot_swap[i]], axis=0), masks[i]], axis=1)
+        for i in range(LINE)
+    ]
+    upstream_rows = plane_all(send_rows(picks, cot_rows))
+    upstream = upstream_rows.reshape(slots, MODEL_WIDTH + 128)
+    mask_rows = upstream[:, MODEL_WIDTH : MODEL_WIDTH + E] > 0
+    upstream = upstream[:, :MODEL_WIDTH].astype(f32)
+
+    normed_swap = swap_cores(normed_line)
+    expert_in = plane_exchange(
+        send_rows(
+            picks,
+            [jnp.concatenate([normed_line[i], normed_swap[i]], axis=0) for i in range(LINE)],
+        ),
+        place * 2 + core,
+    ).reshape(slots, MODEL_WIDTH)
+    down_e = exchange(after(down_weight.transpose(0, 2, 1), upstream_rows))
+
+    logits = jnp.dot(expert_in, router_full, preferred_element_type=f32)
+    top = jnp.max(jnp.where(mask_rows, logits, MASKED), axis=-1, keepdims=True)
+    exponent = jnp.where(mask_rows, jnp.exp(logits - top), 0.0)
+    gates = exponent / jnp.maximum(jnp.sum(exponent, axis=-1, keepdims=True), 1e-30)
+    mine = (expert_ids == my_expert)[None, :]
+    slot_gate = jnp.sum(jnp.where(mine, gates, 0.0), axis=-1, keepdims=True)
+    gate_w = whole_weight(gate_up[:, :, :hidden_block])
+    up_w = whole_weight(gate_up[:, :, hidden_block:])
+    down_t = whole_weight(down_e)
     gate_value = jnp.dot(expert_in, gate_w, preferred_element_type=f32)
     up_value = jnp.dot(expert_in, up_w, preferred_element_type=f32)
     sigmoid_gate = jax.nn.sigmoid(gate_value)
     silu_gate = gate_value * sigmoid_gate
     activation = (silu_gate * up_value).astype(bf16)
     expert_out = lax.dot_general(activation, down_t, nt, preferred_element_type=f32)
-    up32 = upstream.astype(f32)
-    slot_grad = jnp.sum(expert_out * up32, axis=-1)
-    returned = exchange((expert_out * slot_gate).astype(bf16))
-    grad_expert = (up32 * slot_gate).astype(bf16)
+    slot_grad = jnp.sum(expert_out * upstream, axis=-1, keepdims=True)
+    pick_grad = slot_gate * slot_grad
+    grad_logits = (pick_grad * (jnp.where(mine, 1.0, 0.0) - gates)).astype(bf16)
+    grad_expert = (upstream * slot_gate).astype(bf16)
     grad_act = jnp.dot(grad_expert, down_t, preferred_element_type=f32)
     slope = sigmoid_gate * (1.0 + gate_value * (1.0 - sigmoid_gate))
     grad_gate = (grad_act * up_value * slope).astype(bf16)
     grad_up = (grad_act * silu_gate).astype(bf16)
     grad_in = lax.dot_general(grad_gate, gate_w, nt, preferred_element_type=f32)
     grad_in = grad_in + lax.dot_general(grad_up, up_w, nt, preferred_element_type=f32)
-    grad_back = exchange(grad_in.astype(bf16))
-    slot_grad = exchange(slot_grad.reshape(E, share))
+    grad_in = grad_in + lax.dot_general(grad_logits, router_full, nt, preferred_element_type=f32)
+
+    def combine(got):
+        parts = []
+        for i, pick in enumerate(picks):
+            part = got[:, i].reshape(mates * share, MODEL_WIDTH)
+            parts.append(lax.dot_general(pick, part, tn, preferred_element_type=f32))
+        parts = jnp.stack(parts)
+        away = swap_cores(parts[:, local:].astype(bf16))
+        parts = parts[:, :local] + away.astype(f32)
+        return line_reduce(parts.astype(bf16)).astype(f32)
+
+    shape = (mates, LINE, share, MODEL_WIDTH)
+    grad_back = plane_all(grad_in.astype(bf16).reshape(shape))
+    grad_normed = combine(grad_back)
+    router_grad = lax.dot_general(expert_in, grad_logits, tn, preferred_element_type=f32)
 
     def shard_grad(left, right):
         full = lax.dot_general(left, right, tn, preferred_element_type=f32).astype(bf16)
         blocks = full.reshape(rows, row_block, 2, hidden_block).transpose(0, 2, 1, 3)
-        return exchange(blocks.reshape(E, row_block, hidden_block)).astype(f32)
-
-    def combine(slots):
-        return sum_cores(lax.dot_general(pick, slots, tn, preferred_element_type=f32), core)
-
-    input_own = combine(grad_back.reshape(E * share, MODEL_WIDTH))
-    pick_part = jnp.sum(pick3.astype(f32) * slot_grad[:, :, None], axis=1).T
-    pick_own = sum_cores(pick_part, core)
-    own_gates = lax.dynamic_slice_in_dim(gates, core * local, local)
-    centred = own_gates * (pick_own - jnp.sum(own_gates * pick_own, axis=-1, keepdims=True))
-    grad_logits = centred.astype(bf16)
-    grad_normed = input_own + lax.dot_general(
-        grad_logits, router_full, nt, preferred_element_type=f32
-    )
-    router_grad = lax.dot_general(normed_second, grad_logits, tn, preferred_element_type=f32)
+        return blocks.reshape(E, row_block, hidden_block)
+
+    mixture = (expert_out * slot_gate).astype(bf16).reshape(shape)
+    mixture = plane_all(after(mixture, grad_back))
+    down_home = exchange(after(shard_grad(grad_expert, activation), mixture))
+    gate_home = exchange(after(shard_grad(expert_in, grad_gate), down_home))
+    up_home = exchange(after(shard_grad(expert_in, grad_up), gate_home))
+
     tilted = grad_normed * gain_second
     gain_second_grad = jnp.sum(grad_normed * unit_second, axis=0)
     grad_hidden = cotangent.astype(f32) + scale_second * (
         tilted - unit_second * jnp.mean(tilted * unit_second, axis=-1, keepdims=True)
     )
-    branch_all = both_cores(grad_hidden.astype(bf16), core)
+    branch_all = both_cores(grad_hidden.astype(bf16))
 
     output_t_grad = lax.dot_general(branch_all, attended_low, tn, preferred_element_type=f32)
     grad_attended = jnp.dot(branch_all, output_t, preferred_element_type=f32).astype(bf16)
@@ -629,41 +760,61 @@
     )
     grad_key_low = apply_rotary(grad_keys[:, None], places, -1.0)[:, 0].astype(bf16)
     grad_qkv = jnp.concatenate([grad_query_low, grad_key_low, grad_values.astype(bf16)], axis=1)
+    qkv_grad = lax.dot_general(normed_all, grad_qkv, tn, preferred_element_type=f32)
     first_part = lax.dot_general(grad_qkv, qkv_cols, nt, preferred_element_type=f32)
-    qkv_grad = lax.dot_general(normed_all, grad_qkv, tn, preferred_element_type=f32)
-    grad_first = sum_cores(first_part, core)
-    scale_first = lax.dynamic_slice_in_dim(scale_all, core * local, local)
-    unit_first = tokens_in * scale_first
+    grad_first = sum_cores(first_part, f32)
+    unit_first = tokens_in * scale_all[:local]
     tilted_first = grad_first * gain_first
     gain_first_grad = jnp.sum(grad_first * unit_first, axis=0)
-    input_grad = grad_hidden + scale_first * (
+    input_grad = grad_hidden + scale_all[:local] * (
         tilted_first - unit_first * jnp.mean(tilted_first * unit_first, axis=-1, keepdims=True)
     )
-    block_out = (hidden_mid + combine(returned.reshape(E * share, MODEL_WIDTH))).astype(bf16)
-
-    gate_out = shard_grad(expert_in, grad_gate)
-    up_out = shard_grad(expert_in, grad_up)
-    down_out = shard_grad(grad_expert, activation).transpose(0, 2, 1)
-    packed_grad = jnp.concatenate([qkv_grad, output_t_grad], axis=1).astype(bf16)
-    packed_own = lax.psum_scatter(packed_grad, "row", scatter_dimension=0, tiled=True).astype(f32)
-    small = jnp.concatenate(
-        [router_grad, gain_first_grad[:, None], gain_second_grad[:, None]], axis=1
-    )
-    small = lax.psum(small, GRID)
-    small_own = lax.dynamic_slice_in_dim(small, lax.axis_index("row") * row_block, row_block)
+    mixture = combine(after(mixture, grad_qkv))
+    block_out = (hidden_mid + mixture).astype(bf16)
+
+    extra = jnp.concatenate(
+        [
+            router_grad,
+            gain_second_grad[:, None],
+            jnp.zeros((MODEL_WIDTH, 128 - E - 1), f32),
+        ],
+        axis=1,
+    )
+    half = head_cols // 2
+    output_own = [
+        row_reduce(output_t_grad[:, :half], (1, 2), level, place),
+        row_reduce(
+            jnp.concatenate([output_t_grad[:, half:], extra], axis=1), (2, 1), level, place
+        ),
+    ]
+    output_own = jnp.concatenate(output_own, axis=1)
+    small_own = output_own[:, head_cols:]
+    small_own = small_own + swap_cores(small_own)
+    qkv_grad = after(qkv_grad, gate_home)
+    half = qkv_grad.shape[1] // 2
+    qkv_own = jnp.concatenate(
+        [
+            row_reduce(qkv_grad[:, :half], (1, 2), level, place),
+            row_reduce(qkv_grad[:, half:], (2, 1), level, place),
+        ],
+        axis=1,
+    )
+    gain_parts = gain_first_grad.reshape(rows, row_block)
+    gain_first_own = row_reduce(gain_parts, (1, 2), level, place, f32)[0]
+    gain_first_own = gain_first_own + swap_cores(gain_first_own)
     return (
         block_out,
         input_grad,
+        gain_first_own,
+        qkv_own[:, :head_cols],
+        qkv_own[:, head_cols : head_cols + kv_cols],
+        qkv_own[:, head_cols + kv_cols :],
+        output_own[:, :head_cols].T,
         small_own[:, E],
-        packed_own[:, :head_cols],
-        packed_own[:, head_cols : head_cols + kv_cols],
-        packed_own[:, head_cols + kv_cols : o0],
-        packed_own[:, o0:].T,
-        small_own[:, E + 1],
         small_own[:, :E],
-        gate_out,
-        up_out,
-        down_out,
+        gate_home.astype(f32),
+        up_home.astype(f32),
+        down_home.astype(f32).transpose(0, 2, 1),
     )
 
 
@@ -699,7 +850,7 @@
         P(None, "col", "row"),
     )
     rows, cols = mesh.shape["row"], mesh.shape["col"]
-    one_each = rows * cols == E and cols == KEY_VALUE_HEADS
+    one_each = rows == 4 * PLANE and cols == KEY_VALUE_HEADS and rows * cols == E
     return jax.shard_map(
         tokens_move if one_each else weights_move, mesh=mesh,
         in_specs=in_specs,

time: 1100 us -> 926 us (0.84)
  waiting for transfers between devices: 619 us -> 472 us
  blocking collectives: 98.7 us -> 0 us
  starting transfers between devices: 49.5 us -> 93.6 us
  local copies, waits for them, and re-layouts: 98 us -> 122 us
  other arithmetic: 69 us -> 86.9 us
  matrix products: 137 us -> 124 us
    all_to_all x10 -> x5, waiting for transfers between devices: 419 us -> 57.9 us  [exchange(): return lax.all_to_all(block, GRID, split_axis=0, concat_axis=0, tiled=True)]
    ppermute x0 -> x41, waiting for transfers between devices: none -> 257 us  [the longest x21 124 us: line_shift(): return lax.ppermute(block, 'row', pairs)]
    unnamed x4, waiting for transfers between devices: 144 us -> 0.07 us
    all_to_all x2 -> x0, blocking collectives: 98.7 us -> none  [exchange(): return lax.all_to_all(block, GRID, split_axis=0, concat_axis=0, tiled=True)]
    all_to_all x0 -> x3, waiting for transfers between devices: none -> 95.3 us  [plane_all(): lax.all_to_all(block, GRID, split_axis=0, concat_axis=0, tiled=True, axis...]
    ppermute x0 -> x41, starting transfers between devices: none -> 59.7 us  [the longest x21 37.3 us: line_shift(): return lax.ppermute(block, 'row', pairs)]
    all_to_all x10 -> x5, starting transfers between devices: 46.4 us -> 18.4 us  [exchange(): return lax.all_to_all(block, GRID, split_axis=0, concat_axis=0, tiled=True)]
    slice x3 -> x15, local copies, waits for them, and re-layouts: 1.48 us -> 20.3 us  [the longest x2 5.33 us: combine(): part = got[:, i].reshape(mates * share, MODEL_WIDTH)]
  transfers between devices with their start and end apart: 22 -> 63, of which waited for: 15 -> 28; matrix products, arithmetic and copies ran while one was open for 23% -> 27% of each run, Pallas kernels for 0% -> 0%
where the time goes in v2:
time: 926 us; the launch traced here: 917 us
  waiting for transfers between devices  472 us (51%)
  matrix products  124 us (13%)
  local copies, waits for them, and re-layouts  122 us (13%)
  starting transfers between devices  93.6 us (10%)
  other arithmetic  86.9 us (9%)
  between operations  17 us (2%)
    ppermute x21, waiting for transfers between devices, line_shift(): return lax.ppermute(block, 'row', pairs)  124 us
    all_to_all x3, waiting for transfers between devices, plane_all(): lax.all_to_all(block, GRID, split_axis=0, concat_axis=0, tiled=True, axis...  95.3 us
    ppermute x3, waiting for transfers between devices, row_gather(): lax.ppermute(line, 'row', plane_pairs(flip))  75.6 us
    all_to_all x5, waiting for transfers between devices, exchange(): return lax.all_to_all(block, GRID, split_axis=0, concat_axis=0, tiled=True)  57.9 us
    all_gather x2, waiting for transfers between devices, line_gather(): lax.all_gather(block, 'row', axis=0, tiled=False, axis_index_groups=LINES)  57.9 us
    ppermute x7, waiting for transfers between devices, plane_exchange(): out.append(lax.ppermute(block[move], GRID, pairs))  44.5 us
    unnamed x285, local copies, waits for them, and re-layouts  44 us
    ppermute x21, starting transfers between devices, line_shift(): return lax.ppermute(block, 'row', pairs)  37.3 us
  transfers between devices with their start and end apart: 63, of which 28 were waited for; matrix products, arithmetic and copies ran while one was open for 27% of the time, Pallas kernels for 0%

profile of v2, /device:TPU:0, one launch (start us, length us, event | category | flops | bytes accessed | tf_op | source)
XLA Modules:
  0.0 916.7 jit_solution(12878544821987967621)
XLA Ops:
  23.4 6.4 collective-permute-done.3
  29.8 22.1 %collective-permute-done.2 = bf16[96,1920]{1,0:T(8,128)(2,1)} collective-permute-done((bf16[96,1920]{1,0:T(8,128)(2,1)S(1)}, bf16[96,1920]{1,0:T(8,128)(2,1)}, u32[]{:S(2)}, u32[]{:S(2)}) %collective-permute-start.2) | collective-permute-done | bytes 368672 | tf_op jit(solution)/shard_map/ppermute | solution.py:487
  58.3 5.2 pad_maximum_fusion.4.refs_0_
  70.2 33.0 %collective-permute-done.9 = bf16[4,96,1920]{2,1,0:T(8,128)(2,1)} collective-permute-done((bf16[4,96,1920]{2,1,0:T(8,128)(2,1)}, bf16[4,96,1920]{2,1,0:T(8,128)(2,1)}, u32[]{:S(2)}, u32[]{:S(2)}) %collective-permute-start.9) | collective-permute-done | bytes 1474592 | tf_op jit(solution)/shard_map/ppermute | solution.py:500
  103.2 35.5 %collective-permute-done.8 = bf16[4,96,1920]{2,1,0:T(8,128)(2,1)} collective-permute-done((bf16[4,96,1920]{2,1,0:T(8,128)(2,1)}, bf16[4,96,1920]{2,1,0:T(8,128)(2,1)}, u32[]{:S(2)}, u32[]{:S(2)}) %collective-permute-start.8) | collective-permute-done | bytes 1474592 | tf_op jit(solution)/shard_map/ppermute | solution.py:500
  138.7 7.2 collective-permute-done.7
  194.6 9.4 %all-gather.7.cloned.1.call-done = bf16[1024,1536]{1,0:T(8,128)(2,1)} async-done(((bf16[256,1536]{1,0:T(8,128)(2,1)}), bf16[1024,1536]{1,0:T(8,128)(2,1)}) %all-gather.7.cloned.1.call-update) | async-done | bytes 3145744 | tf_op jit(solution)/shard_map/all_gather | solution.py:525
  212.9 12.4 %all-to-all-done.refs_1_ = bf16[32,96,768]{2,1,0:T(8,128)(2,1)} async-done(((bf16[32,96,768]{2,1,0:T(8,128)(2,1)}), bf16[32,96,768]{2,1,0:T(8,128)(2,1)}, u32[]{:S(2)}, u32[]{:S(2)}) %all-to-all-start) | async-done | bytes 4718624 | tf_op jit(solution)/shard_map/all_to_all | solution.py:477
  239.5 48.4 %all-gather.5.cloned.1.call-done = bf16[1024,1536]{1,0:T(8,128)(2,1)} async-done(((bf16[256,1536]{1,0:T(8,128)(2,1)}), bf16[1024,1536]{1,0:T(8,128)(2,1)}) %all-gather.5.cloned.1.call-update) | async-done | bytes 3145744 | tf_op jit(solution)/shard_map/all_gather | solution.py:525
  287.9 10.5 %all-to-all-done.1.refs_1_ = bf16[8,4,48,1664]{3,2,1,0:T(8,128)(2,1)} async-done(((bf16[8,4,48,1664]{3,2,1,0:T(8,128)(2,1)}), bf16[8,4,48,1664]{3,2,1,0:T(8,128)(2,1)}, u32[]{:S(2)}, u32[]{:S(2)}) %all-to-all-start.1) | async-done | bytes 5111840 | tf_op jit(solution)/shard_map/all_to_all | solution.py:546
  325.1 30.8 %all-to-all-done.2 = bf16[32,96,384]{2,1,0:T(8,128)(2,1)S(1)} async-done(((bf16[32,96,384]{2,1,0:T(8,128)(2,1)}), bf16[32,96,384]{2,1,0:T(8,128)(2,1)S(1)}, u32[]{:S(2)}, u32[]{:S(2)}) %all-to-all-start.2) | async-done | bytes 2359328 | tf_op jit(solution)/shard_map/all_to_all | solution.py:477
  367.6 32.4 %collective-permute-done.14 = bf16[4,48,1536]{2,1,0:T(8,128)(2,1)S(1)} collective-permute-done((bf16[4,48,1536]{2,1,0:T(8,128)(2,1)S(1)}, bf16[4,48,1536]{2,1,0:T(8,128)(2,1)S(1)}, u32[]{:S(2)}, u32[]{:S(2)}) %collective-permute-start.14) | collective-permute-done | bytes 589856 | tf_op jit(solution)/shard_map/ppermute | solution.py:540
  400.8 12.1 %collective-permute-done.15 = bf16[4,48,1536]{2,1,0:T(8,128)(2,1)S(1)} collective-permute-done((bf16[4,48,1536]{2,1,0:T(8,128)(2,1)S(1)}, bf16[4,48,1536]{2,1,0:T(8,128)(2,1)S(1)}, u32[]{:S(2)}, u32[]{:S(2)}) %collective-permute-start.15) | collective-permute-done | bytes 589856 | tf_op jit(solution)/shard_map/ppermute | solution.py:540
  433.0 6.1 fusion.84
  439.2 6.7 multiply_convert_fusion.2
  445.9 9.8 %fusion.1 = (f32[1536]{0:T(1024)S(1)}, bf16[1536,1536]{1,0:T(8,128)(2,1)}) fusion(bf16[1536,1664]{1,0:T(8,128)(2,1)} %bitcast.94, f32[1536]{0:T(1024)S(1)} %get-tuple-element.76, bf16[1536,768]{1,0:T(8,128)(2,1)S(1)} %get-tuple-element.84, bf16[1536,768]{1,0:T(8,128)(2,1)S(1)} %bitcast.457), kind=kOutput, calls=%fused_computation.6 | convolution fusion | flops 3635673600 | bytes 14168064 | tf_op jit(solution)/shard_map/dot_general | solution.py:704
  474.2 54.2 %all-to-all-done.3.refs_1_ = bf16[8,4,48,1536]{3,2,1,0:T(8,128)(2,1)} async-done(((bf16[8,4,48,1536]{3,2,1,0:T(8,128)(2,1)}), bf16[8,4,48,1536]{3,2,1,0:T(8,128)(2,1)}, u32[]{:S(2)}, u32[]{:S(2)}) %all-to-all-start.3) | async-done | bytes 4718624 | tf_op jit(solution)/shard_map/all_to_all | solution.py:546
  547.4 6.4 fusion.4
  555.4 7.9 convolution_convert_fusion.1
  570.3 30.7 %all-to-all-done.4.refs_0_.refs_1_ = bf16[8,4,48,1536]{3,2,1,0:T(8,128)(2,1)} async-done(((bf16[8,4,48,1536]{3,2,1,0:T(8,128)(2,1)}), bf16[8,4,48,1536]{3,2,1,0:T(8,128)(2,1)}, u32[]{:S(2)}, u32[]{:S(2)}) %all-to-all-start.4) | async-done | bytes 4718624 | tf_op jit(solution)/shard_map/all_to_all | solution.py:546
  605.4 6.8 copy.301
  612.2 7.7 convolution_convert_fusion.2
  626.8 6.2 convolution_convert_fusion
  647.9 14.7 %all-to-all-done.5.refs_1_ = bf16[32,96,384]{2,1,0:T(8,128)(2,1)} async-done(((bf16[32,96,384]{2,1,0:T(8,128)(2,1)}), bf16[32,96,384]{2,1,0:T(8,128)(2,1)}, u32[]{:S(2)}, u32[]{:S(2)}) %all-to-all-start.5) | async-done | bytes 2359328 | tf_op jit(solution)/shard_map/all_to_all | solution.py:477
  679.5 5.3 fusion.91
  729.9 6.4 collective-permute-done.45
  757.0 6.0 collective-permute-done.43
  764.5 16.0 %collective-permute-done.48 = bf16[96,512]{1,0:T(8,128)(2,1)S(1)} collective-permute-done((bf16[96,512]{1,0:T(8,128)(2,1)S(1)}, bf16[96,512]{1,0:T(8,128)(2,1)S(1)}, u32[]{:S(2)}, u32[]{:S(2)}) %collective-permute-start.48) | collective-permute-done | bytes 98336 | tf_op jit(solution)/shard_map/ppermute | solution.py:487
  804.5 45.0 %collective-permute-done.26 = f32[1,96]{1,0:T(1,128)S(1)} collective-permute-done((f32[1,96]{1,0:T(1,128)S(1)}, f32[1,96]{1,0:T(1,128)S(1)}, u32[]{:S(2)}, u32[]{:S(2)}) %collective-permute-start.26) | collective-permute-done | bytes 416 | tf_op jit(solution)/shard_map/ppermute | solution.py:487
  849.6 15.7 %collective-permute-done.27 = f32[1,96]{1,0:T(1,128)S(1)} collective-permute-done((f32[1,96]{1,0:T(1,128)S(1)}, f32[1,96]{1,0:T(1,128)S(1)}, u32[]{:S(2)}, u32[]{:S(2)}) %collective-permute-start.27) | collective-permute-done | bytes 416 | tf_op jit(solution)/shard_map/ppermute | solution.py:487
  888.1 5.7 collective-permute-done.33
  893.9 5.1 collective-permute-done.38
  (604 shorter events, 371.8 us)
Async XLA Ops:
  7.3 196.7 %all-gather.7.cloned.1.call-start = ((), (), s32[]{:S(2)}) async-start(), calls=%async_computation.13 | async-start | bytes 3932160 | tf_op jit(solution)/shard_map/all_gather | solution.py:525
  19.3 32.6 %collective-permute-start.2 = (bf16[96,1920]{1,0:T(8,128)(2,1)S(1)}, bf16[96,1920]{1,0:T(8,128)(2,1)}, u32[]{:S(2)}, u32[]{:S(2)}) collective-permute-start(bf16[96,1920]{1,0:T(8,128)(2,1)S(1)} %concatenate.146), channel_id=1, source_target_pairs={{0,16},{2,18},{4,20},{6,22},{8,24},{10,26},{12,28},{14,30},{16,0},... | collective-permute-start | bytes 1105928 | tf_op jit(solution)/shard_map/ppermute | solution.py:487
  20.8 31.1 %collective-permute-start.1 = (bf16[96,1920]{1,0:T(8,128)(2,1)S(1)}, bf16[96,1920]{1,0:T(8,128)(2,1)}, u32[]{:S(2)}, u32[]{:S(2)}) collective-permute-start(bf16[96,1920]{1,0:T(8,128)(2,1)S(1)} %concatenate.146), channel_id=1, source_target_pairs={{0,8},{2,10},{4,12},{6,14},{8,16},{10,18},{12,20},{14,22},{16,24},... | collective-permute-start | bytes 1105928 | tf_op jit(solution)/shard_map/ppermute | solution.py:487
  22.7 47.1 %collective-permute-start = (bf16[256,1536]{1,0:T(8,128)(2,1)S(1)}, bf16[256,1536]{1,0:T(8,128)(2,1)S(1)}, u32[]{:S(2)}, u32[]{:S(2)}) collective-permute-start(bf16[256,1536]{1,0:T(8,128)(2,1)S(1)} %copy-done.7), channel_id=1, source_target_pairs={{0,1},{1,0},{2,3},{3,2},{4,5},{5,4},{6,7},{7,6},{8,9},{9,8},{10,11... | collective-permute-start | bytes 2359304 | tf_op jit(solution)/shard_map/ppermute | solution.py:456
  54.4 48.8 %collective-permute-start.9 = (bf16[4,96,1920]{2,1,0:T(8,128)(2,1)}, bf16[4,96,1920]{2,1,0:T(8,128)(2,1)}, u32[]{:S(2)}, u32[]{:S(2)}) collective-permute-start(bf16[4,96,1920]{2,1,0:T(8,128)(2,1)} %after.12.refs_1_), channel_id=1, source_target_pairs={{0,6},{2,4},{4,2},{6,0},{8,14},{10,12},{12,10},{14,8},{16,22},{18,... | collective-permute-start | bytes 4423688 | tf_op jit(solution)/shard_map/ppermute | solution.py:500
  56.9 81.8 %collective-permute-start.8 = (bf16[4,96,1920]{2,1,0:T(8,128)(2,1)}, bf16[4,96,1920]{2,1,0:T(8,128)(2,1)}, u32[]{:S(2)}, u32[]{:S(2)}) collective-permute-start(bf16[4,96,1920]{2,1,0:T(8,128)(2,1)} %after.12.refs_1_), channel_id=1, source_target_pairs={{0,4},{2,6},{4,0},{6,2},{8,12},{10,14},{12,8},{14,10},{16,20},{18,... | collective-permute-start | bytes 4423688 | tf_op jit(solution)/shard_map/ppermute | solution.py:500
  57.4 88.5 %collective-permute-start.7 = (bf16[4,96,1920]{2,1,0:T(8,128)(2,1)}, bf16[4,96,1920]{2,1,0:T(8,128)(2,1)}, u32[]{:S(2)}, u32[]{:S(2)}) collective-permute-start(bf16[4,96,1920]{2,1,0:T(8,128)(2,1)} %after.12.refs_1_), channel_id=1, source_target_pairs={{0,2},{2,0},{4,6},{6,4},{8,10},{10,8},{12,14},{14,12},{16,18},{18,... | collective-permute-start | bytes 4423688 | tf_op jit(solution)/shard_map/ppermute | solution.py:500
  65.4 159.8 %all-to-all-start = ((bf16[32,96,768]{2,1,0:T(8,128)(2,1)}), bf16[32,96,768]{2,1,0:T(8,128)(2,1)}, u32[]{:S(2)}, u32[]{:S(2)}) async-start(bf16[32,96,768]{2,1,0:T(8,128)(2,1)} %after.13), calls=%async_computation | async-start | bytes 9437184 | tf_op jit(solution)/shard_map/all_to_all | solution.py:477
  204.0 83.9 %all-gather.5.cloned.1.call-start = ((), (), s32[]{:S(2)}) async-start(), calls=%async_computation.12 | async-start | bytes 3932160 | tf_op jit(solution)/shard_map/all_gather | solution.py:525
  234.8 63.6 %all-to-all-start.1 = ((bf16[8,4,48,1664]{3,2,1,0:T(8,128)(2,1)}), bf16[8,4,48,1664]{3,2,1,0:T(8,128)(2,1)}, u32[]{:S(2)}, u32[]{:S(2)}) async-start(bf16[8,4,48,1664]{3,2,1,0:T(8,128)(2,1)} %pad_maximum_fusion.3), calls=%async_computation.1 | async-start | bytes 10223616 | tf_op jit(solution)/shard_map/all_to_all | solution.py:546
  298.4 57.5 %all-to-all-start.2 = ((bf16[32,96,384]{2,1,0:T(8,128)(2,1)}), bf16[32,96,384]{2,1,0:T(8,128)(2,1)S(1)}, u32[]{:S(2)}, u32[]{:S(2)}) async-start(bf16[32,96,384]{2,1,0:T(8,128)(2,1)} %after.17), calls=%async_computation.2 | async-start | bytes 4718592 | tf_op jit(solution)/shard_map/all_to_all | solution.py:477
  311.2 50.9 %collective-permute-start.12 = (bf16[4,48,1536]{2,1,0:T(8,128)(2,1)}, bf16[4,48,1536]{2,1,0:T(8,128)(2,1)}, u32[]{:S(2)}, u32[]{:S(2)}) collective-permute-start(bf16[4,48,1536]{2,1,0:T(8,128)(2,1)} %get-tuple-element.107), channel_id=1, source_target_pairs={{0,1},{1,0},{2,3},{3,2},{4,5},{5,4},{6,7},{7,6},{8,9},{9,8},{10,11... | collective-permute-start | bytes 1769480 | tf_op jit(solution)/shard_map/ppermute | solution.py:540
  312.4 52.8 %collective-permute-start.13 = (bf16[4,48,1536]{2,1,0:T(8,128)(2,1)}, bf16[4,48,1536]{2,1,0:T(8,128)(2,1)}, u32[]{:S(2)}, u32[]{:S(2)}) collective-permute-start(bf16[4,48,1536]{2,1,0:T(8,128)(2,1)} %get-tuple-element.106), channel_id=1, source_target_pairs={{0,2},{1,3},{2,0},{3,1},{4,6},{5,7},{6,4},{7,5},{8,10},{9,11},{10,... | collective-permute-start | bytes 1769480 | tf_op jit(solution)/shard_map/ppermute | solution.py:540
  358.6 56.9 %collective-permute-start.18 = (bf16[4,48,1536]{2,1,0:T(8,128)(2,1)S(1)}, bf16[4,48,1536]{2,1,0:T(8,128)(2,1)S(1)}, u32[]{:S(2)}, u32[]{:S(2)}) collective-permute-start(bf16[4,48,1536]{2,1,0:T(8,128)(2,1)S(1)} %get-tuple-element.101), channel_id=1, source_target_pairs={{0,7},{1,6},{2,5},{3,4},{4,3},{5,2},{6,1},{7,0},{8,15},{9,14},{10,... | collective-permute-start | bytes 1769480 | tf_op jit(solution)/shard_map/ppermute | solution.py:540
  360.0 54.7 %collective-permute-start.17 = (bf16[4,48,1536]{2,1,0:T(8,128)(2,1)S(1)}, bf16[4,48,1536]{2,1,0:T(8,128)(2,1)S(1)}, u32[]{:S(2)}, u32[]{:S(2)}) collective-permute-start(bf16[4,48,1536]{2,1,0:T(8,128)(2,1)S(1)} %get-tuple-element.102), channel_id=1, source_target_pairs={{0,6},{1,7},{2,4},{3,5},{4,2},{5,3},{6,0},{7,1},{8,14},{9,15},{10,... | collective-permute-start | bytes 1769480 | tf_op jit(solution)/shard_map/ppermute | solution.py:540
  360.9 53.0 %collective-permute-start.16 = (bf16[4,48,1536]{2,1,0:T(8,128)(2,1)S(1)}, bf16[4,48,1536]{2,1,0:T(8,128)(2,1)S(1)}, u32[]{:S(2)}, u32[]{:S(2)}) collective-permute-start(bf16[4,48,1536]{2,1,0:T(8,128)(2,1)S(1)} %copy-done.52), channel_id=1, source_target_pairs={{0,5},{1,4},{2,7},{3,6},{4,1},{5,0},{6,3},{7,2},{8,13},{9,12},{10,... | collective-permute-start | bytes 1769480 | tf_op jit(solution)/shard_map/ppermute | solution.py:540
  362.2 37.8 %collective-permute-start.14 = (bf16[4,48,1536]{2,1,0:T(8,128)(2,1)S(1)}, bf16[4,48,1536]{2,1,0:T(8,128)(2,1)S(1)}, u32[]{:S(2)}, u32[]{:S(2)}) collective-permute-start(bf16[4,48,1536]{2,1,0:T(8,128)(2,1)S(1)} %copy-done.54), channel_id=1, source_target_pairs={{0,3},{1,2},{2,1},{3,0},{4,7},{5,6},{6,5},{7,4},{8,11},{9,10},{10,... | collective-permute-start | bytes 1769480 | tf_op jit(solution)/shard_map/ppermute | solution.py:540
  365.2 47.8 %collective-permute-start.15 = (bf16[4,48,1536]{2,1,0:T(8,128)(2,1)S(1)}, bf16[4,48,1536]{2,1,0:T(8,128)(2,1)S(1)}, u32[]{:S(2)}, u32[]{:S(2)}) collective-permute-start(bf16[4,48,1536]{2,1,0:T(8,128)(2,1)S(1)} %copy-done.53), channel_id=1, source_target_pairs={{0,4},{1,5},{2,6},{3,7},{4,0},{5,1},{6,2},{7,3},{8,12},{9,13},{10,... | collective-permute-start | bytes 1769480 | tf_op jit(solution)/shard_map/ppermute | solution.py:540
  468.6 59.7 %all-to-all-start.3 = ((bf16[8,4,48,1536]{3,2,1,0:T(8,128)(2,1)}), bf16[8,4,48,1536]{3,2,1,0:T(8,128)(2,1)}, u32[]{:S(2)}, u32[]{:S(2)}) async-start(bf16[8,4,48,1536]{3,2,1,0:T(8,128)(2,1)} %bitcast.427), calls=%async_computation.3 | async-start | bytes 9437184 | tf_op jit(solution)/shard_map/all_to_all | solution.py:546
  541.6 59.4 %all-to-all-start.4 = ((bf16[8,4,48,1536]{3,2,1,0:T(8,128)(2,1)}), bf16[8,4,48,1536]{3,2,1,0:T(8,128)(2,1)}, u32[]{:S(2)}, u32[]{:S(2)}) async-start(bf16[8,4,48,1536]{3,2,1,0:T(8,128)(2,1)} %after.18), calls=%async_computation.4 | async-start | bytes 9437184 | tf_op jit(solution)/shard_map/all_to_all | solution.py:546
  546.2 92.6 %reduce-scatter.3.cloned.1.call-start = ((), (), s32[]{:S(2)}) async-start(), calls=%async_computation.10 | async-start | bytes 3932160 | tf_op jit(solution)/shard_map/reduce_scatter | solution.py:530
  601.0 61.7 %all-to-all-start.5 = ((bf16[32,96,384]{2,1,0:T(8,128)(2,1)}), bf16[32,96,384]{2,1,0:T(8,128)(2,1)}, u32[]{:S(2)}, u32[]{:S(2)}) async-start(bf16[32,96,384]{2,1,0:T(8,128)(2,1)} %after.20), calls=%async_computation.7 | async-start | bytes 4718592 | tf_op jit(solution)/shard_map/all_to_all | solution.py:477
  662.7 120.2 %all-to-all-start.6 = ((bf16[32,96,384]{2,1,0:T(8,128)(2,1)}), bf16[32,96,384]{2,1,0:T(8,128)(2,1)}, u32[]{:S(2)}, u32[]{:S(2)}) async-start(bf16[32,96,384]{2,1,0:T(8,128)(2,1)} %after.21), calls=%async_computation.8 | async-start | bytes 4718592 | tf_op jit(solution)/shard_map/all_to_all | solution.py:477
  666.8 238.3 %reduce-scatter.5.cloned.1.call-start = ((), (), s32[]{:S(2)}) async-start(), calls=%async_computation.11 | async-start | bytes 3932160 | tf_op jit(solution)/shard_map/reduce_scatter | solution.py:530
  705.6 33.8 %collective-permute-start.22 = (bf16[4,256,1536]{2,1,0:T(8,128)(2,1)S(1)}, bf16[4,256,1536]{2,1,0:T(8,128)(2,1)}, u32[]{:S(2)}, u32[]{:S(2)}) collective-permute-start(bf16[4,256,1536]{2,1,0:T(8,128)(2,1)S(1)} %slice.414), channel_id=1, source_target_pairs={{0,1},{1,0},{2,3},{3,2},{4,5},{5,4},{6,7},{7,6},{8,9},{9,8},{10,11... | collective-permute-start | bytes 9437192 | tf_op jit(solution)/shard_map/ppermute | solution.py:456
  718.6 62.8 %collective-permute-start.23 = (f32[256,1536]{1,0:T(8,128)}, f32[256,1536]{1,0:T(8,128)S(1)}, u32[]{:S(2)}, u32[]{:S(2)}) collective-permute-start(f32[256,1536]{1,0:T(8,128)} %slice.321), channel_id=1, source_target_pairs={{0,1},{1,0},{2,3},{3,2},{4,5},{5,4},{6,7},{7,6},{8,9},{9,8},{10,11... | collective-permute-start | bytes 4718600 | tf_op jit(solution)/shard_map/ppermute | solution.py:456
  782.9 117.6 %all-to-all-start.7 = ((bf16[32,96,384]{2,1,0:T(8,128)(2,1)}), bf16[32,96,384]{2,1,0:T(8,128)(2,1)}, u32[]{:S(2)}, u32[]{:S(2)}) async-start(bf16[32,96,384]{2,1,0:T(8,128)(2,1)} %after.23), calls=%async_computation.9 | async-start | bytes 4718592 | tf_op jit(solution)/shard_map/all_to_all | solution.py:477
  791.9 73.4 %collective-permute-start.30 = (bf16[4,2,96,512]{3,2,0,1:T(8,128)(2,1)S(1)}, bf16[4,2,96,512]{3,2,0,1:T(8,128)(2,1)}, u32[]{:S(2)}, u32[]{:S(2)}) collective-permute-start(bf16[4,2,96,512]{3,2,0,1:T(8,128)(2,1)S(1)} %fusion.101), channel_id=1, source_target_pairs={{0,2},{2,0},{4,6},{6,4},{8,10},{10,8},{12,14},{14,12},{16,18},{18,... | collective-permute-start | bytes 2359304 | tf_op jit(solution)/shard_map/ppermute | solution.py:514
  794.5 74.6 %collective-permute-start.35 = (bf16[4,2,96,512]{3,2,0,1:T(8,128)(2,1)S(1)}, bf16[4,2,96,512]{3,2,0,1:T(8,128)(2,1)}, u32[]{:S(2)}, u32[]{:S(2)}) collective-permute-start(bf16[4,2,96,512]{3,2,0,1:T(8,128)(2,1)S(1)} %fusion.102), channel_id=1, source_target_pairs={{0,4},{2,6},{4,0},{6,2},{8,12},{10,14},{12,8},{14,10},{16,20},{18,... | collective-permute-start | bytes 2359304 | tf_op jit(solution)/shard_map/ppermute | solution.py:514
  794.8 54.7 %collective-permute-start.26 = (f32[1,96]{1,0:T(1,128)S(1)}, f32[1,96]{1,0:T(1,128)S(1)}, u32[]{:S(2)}, u32[]{:S(2)}) collective-permute-start(f32[1,96]{1,0:T(1,128)S(1)} %get-tuple-element.176), channel_id=1, source_target_pairs={{0,8},{2,10},{4,12},{6,14},{8,16},{10,18},{12,20},{14,22},{16,24},... | collective-permute-start | bytes 1160 | tf_op jit(solution)/shard_map/ppermute | solution.py:487
  799.9 49.6 %collective-permute-start.28 = (f32[1,96]{1,0:T(1,128)S(1)}, f32[1,96]{1,0:T(1,128)S(1)}, u32[]{:S(2)}, u32[]{:S(2)}) collective-permute-start(f32[1,96]{1,0:T(1,128)S(1)} %get-tuple-element.177), channel_id=1, source_target_pairs={{0,24},{2,26},{4,28},{6,30},{8,0},{10,2},{12,4},{14,6},{16,8},{18,... | collective-permute-start | bytes 1160 | tf_op jit(solution)/shard_map/ppermute | solution.py:487
  802.3 63.0 %collective-permute-start.27 = (f32[1,96]{1,0:T(1,128)S(1)}, f32[1,96]{1,0:T(1,128)S(1)}, u32[]{:S(2)}, u32[]{:S(2)}) collective-permute-start(f32[1,96]{1,0:T(1,128)S(1)} %get-tuple-element.178), channel_id=1, source_target_pairs={{0,16},{2,18},{4,20},{6,22},{8,24},{10,26},{12,28},{14,30},{16,0},... | collective-permute-start | bytes 1160 | tf_op jit(solution)/shard_map/ppermute | solution.py:487
  (154 other events, 1791.8 us)
Sparse Core Ops, SparseCore 0:
  65.5 138.4 all-gather.6
  225.3 62.5 all-gather.4
  553.9 60.6 reduce-scatter.2
  744.1 91.8 reduce-scatter.4

commit v3 on v2

--- a/solution.py
+++ b/solution.py
@@ -503,18 +503,23 @@
     return reorder(whole, order, 0).reshape(LINE * PLANE * line.shape[1], line.shape[2])
 
 
-def row_reduce(total, flips, level, place, kind=jnp.bfloat16):
-    block = total.shape[0] // (LINE * PLANE)
-    parts = total.reshape(LINE, 2, 2, block, total.shape[1])
-    for flip in flips:
-        axis = min(3 - flip, parts.ndim - 3)
-        bit = (place // flip) % 2
-        kept = lax.dynamic_index_in_dim(parts, bit, axis, False)
-        away = lax.dynamic_index_in_dim(parts, 1 - bit, axis, False).astype(kind)
-        parts = kept + lax.ppermute(away, "row", plane_pairs(flip)).astype(jnp.float32)
+def row_reduce(halves, level, place):
+    block = halves[0].shape[0] // (LINE * PLANE)
+    halves = [h.reshape(LINE, 2, 2, block, h.shape[1]) for h in halves]
+    for flips in ((1, 2), (2, 1)):
+        for i, flip in enumerate(flips):
+            axis = min(3 - flip, halves[i].ndim - 3)
+            bit = (place // flip) % 2
+            kept = lax.dynamic_index_in_dim(halves[i], bit, axis, False)
+            away = lax.dynamic_index_in_dim(halves[i], 1 - bit, axis, False)
+            away = lax.ppermute(away.astype(jnp.bfloat16), "row", plane_pairs(flip))
+            halves[i] = kept + away.astype(jnp.float32)
     order = [(level + step) % LINE for step in range(LINE)]
-    parts = [lax.dynamic_index_in_dim(parts, i, 0, False) for i in order]
-    moved = [line_shift(parts[step].astype(kind), step) for step in range(1, LINE)]
+    parts = [
+        jnp.concatenate([lax.dynamic_index_in_dim(h, i, 0, False) for h in halves], axis=1)
+        for i in order
+    ]
+    moved = [line_shift(parts[step].astype(jnp.bfloat16), step) for step in range(1, LINE)]
     total = parts[0]
     for part in moved:
         total = total + part.astype(jnp.float32)
@@ -532,13 +537,15 @@
     )
 
 
-def plane_exchange(block, mate):
-    block = reorder(block, [mate ^ m for m in range(2 * PLANE)], 0)
-    out = [block[0]]
-    for move in range(1, 2 * PLANE):
-        pairs = [(d, d ^ move) for d in range(2 * PLANE * LINE)]
-        out.append(lax.ppermute(block[move], GRID, pairs))
-    return reorder(jnp.stack(out), [mate ^ m for m in range(2 * PLANE)], 0)
+def plane_move(block, move):
+    return lax.ppermute(block, "row", plane_pairs(move))
+
+
+def plane_exchange(block):
+    far = swap_cores(block[1])
+    pairs = [jnp.stack([block[0, m], far[m]]) for m in range(PLANE)]
+    moved = {m: plane_move(pairs[m], m) for m in (1, 2, 3)}
+    return [pairs[0], moved[1], moved[2], moved[3]]
 
 
 def plane_all(block):
@@ -546,6 +553,243 @@
     return lax.all_to_all(
         block, GRID, split_axis=0, concat_axis=0, tiled=True, axis_index_groups=groups
     )
+
+
+def expert_body(
+    where_ref,
+    x_ref,
+    cot_ref,
+    weights_ref,
+    router_ref,
+    _,
+    grad_in_ref,
+    mix_ref,
+    grad_expert_ref,
+    act_ref,
+    grad_gate_ref,
+    grad_up_ref,
+    grad_logits_ref,
+):
+    bf16, f32 = jnp.bfloat16, jnp.float32
+    core, expert = where_ref[1], where_ref[2]
+    nt = (((1,), (1,)), ((), ()))
+    width = x_ref.shape[1]
+    x = x_ref[...]
+    half = x.shape[0] // 2
+    there = jnp.concatenate([cot_ref[0, core], cot_ref[0, 1 - core]], axis=0)
+    mask = there[:, width:].astype(f32) > 0
+    upstream = there[:, :width].astype(f32)
+    router = router_ref[...]
+    logits = jnp.dot(x, router, preferred_element_type=f32)
+    top = jnp.max(jnp.where(mask, logits, MASKED), axis=-1, keepdims=True)
+    exponent = jnp.where(mask, jnp.exp(logits - top), 0.0)
+    gates = exponent / jnp.maximum(jnp.sum(exponent, axis=-1, keepdims=True), 1e-30)
+    mine = lax.broadcasted_iota(jnp.int32, gates.shape, 1) == expert
+    slot_gate = jnp.sum(jnp.where(mine, gates, 0.0), axis=-1, keepdims=True)
+    grad_expert = (upstream * slot_gate).astype(bf16)
+    grad_expert_ref[...] = grad_expert
+    cols = weights_ref.shape[3] // 3
+    parts, out = [], None
+    for side in range(2):
+        gate_w = weights_ref[:, side, :, :cols].reshape(width, cols)
+        up_w = weights_ref[:, side, :, cols : 2 * cols].reshape(width, cols)
+        down_t = weights_ref[:, side, :, 2 * cols :].reshape(width, cols)
+        gate_value = jnp.dot(x, gate_w, preferred_element_type=f32)
+        up_value = jnp.dot(x, up_w, preferred_element_type=f32)
+        sigmoid = 1.0 / (1.0 + jnp.exp(-gate_value))
+        silu = gate_value * sigmoid
+        act = (silu * up_value).astype(bf16)
+        part = lax.dot_general(act, down_t, nt, preferred_element_type=f32)
+        out = part if out is None else out + part
+        grad_act = jnp.dot(grad_expert, down_t, preferred_element_type=f32)
+        slope = sigmoid * (1.0 + gate_value * (1.0 - sigmoid))
+        grad_gate = (grad_act * up_value * slope).astype(bf16)
+        grad_up = (grad_act * silu).astype(bf16)
+        act_ref[:, side * cols : (side + 1) * cols] = act
+        grad_gate_ref[:, side * cols : (side + 1) * cols] = grad_gate
+        grad_up_ref[:, side * cols : (side + 1) * cols] = grad_up
+        parts.append((grad_gate, grad_up, gate_w, up_w))
+    scaled = (out * slot_gate).astype(bf16)
+    mix_ref[0, core] = scaled[:half]
+    mix_ref[0, 1 - core] = scaled[half:]
+    pick_grad = slot_gate * jnp.sum(out * upstream, axis=-1, keepdims=True)
+    grad_logits = (pick_grad * (jnp.where(mine, 1.0, 0.0) - gates)).astype(bf16)
+    grad_logits_ref[...] = grad_logits
+    grad_in = lax.dot_general(grad_logits, router, nt, preferred_element_type=f32)
+    for grad_gate, grad_up, gate_w, up_w in parts:
+        grad_in += lax.dot_general(grad_gate, gate_w, nt, preferred_element_type=f32)
+        grad_in += lax.dot_general(grad_up, up_w, nt, preferred_element_type=f32)
+    grad_in_ref[...] = grad_in.astype(bf16)
+
+
+def expert_rows(move, place, core, expert, x, cot, weights, router, mixture):
+    slots, width = x.shape
+    cols = weights.shape[3] // 3
+    where = jnp.stack([place, core, expert]).astype(jnp.int32)
+
+    def whole(shape):
+        return pl.BlockSpec(shape, lambda i, w: (0,) * len(shape))
+
+    outs = [width, width, width, 2 * cols, 2 * cols, 2 * cols, router.shape[1]]
+    out_specs = [whole((slots, n)) for n in outs]
+    out_shape = [jax.ShapeDtypeStruct((slots, n), jnp.bfloat16) for n in outs]
+    mix_block = (1, 2, slots // 2, width)
+    out_specs[1] = pl.BlockSpec(mix_block, lambda i, w: (w[0] ^ move, 0, 0, 0))
+    out_shape[1] = jax.ShapeDtypeStruct((PLANE, *mix_block[1:]), jnp.bfloat16)
+    resident = pl.BlockSpec(memory_space=pltpu.VMEM)
+    first = mixture is None
+    cot_spec = pl.BlockSpec((1, *cot.shape[1:]), lambda i, w: (w[0] ^ move, 0, 0, 0))
+    anywhere = pl.BlockSpec(memory_space=pl.ANY)
+    return pl.pallas_call(
+        expert_body,
+        grid_spec=pltpu.PrefetchScalarGridSpec(
+            num_scalar_prefetch=1,
+            grid=(1,),
+            in_specs=[whole(x.shape), cot_spec, resident, resident, anywhere],
+            out_specs=out_specs,
+        ),
+        out_shape=out_shape,
+        input_output_aliases={} if first else {5: 1},
+        compiler_params=pltpu.CompilerParams(vmem_limit_bytes=40 << 20),
+        cost_estimate=pl.CostEstimate(
+            flops=24 * slots * width * cols,
+            bytes_accessed=2 * (5 * slots * width + 6 * slots * cols),
+            transcendentals=slots * 2 * cols,
+        ),
+        name="expert_rows",
+    )(where, x, cot, weights, router, x if first else mixture)
+
+
+def picked(slots, share):
+    ids = lax.broadcasted_iota(jnp.int32, (share, slots.shape[1]), 0)
+    rows = [(slots[e : e + 1] == ids).astype(jnp.bfloat16) for e in range(slots.shape[0])]
+    return jnp.concatenate(rows, axis=0)
+
+
+def select_body(slots_ref, own_ref, other_ref, *rest):
+    out_ref = rest[-1]
+    share = out_ref.shape[3]
+    pick = picked(slots_ref[0], share)
+    half, width = own_ref.shape[1], own_ref.shape[2]
+    rows = jnp.dot(pick[:, :half], own_ref[0], preferred_element_type=jnp.float32)
+    rows += jnp.dot(pick[:, half:], other_ref[0], preferred_element_type=jnp.float32)
+    out_ref[:, :, 0, :, :width] = rows.astype(jnp.bfloat16).reshape(2, PLANE, share, width)
+    if len(rest) == 2:
+        extra = jnp.dot(pick, rest[0][0], preferred_element_type=jnp.float32)
+        extra = extra.astype(jnp.bfloat16)
+        out_ref[:, :, 0, :, width:] = extra.reshape(2, PLANE, share, extra.shape[1])
+
+
+def select_rows(slots, own, other, share, extra=None):
+    lines, mates, span = slots.shape
+    half, width = own.shape[1:]
+    wide = width + (0 if extra is None else extra.shape[2])
+    parts = [slots, own, other] + ([] if extra is None else [extra])
+
+    def block(shape):
+        return pl.BlockSpec((1, *shape), lambda i: (i, 0, 0))
+
+    specs = [block((mates, span)), block((half, width)), block((half, width))]
+    if extra is not None:
+        specs.append(block((span, extra.shape[2])))
+    return pl.pallas_call(
+        select_body,
+        grid=(lines,),
+        in_specs=specs,
+        out_specs=pl.BlockSpec((2, PLANE, 1, share, wide), lambda i: (0, 0, i, 0, 0)),
+        out_shape=jax.ShapeDtypeStruct((2, PLANE, lines, share, wide), jnp.bfloat16),
+        compiler_params=pltpu.CompilerParams(vmem_limit_bytes=40 << 20),
+        cost_estimate=pl.CostEstimate(
+            flops=2 * lines * mates * share * span * wide,
+            bytes_accessed=2 * lines * (span + mates * share) * wide,
+            transcendentals=0,
+        ),
+        name="select_rows",
+    )(*parts)
+
+
+def combine_body(slots_ref, near_ref, far_ref, kept_ref, away_ref):
+    chips, _, share, width = near_ref.shape
+    half = kept_ref.shape[1]
+    pick = picked(slots_ref[0], share).T
+    near = near_ref[:, 0].reshape(chips * share, width)
+    far = far_ref[:, 0].reshape(chips * share, width)
+    total = jnp.dot(pick, jnp.concatenate([near, far]), preferred_element_type=jnp.float32)
+    kept_ref[0] = total[:half].astype(kept_ref.dtype)
+    away_ref[0] = total[half:].astype(away_ref.dtype)
+
+
+def combine_rows(slots, near, far, far_block=0):
+    lines, mates, span = slots.shape
+    chips = mates // 2
+    share, width = near.shape[2:]
+    part = pl.BlockSpec((1, span // 2, width), lambda i: (i, 0, 0))
+    shape = (lines, span // 2, width)
+    return pl.pallas_call(
+        combine_body,
+        grid=(lines,),
+        in_specs=[
+            pl.BlockSpec((1, mates, span), lambda i: (i, 0, 0)),
+            pl.BlockSpec((chips, 1, share, width), lambda i: (0, i, 0, 0)),
+            pl.BlockSpec((chips, 1, share, width), lambda i: (far_block, i, 0, 0)),
+        ],
+        out_specs=[part, part],
+        out_shape=[
+            jax.ShapeDtypeStruct(shape, jnp.float32),
+            jax.ShapeDtypeStruct(shape, jnp.bfloat16),
+        ],
+        compiler_params=pltpu.CompilerParams(vmem_limit_bytes=40 << 20),
+        cost_estimate=pl.CostEstimate(
+            flops=2 * lines * mates * share * span * width,
+            bytes_accessed=2 * lines * (2 * span + mates * share) * width,
+            transcendentals=0,
+        ),
+        name="combine_rows",
+    )(slots, near, far)
+
+
+def shard_body(pieces, left_refs, right_refs, out_ref):
+    count, _, block, _ = out_ref.shape
+    lefts = [ref[...].T for ref in left_refs]
+    for i in range(len(right_refs) // pieces):
+        rights = right_refs[i * pieces : (i + 1) * pieces]
+        full = None
+        for left, right in zip(lefts, rights):
+            part = jnp.dot(left, right[...], preferred_element_type=jnp.float32)
+            full = part if full is None else full + part
+        full = full.astype(jnp.bfloat16)
+        cols = full.shape[1] // 2
+        for core in range(2):
+            part = full[:, core * cols : (core + 1) * cols]
+            out_ref[:, core, :, i * cols : (i + 1) * cols] = part.reshape(count, block, cols)
+
+
+def shard_grad(lefts, rights, rows, count=4):
+    pieces = len(lefts)
+    slots, width = lefts[0].shape
+    cols = rights[0].shape[1] // 2
+    block = width // rows
+    wide = cols * (len(rights) // pieces)
+
+    def body(*refs):
+        shard_body(pieces, refs[:pieces], refs[pieces:-1], refs[-1])
+
+    out = pl.pallas_call(
+        body,
+        grid=(rows // count,),
+        in_specs=[pl.BlockSpec((slots, count * block), lambda i: (0, i)) for _ in lefts]
+        + [pl.BlockSpec((slots, 2 * cols), lambda i: (0, 0)) for _ in rights],
+        out_specs=pl.BlockSpec((count, 2, block, wide), lambda i: (i, 0, 0, 0)),
+        out_shape=jax.ShapeDtypeStruct((rows, 2, block, wide), jnp.bfloat16),
+        compiler_params=pltpu.CompilerParams(vmem_limit_bytes=48 << 20),
+        cost_estimate=pl.CostEstimate(
+            flops=4 * pieces * slots * width * wide,
+            bytes_accessed=2 * (pieces * slots * (width + 2 * wide) + 2 * width * wide),
+            transcendentals=0,
+        ),
+        name="shard_grad",
+    )(*lefts, *rights)
+    return out.reshape(2 * rows, block, wide)
 
 
 def tokens_move(
@@ -580,6 +824,7 @@
     heads = head_cols // HEAD_SIZE
     mates = 2 * PLANE
     my_expert = row * 2 + core
+    relative = [(place * 2 + core) ^ (2 * m + k) for k in range(2) for m in range(PLANE)]
     nt = (((1,), (1,)), ((), ()))
     tn = (((0,), (0,)), ((), ()))
 
@@ -597,9 +842,9 @@
         axis=1,
     )
     packed_line = jnp.stack([packed] + [line_shift(packed, step) for step in range(1, LINE)])
-    routes_line = [routes.T] + [line_shift(routes.T, step) for step in range(1, LINE)]
+    routes_own = after(routes.T, packed)
+    routes_line = [routes_own] + [line_shift(routes_own, step) for step in range(1, LINE)]
     routes_line = reorder(jnp.stack(routes_line), [(level - z) % LINE for z in range(LINE)], 0)
-    packed_line = after(packed_line, routes_line)
     packed_full = row_gather(packed_line, level, place)
     o0 = head_cols + 2 * kv_cols
     qkv_cols, out_full = packed_full[:, :o0], packed_full[:, o0:]
@@ -609,34 +854,24 @@
     gain_second = out_full[:, head_cols + E + 1].astype(f32)
 
     expert_ids = jnp.arange(E, dtype=jnp.int32)
-    share_slots = core * share + jnp.arange(share, dtype=jnp.int32)
-    picks, masks = [], []
+    slot_near, slot_there, masks = [], [], []
     for i in range(LINE):
         named, counts = slot_ranks(routes_line[i].T)
-        slot_of = jnp.where(named, counts, -1).T
+        slot_of = jnp.where(named, counts - core * share, -1).T
         slot_of = lax.dynamic_slice_in_dim(own_first(slot_of, core, 1), level * mates, mates)
-        pick = (slot_of[:, None, :] == share_slots[None, :, None]).astype(bf16)
-        picks.append(pick.reshape(mates * share, span))
+        slot_there.append(slot_of)
+        slot_near.append(reorder(slot_of, relative, 0))
         masks.append(own_first(jnp.pad(named.astype(bf16), ((0, 0), (0, 128 - E))), core, 0))
-
-    def send_rows(tables, chunks):
-        sent = []
-        for pick, chunk in zip(tables, chunks):
-            part = jnp.dot(pick, chunk, preferred_element_type=f32).astype(bf16)
-            sent.append(part.reshape(mates, 1, share, chunk.shape[1]))
-        return jnp.concatenate(sent, axis=1)
+    slot_near, slot_there, mask_line = [jnp.stack(t) for t in (slot_near, slot_there, masks)]
 
     slots = LINE * share * mates
 
-    gate_up = exchange(after(jnp.concatenate([gate_weight, up_weight], axis=2), packed_line))
+    nil = packed_line[0, 0, 0] * 0
+    weights = jnp.concatenate(
+        [gate_weight, up_weight, down_weight.transpose(0, 2, 1) + nil], axis=2
+    )
+    weights = exchange(after(weights, routes_line))
     cot_line = line_gather(after(cotangent, packed_line))
-
-    def whole_weight(blocks):
-        return (
-            blocks.reshape(rows, 2, row_block, hidden_block)
-            .transpose(0, 2, 1, 3)
-            .reshape(MODEL_WIDTH, ffe)
-        )
 
     hidden_all = both_cores(hidden_in)
     tokens_all = hidden_all.astype(f32)
@@ -665,81 +900,56 @@
     unit_second = hidden_mid * scale_second
     normed_second = (unit_second * gain_second).astype(bf16)
 
-    normed_line = line_gather(after(normed_second, gate_up))
     cot_line = after(cot_line, normed_second)
     cot_swap = swap_cores(cot_line)
-    cot_rows = [
-        jnp.concatenate([jnp.concatenate([cot_line[i], cot_swap[i]], axis=0), masks[i]], axis=1)
-        for i in range(LINE)
+    cot_rows = select_rows(slot_there, cot_line, cot_swap, share, mask_line)
+    normed_line = line_gather(after(normed_second, weights, cot_rows))
+    cot_rows = plane_all(cot_rows.reshape(mates, LINE, share, MODEL_WIDTH + 128))
+    normed_swap = swap_cores(normed_line)
+    normed_rows = select_rows(slot_near, after(normed_line, cot_rows), normed_swap, share)
+    pieces = plane_exchange(normed_rows)
+
+    pieces = [p.reshape(2 * LINE * share, MODEL_WIDTH) for p in pieces]
+    cot_rows = cot_rows.reshape(PLANE, 2, LINE * share, MODEL_WIDTH + 128)
+    weights = weights.reshape(rows, 2, row_block, 3 * hidden_block)
+    done, mixture, back = [], None, []
+    for move in range(PLANE):
+        if move == 3:
+            pieces[3] = after(pieces[3], back[1])
+        found = expert_rows(
+            move, place, core, my_expert, pieces[move], cot_rows, weights, out_full[:, head_cols:], mixture
+        )
+        mixture = found[1]
+        done.append(found)
+        back.append(plane_move(found[0], move) if move else found[0])
+    _, _, grad_expert, activation, grad_gate, grad_up, grad_logits = [
+        list(a) for a in zip(*done)
     ]
-    upstream_rows = plane_all(send_rows(picks, cot_rows))
-    upstream = upstream_rows.reshape(slots, MODEL_WIDTH + 128)
-    mask_rows = upstream[:, MODEL_WIDTH : MODEL_WIDTH + E] > 0
-    upstream = upstream[:, :MODEL_WIDTH].astype(f32)
-
-    normed_swap = swap_cores(normed_line)
-    expert_in = plane_exchange(
-        send_rows(
-            picks,
-            [jnp.concatenate([normed_line[i], normed_swap[i]], axis=0) for i in range(LINE)],
-        ),
-        place * 2 + core,
-    ).reshape(slots, MODEL_WIDTH)
-    down_e = exchange(after(down_weight.transpose(0, 2, 1), upstream_rows))
-
-    logits = jnp.dot(expert_in, router_full, preferred_element_type=f32)
-    top = jnp.max(jnp.where(mask_rows, logits, MASKED), axis=-1, keepdims=True)
-    exponent = jnp.where(mask_rows, jnp.exp(logits - top), 0.0)
-    gates = exponent / jnp.maximum(jnp.sum(exponent, axis=-1, keepdims=True), 1e-30)
-    mine = (expert_ids == my_expert)[None, :]
-    slot_gate = jnp.sum(jnp.where(mine, gates, 0.0), axis=-1, keepdims=True)
-    gate_w = whole_weight(gate_up[:, :, :hidden_block])
-    up_w = whole_weight(gate_up[:, :, hidden_block:])
-    down_t = whole_weight(down_e)
-    gate_value = jnp.dot(expert_in, gate_w, preferred_element_type=f32)
-    up_value = jnp.dot(expert_in, up_w, preferred_element_type=f32)
-    sigmoid_gate = jax.nn.sigmoid(gate_value)
-    silu_gate = gate_value * sigmoid_gate
-    activation = (silu_gate * up_value).astype(bf16)
-    expert_out = lax.dot_general(activation, down_t, nt, preferred_element_type=f32)
-    slot_grad = jnp.sum(expert_out * upstream, axis=-1, keepdims=True)
-    pick_grad = slot_gate * slot_grad
-    grad_logits = (pick_grad * (jnp.where(mine, 1.0, 0.0) - gates)).astype(bf16)
-    grad_expert = (upstream * slot_gate).astype(bf16)
-    grad_act = jnp.dot(grad_expert, down_t, preferred_element_type=f32)
-    slope = sigmoid_gate * (1.0 + gate_value * (1.0 - sigmoid_gate))
-    grad_gate = (grad_act * up_value * slope).astype(bf16)
-    grad_up = (grad_act * silu_gate).astype(bf16)
-    grad_in = lax.dot_general(grad_gate, gate_w, nt, preferred_element_type=f32)
-    grad_in = grad_in + lax.dot_general(grad_up, up_w, nt, preferred_element_type=f32)
-    grad_in = grad_in + lax.dot_general(grad_logits, router_full, nt, preferred_element_type=f32)
-
-    def combine(got):
-        parts = []
-        for i, pick in enumerate(picks):
-            part = got[:, i].reshape(mates * share, MODEL_WIDTH)
-            parts.append(lax.dot_general(pick, part, tn, preferred_element_type=f32))
-        parts = jnp.stack(parts)
-        away = swap_cores(parts[:, local:].astype(bf16))
-        parts = parts[:, :local] + away.astype(f32)
-        return line_reduce(parts.astype(bf16)).astype(f32)
-
-    shape = (mates, LINE, share, MODEL_WIDTH)
-    grad_back = plane_all(grad_in.astype(bf16).reshape(shape))
-    grad_normed = combine(grad_back)
-    router_grad = lax.dot_general(expert_in, grad_logits, tn, preferred_element_type=f32)
-
-    def shard_grad(left, right):
-        full = lax.dot_general(left, right, tn, preferred_element_type=f32).astype(bf16)
-        blocks = full.reshape(rows, row_block, 2, hidden_block).transpose(0, 2, 1, 3)
-        return blocks.reshape(E, row_block, hidden_block)
-
-    mixture = (expert_out * slot_gate).astype(bf16).reshape(shape)
-    mixture = plane_all(after(mixture, grad_back))
-    down_home = exchange(after(shard_grad(grad_expert, activation), mixture))
-    gate_home = exchange(after(shard_grad(expert_in, grad_gate), down_home))
-    up_home = exchange(after(shard_grad(expert_in, grad_up), gate_home))
-
+
+    def combine(table, near, far, far_block=0):
+        kept, away = combine_rows(table, near, far, far_block)
+        return (kept + swap_cores(away).astype(f32)).astype(bf16)
+
+    shape = (2, LINE, share, MODEL_WIDTH)
+    back = [b.reshape(shape) for b in back]
+    grad_expert[3] = after(grad_expert[3], back[2])
+    down_home = exchange(after(shard_grad(grad_expert, activation, rows), back[3]))
+    far = swap_cores(after(jnp.stack([b[1] for b in back]), down_home))
+    grad_parts = combine(slot_near, jnp.stack([b[0] for b in back]), far)
+    grad_normed = line_reduce(grad_parts).astype(f32)
+    router_grad = sum(
+        lax.dot_general(g, p, tn, preferred_element_type=f32) for g, p in zip(grad_logits, pieces)
+    )
+    router_grad = router_grad[:E].T
+    mixture = mixture.reshape(mates, LINE, share, MODEL_WIDTH)
+    mixture = plane_all(after(mixture, down_home))
+    mixture_there = after(mixture, grad_parts)
+    mixture_parts = combine(slot_there, mixture_there, mixture_there, 1)
+    mixture_own = line_reduce(mixture_parts).astype(f32)
+    gate_up_home = shard_grad(pieces, grad_gate + grad_up, rows)
+    gate_up_home = exchange(after(gate_up_home, mixture))
+
+    grad_normed = after(grad_normed, mixture_parts)
     tilted = grad_normed * gain_second
     gain_second_grad = jnp.sum(grad_normed * unit_second, axis=0)
     grad_hidden = cotangent.astype(f32) + scale_second * (
@@ -762,15 +972,15 @@
     grad_qkv = jnp.concatenate([grad_query_low, grad_key_low, grad_values.astype(bf16)], axis=1)
     qkv_grad = lax.dot_general(normed_all, grad_qkv, tn, preferred_element_type=f32)
     first_part = lax.dot_general(grad_qkv, qkv_cols, nt, preferred_element_type=f32)
+    unit_all = tokens_all * scale_all
+    gain_first_grad = jnp.sum(first_part * unit_all, axis=0)
     grad_first = sum_cores(first_part, f32)
     unit_first = tokens_in * scale_all[:local]
     tilted_first = grad_first * gain_first
-    gain_first_grad = jnp.sum(grad_first * unit_first, axis=0)
     input_grad = grad_hidden + scale_all[:local] * (
         tilted_first - unit_first * jnp.mean(tilted_first * unit_first, axis=-1, keepdims=True)
     )
-    mixture = combine(after(mixture, grad_qkv))
-    block_out = (hidden_mid + mixture).astype(bf16)
+    block_out = (hidden_mid + mixture_own).astype(bf16)
 
     extra = jnp.concatenate(
         [
@@ -780,40 +990,33 @@
         ],
         axis=1,
     )
-    half = head_cols // 2
-    output_own = [
-        row_reduce(output_t_grad[:, :half], (1, 2), level, place),
-        row_reduce(
-            jnp.concatenate([output_t_grad[:, half:], extra], axis=1), (2, 1), level, place
-        ),
-    ]
-    output_own = jnp.concatenate(output_own, axis=1)
-    small_own = output_own[:, head_cols:]
+    down_home = after(down_home, grad_qkv)
+    pad = jnp.zeros((MODEL_WIDTH, 127), f32)
+    owned = row_reduce(
+        [
+            jnp.concatenate([output_t_grad, extra], axis=1),
+            jnp.concatenate([qkv_grad, gain_first_grad[:, None], pad], axis=1),
+        ],
+        level,
+        place,
+    )
+    output_own, owned = owned[:, :head_cols], owned[:, head_cols:]
+    small_own, qkv_own = owned[:, :128], owned[:, 128 : 128 + o0]
+    small_own = jnp.concatenate([small_own[:, : E + 1], owned[:, 128 + o0 : 129 + o0]], axis=1)
     small_own = small_own + swap_cores(small_own)
-    qkv_grad = after(qkv_grad, gate_home)
-    half = qkv_grad.shape[1] // 2
-    qkv_own = jnp.concatenate(
-        [
-            row_reduce(qkv_grad[:, :half], (1, 2), level, place),
-            row_reduce(qkv_grad[:, half:], (2, 1), level, place),
-        ],
-        axis=1,
-    )
-    gain_parts = gain_first_grad.reshape(rows, row_block)
-    gain_first_own = row_reduce(gain_parts, (1, 2), level, place, f32)[0]
-    gain_first_own = gain_first_own + swap_cores(gain_first_own)
+    gate_up_home = after(gate_up_home, small_own)
     return (
         block_out,
         input_grad,
-        gain_first_own,
+        small_own[:, E + 1],
         qkv_own[:, :head_cols],
         qkv_own[:, head_cols : head_cols + kv_cols],
         qkv_own[:, head_cols + kv_cols :],
         output_own[:, :head_cols].T,
         small_own[:, E],
         small_own[:, :E],
-        gate_home.astype(f32),
-        up_home.astype(f32),
+        gate_up_home[:, :, :hidden_block].astype(f32),
+        gate_up_home[:, :, hidden_block:].astype(f32),
         down_home.astype(f32).transpose(0, 2, 1),
     )
 

time: 926 us -> 860 us (0.929)
  Pallas kernels: 0.01 us -> 95.4 us
  waiting for transfers between devices: 472 us -> 388 us
  matrix products: 124 us -> 42.5 us
  local copies, waits for them, and re-layouts: 122 us -> 153 us
  starting transfers between devices: 93.6 us -> 65.8 us
    pallas_call x0 -> x10, Pallas kernels: none -> 95.4 us  [the longest x4 54.9 us: expert_rows(): pl.pallas_call(expert_body, grid_spec=pltpu.PrefetchScalarGridSpec(num_sc...]
    ppermute x21 -> x9, waiting for transfers between devices: 124 us -> 28.4 us  [line_shift(): return lax.ppermute(block, 'row', pairs)]
    dot_general x28 -> x4, matrix products: 84.4 us -> 3.4 us  [tokens_move(): lax.dot_general(g, p, tn, preferred_element_type=f32)]
    all_to_all x3 -> x2, waiting for transfers between devices: 95.3 us -> 29.3 us  [plane_all(): lax.all_to_all(block, GRID, split_axis=0, concat_axis=0, tiled=True, axis...]
    unnamed x285 -> x305, local copies, waits for them, and re-layouts: 44 us -> 90.3 us
    ppermute x17 -> x10, waiting for transfers between devices: 58 us -> 85.3 us  [the longest x4 57.1 us: row_reduce(): away = lax.ppermute(away.astype(jnp.bfloat16), 'row', plane_pairs(flip))]
    ppermute x3, waiting for transfers between devices: 75.6 us -> 102 us  [row_gather(): lax.ppermute(line, 'row', plane_pairs(flip))]
    reshape x9 -> x0, local copies, waits for them, and re-layouts: 25.8 us -> none  [the longest x6 19.2 us: shard_grad(): full.reshape(rows, row_block, 2, hidden_block).transpose(0, 2, 1, 3)]
  transfers between devices with their start and end apart: 63 -> 42, of which waited for: 28 -> 26; matrix products, arithmetic and copies ran while one was open for 27% -> 23% of each run, Pallas kernels for 0% -> 10%
where the time goes in v3:
time: 860 us; the launch traced here: 844 us
  waiting for transfers between devices  388 us (45%)
  local copies, waits for them, and re-layouts  153 us (18%)
  Pallas kernels  95.4 us (11%)
  other arithmetic  82.7 us (10%)
  starting transfers between devices  65.8 us (8%)
  matrix products  42.5 us (5%)
  between operations  16.8 us (2%)
    ppermute x3, waiting for transfers between devices, row_gather(): lax.ppermute(line, 'row', plane_pairs(flip))  102 us
    unnamed x305, local copies, waits for them, and re-layouts  90.3 us
    all_to_all x3, waiting for transfers between devices, exchange(): return lax.all_to_all(block, GRID, split_axis=0, concat_axis=0, tiled=True)  67.7 us
    all_gather x2, waiting for transfers between devices, line_gather(): lax.all_gather(block, 'row', axis=0, tiled=False, axis_index_groups=LINES)  57.3 us
    ppermute x4, waiting for transfers between devices, row_reduce(): away = lax.ppermute(away.astype(jnp.bfloat16), 'row', plane_pairs(flip))  57.1 us
    pallas_call x4, Pallas kernels, expert_rows(): pl.pallas_call(expert_body, grid_spec=pltpu.PrefetchScalarGridSpec(num_sc...  54.9 us
    all_to_all x2, waiting for transfers between devices, plane_all(): lax.all_to_all(block, GRID, split_axis=0, concat_axis=0, tiled=True, axis...  29.3 us
    ppermute x9, waiting for transfers between devices, line_shift(): return lax.ppermute(block, 'row', pairs)  28.4 us
  transfers between devices with their start and end apart: 42, of which 26 were waited for; matrix products, arithmetic and copies ran while one was open for 23% of the time, Pallas kernels for 10%

profile of v3, /device:TPU:0, one launch (start us, length us, event | category | flops | bytes accessed | tf_op | source)
XLA Modules:
  0.0 844.4 jit_solution(4873354536892329293)
XLA Ops:
  42.1 5.3 collective-permute-done.2
  47.4 9.3 %collective-permute-done.3 = bf16[96,1920]{1,0:T(8,128)(2,1)S(1)} collective-permute-done((bf16[96,1920]{1,0:T(8,128)(2,1)S(1)}, bf16[96,1920]{1,0:T(8,128)(2,1)S(1)}, u32[]{:S(2)}, u32[]{:S(2)}) %collective-permute-start.3) | collective-permute-done | bytes 368672 | tf_op jit(solution)/shard_map/ppermute | solution.py:487
  67.8 58.5 %collective-permute-done.4 = bf16[4,96,1920]{2,1,0:T(8,128)(2,1)} collective-permute-done((bf16[4,96,1920]{2,1,0:T(8,128)(2,1)S(1)}, bf16[4,96,1920]{2,1,0:T(8,128)(2,1)}, u32[]{:S(2)}, u32[]{:S(2)}) %collective-permute-start.4) | collective-permute-done | bytes 1474592 | tf_op jit(solution)/shard_map/ppermute | solution.py:500
  131.7 43.2 %collective-permute-done.6 = bf16[4,96,1920]{2,1,0:T(8,128)(2,1)} collective-permute-done((bf16[4,96,1920]{2,1,0:T(8,128)(2,1)S(1)}, bf16[4,96,1920]{2,1,0:T(8,128)(2,1)}, u32[]{:S(2)}, u32[]{:S(2)}) %collective-permute-start.6) | collective-permute-done | bytes 1474592 | tf_op jit(solution)/shard_map/ppermute | solution.py:500
  239.0 17.9 %all-to-all-done.refs_1_ = bf16[32,96,1152]{2,1,0:T(8,128)(2,1)} async-done(((bf16[32,96,1152]{2,1,0:T(8,128)(2,1)}), bf16[32,96,1152]{2,1,0:T(8,128)(2,1)}, u32[]{:S(2)}, u32[]{:S(2)}) %all-to-all-start) | async-done | bytes 7077920 | tf_op jit(solution)/shard_map/all_to_all | solution.py:477
  261.6 57.3 %all-gather.7.cloned.1.call-done = bf16[1024,1536]{1,0:T(8,128)(2,1)} async-done(((bf16[256,1536]{1,0:T(8,128)(2,1)}), bf16[1024,1536]{1,0:T(8,128)(2,1)}) %all-gather.7.cloned.1.call-update) | async-done | bytes 3145744 | tf_op jit(solution)/shard_map/all_gather | solution.py:530
  343.1 13.2 %expert_rows.4 = (bf16[384,1536]{1,0:T(8,128)(2,1)S(1)}, bf16[4,2,192,1536]{3,2,1,0:T(8,128)(2,1)S(1)}, bf16[384,1536]{1,0:T(8,128)(2,1)S(1)}, bf16[384,768]{1,0...) custom-call(s32[3]{0:T(128)S(1)} %pad_add_fusion.6.where_ref, ...), custom_call_target="tpu_custom_call" | custom-call | flops 5435817984 | bytes 7667712 | tf_op jit(solution)/shard_map/expert_rows/pallas_call | solution.py:643
  358.1 9.8 %collective-permute-done.15 = bf16[2,4,48,1536]{3,2,1,0:T(8,128)(2,1)S(1)} collective-permute-done((bf16[2,4,48,1536]{3,2,1,0:T(8,128)(2,1)S(1)}, bf16[2,4,48,1536]{3,2,1,0:T(8,128)(2,1)S(1)}, u32[]{:S(2)}, u32[]{:S(2)}) %collective-permute-start.15) | collective-permute-done | bytes 1179680 | tf_op jit(solution)/shard_map/ppermute | solution.py:541
  367.9 13.6 %expert_rows.5 = (bf16[384,1536]{1,0:T(8,128)(2,1)S(1)}, bf16[4,2,192,1536]{3,2,1,0:T(8,128)(2,1)S(1)}, bf16[384,1536]{1,0:T(8,128)(2,1)S(1)}, bf16[384,768]{1,0...) custom-call(s32[3]{0:T(128)S(1)} %pad_add_fusion.6.where_ref, ...), custom_call_target="tpu_custom_call", output_to_operand_aliasing={{1}: (5, {})} | custom-call | flops 5435817984 | bytes 7667712 | tf_op jit(solution)/shard_map/expert_rows/pallas_call | solution.py:643
  386.6 6.8 collective-permute-done.17
  393.4 14.4 %expert_rows.6 = (bf16[384,1536]{1,0:T(8,128)(2,1)}, bf16[4,2,192,1536]{3,2,1,0:T(8,128)(2,1)S(1)}, bf16[384,1536]{1,0:T(8,128)(2,1)S(1)}, bf16[384,768]{1,0:T(8...) custom-call(s32[3]{0:T(128)S(1)} %pad_add_fusion.6.where_ref, ...), custom_call_target="tpu_custom_call", output_to_operand_aliasing={{1}: (5, {})} | custom-call | flops 5435817984 | bytes 7667712 | tf_op jit(solution)/shard_map/expert_rows/pallas_call | solution.py:643
  423.3 13.6 %expert_rows.7 = (bf16[384,1536]{1,0:T(8,128)(2,1)S(1)}, bf16[4,2,192,1536]{3,2,1,0:T(8,128)(2,1)S(1)}, bf16[384,1536]{1,0:T(8,128)(2,1)S(1)}, bf16[384,768]{1,0...) custom-call(s32[3]{0:T(128)S(1)} %pad_add_fusion.6.where_ref, ...), custom_call_target="tpu_custom_call", output_to_operand_aliasing={{1}: (5, {})} | custom-call | flops 5435817984 | bytes 7667712 | tf_op jit(solution)/shard_map/expert_rows/pallas_call | solution.py:643
  453.8 7.8 shard_grad.2
  461.6 10.0 %collective-permute-done.19 = bf16[384,1536]{1,0:T(8,128)(2,1)} collective-permute-done((bf16[384,1536]{1,0:T(8,128)(2,1)S(1)}, bf16[384,1536]{1,0:T(8,128)(2,1)}, u32[]{:S(2)}, u32[]{:S(2)}) %collective-permute-start.19) | collective-permute-done | bytes 1179680 | tf_op jit(solution)/shard_map/ppermute | solution.py:541
  479.9 49.8 %all-to-all-done.2.refs_1_.refs_0_ = bf16[32,96,384]{2,1,0:T(8,128)(2,1)} async-done(((bf16[32,96,384]{2,1,0:T(8,128)(2,1)}), bf16[32,96,384]{2,1,0:T(8,128)(2,1)}, u32[]{:S(2)}, u32[]{:S(2)}) %all-to-all-start.2) | async-done | bytes 2359328 | tf_op jit(solution)/shard_map/all_to_all | solution.py:477
  534.5 5.3 combine_rows.2
  548.5 6.4 add_convert_fusion.1.refs_1_
  560.9 13.1 %shard_grad.3 = bf16[16,2,96,768]{3,2,1,0:T(8,128)(2,1)} custom-call(bf16[384,1536]{1,0:T(8,128)(2,1)S(1)} %bitcast.237, bf16[384,1536]{1,0:T(8,128)(2,1)} %bitcast.243, bf16[384,1536]{1,0:T(8,128)(2,1)} %bitcast.240, bf16[384,1536]{1,0:T(8,128)(2,1)} %after.22.x_ref.refs_3_, bf16[384,768]{1,0:T(8,128)(2,1)S(1)} %copy-done.58, ...), custom_call_target="tpu_custom_call" | custom-call | flops 7247757312 | bytes 14155776 | tf_op jit(solution)/shard_map/shard_grad/pallas_call | solution.py:777
  574.0 28.0 %all-to-all-done.3.refs_0_.refs_1_ = bf16[8,4,48,1536]{3,2,1,0:T(8,128)(2,1)} async-done(((bf16[8,4,48,1536]{3,2,1,0:T(8,128)(2,1)}), bf16[8,4,48,1536]{3,2,1,0:T(8,128)(2,1)}, u32[]{:S(2)}, u32[]{:S(2)}) %all-to-all-start.3) | async-done | bytes 4718624 | tf_op jit(solution)/shard_map/all_to_all | solution.py:553
  602.8 6.9 combine_rows.3
  618.3 6.3 add_convert_fusion.refs_1_
  649.4 6.2 multiply_reduce_fusion
  692.6 4.7 fusion.5
  699.5 8.4 concatenate.165
  725.5 8.1 collective-permute-start.26
  733.5 31.3 %collective-permute-done.27 = bf16[4,2,96,1152]{3,2,0,1:T(8,128)(2,1)} collective-permute-done((bf16[4,2,96,1152]{3,2,0,1:T(8,128)(2,1)}, bf16[4,2,96,1152]{3,2,0,1:T(8,128)(2,1)}, u32[]{:S(2)}, u32[]{:S(2)}) %collective-permute-start.27) | collective-permute-done | bytes 1769504 | tf_op jit(solution)/shard_map/ppermute | solution.py:515
  769.4 16.2 %collective-permute-done.26 = bf16[4,96,896]{2,1,0:T(8,128)(2,1)S(1)} collective-permute-done((bf16[4,96,896]{2,1,0:T(8,128)(2,1)S(1)}, bf16[4,96,896]{2,1,0:T(8,128)(2,1)S(1)}, u32[]{:S(2)}, u32[]{:S(2)}) %collective-permute-start.26) | collective-permute-done | bytes 688160 | tf_op jit(solution)/shard_map/ppermute | solution.py:515
  785.8 8.1 collective-permute-done.28
  796.2 5.7 collective-permute-start.29
  805.8 4.8 fusion.24
  811.8 13.6 %collective-permute-done.30 = bf16[96,2048]{1,0:T(8,128)(2,1)} collective-permute-done((bf16[96,2048]{1,0:T(8,128)(2,1)}, bf16[96,2048]{1,0:T(8,128)(2,1)}, u32[]{:S(2)}, u32[]{:S(2)}) %collective-permute-start.30) | collective-permute-done | bytes 393248 | tf_op jit(solution)/shard_map/ppermute | solution.py:487
  829.3 7.4 slice_convert_fusion
  (564 shorter events, 316.6 us)
Async XLA Ops:
  12.8 19.1 %collective-permute-start.8 = (s32[4,512]{1,0:T(4,128)}, s32[4,512]{1,0:T(4,128)S(1)}, u32[]{:S(2)}, u32[]{:S(2)}) collective-permute-start(s32[4,512]{1,0:T(4,128)} %after.16), channel_id=1, source_target_pairs={{0,8},{2,10},{4,12},{6,14},{8,16},{10,18},{12,20},{14,22},{16,24},... | collective-permute-start | bytes 24584 | tf_op jit(solution)/shard_map/ppermute | solution.py:487
  15.9 20.3 %collective-permute-start.9 = (s32[4,512]{1,0:T(4,128)}, s32[4,512]{1,0:T(4,128)S(1)}, u32[]{:S(2)}, u32[]{:S(2)}) collective-permute-start(s32[4,512]{1,0:T(4,128)} %after.16), channel_id=1, source_target_pairs={{0,16},{2,18},{4,20},{6,22},{8,24},{10,26},{12,28},{14,30},{16,0},... | collective-permute-start | bytes 24584 | tf_op jit(solution)/shard_map/ppermute | solution.py:487
  18.5 17.8 %collective-permute-start.10 = (s32[4,512]{1,0:T(4,128)}, s32[4,512]{1,0:T(4,128)}, u32[]{:S(2)}, u32[]{:S(2)}) collective-permute-start(s32[4,512]{1,0:T(4,128)} %after.16), channel_id=1, source_target_pairs={{0,24},{2,26},{4,28},{6,30},{8,0},{10,2},{12,4},{14,6},{16,8},{18,... | collective-permute-start | bytes 24584 | tf_op jit(solution)/shard_map/ppermute | solution.py:487
  19.8 22.3 %collective-permute-start.1 = (bf16[96,1920]{1,0:T(8,128)(2,1)}, bf16[96,1920]{1,0:T(8,128)(2,1)S(1)}, u32[]{:S(2)}, u32[]{:S(2)}) collective-permute-start(bf16[96,1920]{1,0:T(8,128)(2,1)} %concatenate.134.refs_1_), channel_id=1, source_target_pairs={{0,8},{2,10},{4,12},{6,14},{8,16},{10,18},{12,20},{14,22},{16,24},... | collective-permute-start | bytes 1105928 | tf_op jit(solution)/shard_map/ppermute | solution.py:487
  20.5 26.9 %collective-permute-start.2 = (bf16[96,1920]{1,0:T(8,128)(2,1)}, bf16[96,1920]{1,0:T(8,128)(2,1)}, u32[]{:S(2)}, u32[]{:S(2)}) collective-permute-start(bf16[96,1920]{1,0:T(8,128)(2,1)} %concatenate.134.refs_1_), channel_id=1, source_target_pairs={{0,16},{2,18},{4,20},{6,22},{8,24},{10,26},{12,28},{14,30},{16,0},... | collective-permute-start | bytes 1105928 | tf_op jit(solution)/shard_map/ppermute | solution.py:487
  32.0 24.8 %collective-permute-start.3 = (bf16[96,1920]{1,0:T(8,128)(2,1)S(1)}, bf16[96,1920]{1,0:T(8,128)(2,1)S(1)}, u32[]{:S(2)}, u32[]{:S(2)}) collective-permute-start(bf16[96,1920]{1,0:T(8,128)(2,1)S(1)} %copy-done.78), channel_id=1, source_target_pairs={{0,24},{2,26},{4,28},{6,30},{8,0},{10,2},{12,4},{14,6},{16,8},{18,... | collective-permute-start | bytes 1105928 | tf_op jit(solution)/shard_map/ppermute | solution.py:487
  36.2 30.1 %collective-permute-start = (bf16[256,1536]{1,0:T(8,128)(2,1)S(1)}, bf16[256,1536]{1,0:T(8,128)(2,1)}, u32[]{:S(2)}, u32[]{:S(2)}) collective-permute-start(bf16[256,1536]{1,0:T(8,128)(2,1)S(1)} %copy-done.66), channel_id=1, source_target_pairs={{0,1},{1,0},{2,3},{3,2},{4,5},{5,4},{6,7},{7,6},{8,9},{9,8},{10,11... | collective-permute-start | bytes 2359304 | tf_op jit(solution)/shard_map/ppermute | solution.py:456
  37.6 219.3 %all-to-all-start = ((bf16[32,96,1152]{2,1,0:T(8,128)(2,1)}), bf16[32,96,1152]{2,1,0:T(8,128)(2,1)}, u32[]{:S(2)}, u32[]{:S(2)}) async-start(bf16[32,96,1152]{2,1,0:T(8,128)(2,1)} %after.17), calls=%async_computation | async-start | bytes 14155776 | tf_op jit(solution)/shard_map/all_to_all | solution.py:477
  42.1 184.8 %all-gather.5.cloned.1.call-start = ((), (), s32[]{:S(2)}) async-start(), calls=%async_computation.9 | async-start | bytes 3932160 | tf_op jit(solution)/shard_map/all_gather | solution.py:530
  58.8 67.5 %collective-permute-start.4 = (bf16[4,96,1920]{2,1,0:T(8,128)(2,1)S(1)}, bf16[4,96,1920]{2,1,0:T(8,128)(2,1)}, u32[]{:S(2)}, u32[]{:S(2)}) collective-permute-start(bf16[4,96,1920]{2,1,0:T(8,128)(2,1)S(1)} %pad_maximum_fusion.5.refs_1_), channel_id=1, source_target_pairs={{0,2},{2,0},{4,6},{6,4},{8,10},{10,8},{12,14},{14,12},{16,18},{18,... | collective-permute-start | bytes 4423688 | tf_op jit(solution)/shard_map/ppermute | solution.py:500
  61.3 67.7 %collective-permute-start.5 = (bf16[4,96,1920]{2,1,0:T(8,128)(2,1)S(1)}, bf16[4,96,1920]{2,1,0:T(8,128)(2,1)}, u32[]{:S(2)}, u32[]{:S(2)}) collective-permute-start(bf16[4,96,1920]{2,1,0:T(8,128)(2,1)S(1)} %pad_maximum_fusion.5.refs_1_), channel_id=1, source_target_pairs={{0,4},{2,6},{4,0},{6,2},{8,12},{10,14},{12,8},{14,10},{16,20},{18,... | collective-permute-start | bytes 4423688 | tf_op jit(solution)/shard_map/ppermute | solution.py:500
  61.3 113.6 %collective-permute-start.6 = (bf16[4,96,1920]{2,1,0:T(8,128)(2,1)S(1)}, bf16[4,96,1920]{2,1,0:T(8,128)(2,1)}, u32[]{:S(2)}, u32[]{:S(2)}) collective-permute-start(bf16[4,96,1920]{2,1,0:T(8,128)(2,1)S(1)} %pad_maximum_fusion.5.refs_1_), channel_id=1, source_target_pairs={{0,6},{2,4},{4,2},{6,0},{8,14},{10,12},{12,10},{14,8},{16,22},{18,... | collective-permute-start | bytes 4423688 | tf_op jit(solution)/shard_map/ppermute | solution.py:500
  62.9 256.0 %all-gather.7.cloned.1.call-start = ((), (), s32[]{:S(2)}) async-start(), calls=%async_computation.10 | async-start | bytes 3932160 | tf_op jit(solution)/shard_map/all_gather | solution.py:530
  256.9 63.6 %all-to-all-start.1 = ((bf16[8,4,48,1664]{3,2,1,0:T(8,128)(2,1)}), bf16[8,4,48,1664]{3,2,1,0:T(8,128)(2,1)}, u32[]{:S(2)}, u32[]{:S(2)}) async-start(bf16[8,4,48,1664]{3,2,1,0:T(8,128)(2,1)} %bitcast.229), calls=%async_computation.1 | async-start | bytes 10223616 | tf_op jit(solution)/shard_map/all_to_all | solution.py:553
  339.0 28.9 %collective-permute-start.15 = (bf16[2,4,48,1536]{3,2,1,0:T(8,128)(2,1)S(1)}, bf16[2,4,48,1536]{3,2,1,0:T(8,128)(2,1)S(1)}, u32[]{:S(2)}, u32[]{:S(2)}) collective-permute-start(bf16[2,4,48,1536]{3,2,1,0:T(8,128)(2,1)S(1)} %pad_maximum_fusion.7), channel_id=1, source_target_pairs={{0,2},{2,0},{4,6},{6,4},{8,10},{10,8},{12,14},{14,12},{16,18},{18,... | collective-permute-start | bytes 3538952 | tf_op jit(solution)/shard_map/ppermute | solution.py:541
  340.7 52.7 %collective-permute-start.17 = (bf16[2,4,48,1536]{3,2,1,0:T(8,128)(2,1)S(1)}, bf16[2,4,48,1536]{3,2,1,0:T(8,128)(2,1)S(1)}, u32[]{:S(2)}, u32[]{:S(2)}) collective-permute-start(bf16[2,4,48,1536]{3,2,1,0:T(8,128)(2,1)S(1)} %pad_maximum_fusion.9), channel_id=1, source_target_pairs={{0,4},{2,6},{4,0},{6,2},{8,12},{10,14},{12,8},{14,10},{16,20},{18,... | collective-permute-start | bytes 3538952 | tf_op jit(solution)/shard_map/ppermute | solution.py:541
  342.3 73.7 %collective-permute-start.14 = (bf16[2,4,48,1536]{3,2,1,0:T(8,128)(2,1)S(1)}, bf16[2,4,48,1536]{3,2,1,0:T(8,128)(2,1)S(1)}, u32[]{:S(2)}, u32[]{:S(2)}) collective-permute-start(bf16[2,4,48,1536]{3,2,1,0:T(8,128)(2,1)S(1)} %pad_maximum_fusion.6), channel_id=1, source_target_pairs={{0,6},{2,4},{4,2},{6,0},{8,14},{10,12},{12,10},{14,8},{16,22},{18,... | collective-permute-start | bytes 3538952 | tf_op jit(solution)/shard_map/ppermute | solution.py:541
  385.2 32.6 %collective-permute-start.16 = (bf16[384,1536]{1,0:T(8,128)(2,1)S(1)}, bf16[384,1536]{1,0:T(8,128)(2,1)S(1)}, u32[]{:S(2)}, u32[]{:S(2)}) collective-permute-start(bf16[384,1536]{1,0:T(8,128)(2,1)S(1)} %get-tuple-element.45), channel_id=1, source_target_pairs={{0,2},{2,0},{4,6},{6,4},{8,10},{10,8},{12,14},{14,12},{16,18},{18,... | collective-permute-start | bytes 3538952 | tf_op jit(solution)/shard_map/ppermute | solution.py:541
  414.2 31.6 %collective-permute-start.18 = (bf16[384,1536]{1,0:T(8,128)(2,1)}, bf16[384,1536]{1,0:T(8,128)(2,1)}, u32[]{:S(2)}, u32[]{:S(2)}) collective-permute-start(bf16[384,1536]{1,0:T(8,128)(2,1)} %get-tuple-element.53), channel_id=1, source_target_pairs={{0,4},{2,6},{4,0},{6,2},{8,12},{10,14},{12,8},{14,10},{16,20},{18,... | collective-permute-start | bytes 3538952 | tf_op jit(solution)/shard_map/ppermute | solution.py:541
  443.4 28.2 %collective-permute-start.19 = (bf16[384,1536]{1,0:T(8,128)(2,1)S(1)}, bf16[384,1536]{1,0:T(8,128)(2,1)}, u32[]{:S(2)}, u32[]{:S(2)}) collective-permute-start(bf16[384,1536]{1,0:T(8,128)(2,1)S(1)} %get-tuple-element.58), channel_id=1, source_target_pairs={{0,6},{2,4},{4,2},{6,0},{8,14},{10,12},{12,10},{14,8},{16,22},{18,... | collective-permute-start | bytes 3538952 | tf_op jit(solution)/shard_map/ppermute | solution.py:541
  471.6 58.1 %all-to-all-start.2 = ((bf16[32,96,384]{2,1,0:T(8,128)(2,1)}), bf16[32,96,384]{2,1,0:T(8,128)(2,1)}, u32[]{:S(2)}, u32[]{:S(2)}) async-start(bf16[32,96,384]{2,1,0:T(8,128)(2,1)} %after.24), calls=%async_computation.2 | async-start | bytes 4718592 | tf_op jit(solution)/shard_map/all_to_all | solution.py:477
  542.6 59.3 %all-to-all-start.3 = ((bf16[8,4,48,1536]{3,2,1,0:T(8,128)(2,1)}), bf16[8,4,48,1536]{3,2,1,0:T(8,128)(2,1)}, u32[]{:S(2)}, u32[]{:S(2)}) async-start(bf16[8,4,48,1536]{3,2,1,0:T(8,128)(2,1)} %after.25), calls=%async_computation.3 | async-start | bytes 9437184 | tf_op jit(solution)/shard_map/all_to_all | solution.py:553
  547.2 77.4 %reduce-scatter.5.cloned.1.call-start = ((), (), s32[]{:S(2)}) async-start(), calls=%async_computation.8 | async-start | bytes 3932160 | tf_op jit(solution)/shard_map/reduce_scatter | solution.py:535
  637.2 192.1 %all-to-all-start.4 = ((bf16[32,96,768]{2,1,0:T(8,128)(2,1)}), bf16[32,96,768]{2,1,0:T(8,128)(2,1)}, u32[]{:S(2)}, u32[]{:S(2)}) async-start(bf16[32,96,768]{2,1,0:T(8,128)(2,1)} %after.29), calls=%async_computation.6 | async-start | bytes 9437184 | tf_op jit(solution)/shard_map/all_to_all | solution.py:477
  640.8 165.0 %reduce-scatter.3.cloned.1.call-start = ((), (), s32[]{:S(2)}) async-start(), calls=%async_computation.7 | async-start | bytes 3932160 | tf_op jit(solution)/shard_map/reduce_scatter | solution.py:535
  683.2 39.7 %collective-permute-start.25 = (bf16[4,2,96,896]{3,2,0,1:T(8,128)(2,1)}, bf16[4,2,96,896]{3,2,0,1:T(8,128)(2,1)}, u32[]{:S(2)}, u32[]{:S(2)}) collective-permute-start(bf16[4,2,96,896]{3,2,0,1:T(8,128)(2,1)} %fusion.33), channel_id=1, source_target_pairs={{0,2},{2,0},{4,6},{6,4},{8,10},{10,8},{12,14},{14,12},{16,18},{18,... | collective-permute-start | bytes 4128776 | tf_op jit(solution)/shard_map/ppermute | solution.py:515
  711.3 53.5 %collective-permute-start.27 = (bf16[4,2,96,1152]{3,2,0,1:T(8,128)(2,1)}, bf16[4,2,96,1152]{3,2,0,1:T(8,128)(2,1)}, u32[]{:S(2)}, u32[]{:S(2)}) collective-permute-start(bf16[4,2,96,1152]{3,2,0,1:T(8,128)(2,1)} %fusion.20), channel_id=1, source_target_pairs={{0,4},{2,6},{4,0},{6,2},{8,12},{10,14},{12,8},{14,10},{16,20},{18,... | collective-permute-start | bytes 5308424 | tf_op jit(solution)/shard_map/ppermute | solution.py:515
  715.6 51.9 %collective-permute-start.24 = (f32[256,1536]{1,0:T(8,128)}, f32[256,1536]{1,0:T(8,128)}, u32[]{:S(2)}, u32[]{:S(2)}) collective-permute-start(f32[256,1536]{1,0:T(8,128)} %slice.292), channel_id=1, source_target_pairs={{0,1},{1,0},{2,3},{3,2},{4,5},{5,4},{6,7},{7,6},{8,9},{9,8},{10,11... | collective-permute-start | bytes 4718600 | tf_op jit(solution)/shard_map/ppermute | solution.py:456
  725.5 60.1 %collective-permute-start.26 = (bf16[4,96,896]{2,1,0:T(8,128)(2,1)S(1)}, bf16[4,96,896]{2,1,0:T(8,128)(2,1)S(1)}, u32[]{:S(2)}, u32[]{:S(2)}) collective-permute-start(bf16[4,96,896]{2,1,0:T(8,128)(2,1)S(1)} %fusion.55), channel_id=1, source_target_pairs={{0,4},{2,6},{4,0},{6,2},{8,12},{10,14},{12,8},{14,10},{16,20},{18,... | collective-permute-start | bytes 2064392 | tf_op jit(solution)/shard_map/ppermute | solution.py:515
  766.9 26.9 %collective-permute-start.28 = (bf16[4,96,1152]{2,1,0:T(8,128)(2,1)S(1)}, bf16[4,96,1152]{2,1,0:T(8,128)(2,1)S(1)}, u32[]{:S(2)}, u32[]{:S(2)}) collective-permute-start(bf16[4,96,1152]{2,1,0:T(8,128)(2,1)S(1)} %fusion.52), channel_id=1, source_target_pairs={{0,2},{2,0},{4,6},{6,4},{8,10},{10,8},{12,14},{14,12},{16,18},{18,... | collective-permute-start | bytes 2654216 | tf_op jit(solution)/shard_map/ppermute | solution.py:515
  802.7 22.7 %collective-permute-start.30 = (bf16[96,2048]{1,0:T(8,128)(2,1)}, bf16[96,2048]{1,0:T(8,128)(2,1)}, u32[]{:S(2)}, u32[]{:S(2)}) collective-permute-start(bf16[96,2048]{1,0:T(8,128)(2,1)} %pad_maximum_fusion.15), channel_id=1, source_target_pairs={{0,16},{2,18},{4,20},{6,22},{8,24},{10,26},{12,28},{14,30},{16,0},... | collective-permute-start | bytes 1179656 | tf_op jit(solution)/shard_map/ppermute | solution.py:487
  803.5 21.9 %collective-permute-start.31 = (bf16[96,2048]{1,0:T(8,128)(2,1)}, bf16[96,2048]{1,0:T(8,128)(2,1)}, u32[]{:S(2)}, u32[]{:S(2)}) collective-permute-start(bf16[96,2048]{1,0:T(8,128)(2,1)} %pad_maximum_fusion.16), channel_id=1, source_target_pairs={{0,24},{2,26},{4,28},{6,30},{8,0},{10,2},{12,4},{14,6},{16,8},{18,... | collective-permute-start | bytes 1179656 | tf_op jit(solution)/shard_map/ppermute | solution.py:487
  (149 other events, 1629.5 us)
Sparse Core Ops, SparseCore 0:
  63.0 151.7 all-gather.4
  257.0 61.7 all-gather.6
  555.0 59.5 reduce-scatter.4
  643.6 109.4 reduce-scatter.2

commit v4 on v3

--- a/solution.py
+++ b/solution.py
@@ -506,6 +506,7 @@
 def row_reduce(halves, level, place):
     block = halves[0].shape[0] // (LINE * PLANE)
     halves = [h.reshape(LINE, 2, 2, block, h.shape[1]) for h in halves]
+    marks = []
     for flips in ((1, 2), (2, 1)):
         for i, flip in enumerate(flips):
             axis = min(3 - flip, halves[i].ndim - 3)
@@ -514,6 +515,7 @@
             away = lax.dynamic_index_in_dim(halves[i], 1 - bit, axis, False)
             away = lax.ppermute(away.astype(jnp.bfloat16), "row", plane_pairs(flip))
             halves[i] = kept + away.astype(jnp.float32)
+            marks.append(halves[i])
     order = [(level + step) % LINE for step in range(LINE)]
     parts = [
         jnp.concatenate([lax.dynamic_index_in_dim(h, i, 0, False) for h in halves], axis=1)
@@ -523,7 +525,7 @@
     total = parts[0]
     for part in moved:
         total = total + part.astype(jnp.float32)
-    return total
+    return total, marks[2:]
 
 
 def line_gather(block):
@@ -735,7 +737,7 @@
         ],
         out_specs=[part, part],
         out_shape=[
-            jax.ShapeDtypeStruct(shape, jnp.float32),
+            jax.ShapeDtypeStruct(shape, jnp.bfloat16),
             jax.ShapeDtypeStruct(shape, jnp.bfloat16),
         ],
         compiler_params=pltpu.CompilerParams(vmem_limit_bytes=40 << 20),
@@ -828,6 +830,9 @@
     nt = (((1,), (1,)), ((), ()))
     tn = (((0,), (0,)), ((), ()))
 
+    routes_rows = span * TOPK // 64
+    routes_own = routes.T.astype(bf16).reshape(routes_rows, 64)
+    routes_own = jnp.pad(routes_own, ((0, row_block - routes_rows), (0, 0)))
     packed = jnp.concatenate(
         [
             query_weight,
@@ -837,16 +842,18 @@
             router_weight,
             attention_gain[:, None],
             expert_gain[:, None],
-            jnp.zeros((row_block, 128 - E - 2), bf16),
+            routes_own,
+            jnp.zeros((row_block, 126 - E - routes_own.shape[1]), bf16),
         ],
         axis=1,
     )
     packed_line = jnp.stack([packed] + [line_shift(packed, step) for step in range(1, LINE)])
-    routes_own = after(routes.T, packed)
-    routes_line = [routes_own] + [line_shift(routes_own, step) for step in range(1, LINE)]
-    routes_line = reorder(jnp.stack(routes_line), [(level - z) % LINE for z in range(LINE)], 0)
+    o0 = head_cols + 2 * kv_cols
+    first = o0 + head_cols + E + 2
+    routes_line = packed_line[:, :routes_rows, first : first + 64].reshape(LINE, TOPK, span)
+    routes_line = reorder(routes_line, [(level - z) % LINE for z in range(LINE)], 0)
+    routes_line = routes_line.astype(jnp.int32)
     packed_full = row_gather(packed_line, level, place)
-    o0 = head_cols + 2 * kv_cols
     qkv_cols, out_full = packed_full[:, :o0], packed_full[:, o0:]
     output_t = out_full[:, :head_cols]
     router_full = out_full[:, head_cols : head_cols + E]
@@ -866,11 +873,11 @@
 
     slots = LINE * share * mates
 
-    nil = packed_line[0, 0, 0] * 0
+    nil = packed_line[1, 0, 0] * 0
     weights = jnp.concatenate(
         [gate_weight, up_weight, down_weight.transpose(0, 2, 1) + nil], axis=2
     )
-    weights = exchange(after(weights, routes_line))
+    weights = exchange(after(weights, packed_line))
     cot_line = line_gather(after(cotangent, packed_line))
 
     hidden_all = both_cores(hidden_in)
@@ -928,7 +935,7 @@
 
     def combine(table, near, far, far_block=0):
         kept, away = combine_rows(table, near, far, far_block)
-        return (kept + swap_cores(away).astype(f32)).astype(bf16)
+        return (kept.astype(f32) + swap_cores(away).astype(f32)).astype(bf16)
 
     shape = (2, LINE, share, MODEL_WIDTH)
     back = [b.reshape(shape) for b in back]
@@ -986,25 +993,18 @@
         [
             router_grad,
             gain_second_grad[:, None],
-            jnp.zeros((MODEL_WIDTH, 128 - E - 1), f32),
+            gain_first_grad[:, None],
+            jnp.zeros((MODEL_WIDTH, 128 - E - 2), f32),
         ],
         axis=1,
     )
-    down_home = after(down_home, grad_qkv)
-    pad = jnp.zeros((MODEL_WIDTH, 127), f32)
-    owned = row_reduce(
-        [
-            jnp.concatenate([output_t_grad, extra], axis=1),
-            jnp.concatenate([qkv_grad, gain_first_grad[:, None], pad], axis=1),
-        ],
-        level,
-        place,
-    )
-    output_own, owned = owned[:, :head_cols], owned[:, head_cols:]
-    small_own, qkv_own = owned[:, :128], owned[:, 128 : 128 + o0]
-    small_own = jnp.concatenate([small_own[:, : E + 1], owned[:, 128 + o0 : 129 + o0]], axis=1)
+    owned, marks = row_reduce(
+        [jnp.concatenate([output_t_grad, extra], axis=1), qkv_grad], level, place
+    )
+    output_own, qkv_own = owned[:, :head_cols], owned[:, head_cols + 128 :]
+    small_own = owned[:, head_cols : head_cols + 128]
     small_own = small_own + swap_cores(small_own)
-    gate_up_home = after(gate_up_home, small_own)
+    gate_up_home = after(gate_up_home, *marks)
     return (
         block_out,
         input_grad,

time: 860 us -> 860 us (level)
  waiting for transfers between devices: 388 us -> 406 us
  local copies, waits for them, and re-layouts: 153 us -> 143 us
    all_to_all x3, waiting for transfers between devices: 67.7 us -> 121 us  [exchange(): return lax.all_to_all(block, GRID, split_axis=0, concat_axis=0, tiled=True)]
    ppermute x3, waiting for transfers between devices: 102 us -> 56.9 us  [row_gather(): lax.ppermute(line, 'row', plane_pairs(flip))]
    all_gather x2, waiting for transfers between devices: 57.3 us -> 81 us  [line_gather(): lax.all_gather(block, 'row', axis=0, tiled=False, axis_index_groups=LINES)]
    concatenate x4 -> x0, local copies, waits for them, and re-layouts: 12.9 us -> none  [tokens_move(): jnp.concatenate([qkv_grad, gain_first_grad[:, None], pad], axis=1)]
    ppermute x9 -> x6, waiting for transfers between devices: 28.4 us -> 17.6 us  [line_shift(): return lax.ppermute(block, 'row', pairs)]
    concatenate x5 -> x7, local copies, waits for them, and re-layouts: 4.41 us -> 13.5 us  [tokens_move(): jnp.concatenate([output_t_grad, extra], axis=1)]
    unnamed x305 -> x274, local copies, waits for them, and re-layouts: 90.3 us -> 84.1 us
    ppermute x9 -> x6, starting transfers between devices: 19 us -> 18.6 us  [line_shift(): return lax.ppermute(block, 'row', pairs)]
  transfers between devices with their start and end apart: 42 -> 39, of which waited for: 26 -> 29; matrix products, arithmetic and copies ran while one was open for 23% -> 23% of each run, Pallas kernels for 10% -> 10%
where the time goes in v4:
time: 860 us; the launch traced here: 851 us
  waiting for transfers between devices  406 us (47%)
  local copies, waits for them, and re-layouts  143 us (17%)
  Pallas kernels  95.5 us (11%)
  other arithmetic  78.9 us (9%)
  starting transfers between devices  65 us (8%)
  matrix products  46.1 us (5%)
  between operations  16.6 us (2%)
    all_to_all x3, waiting for transfers between devices, exchange(): return lax.all_to_all(block, GRID, split_axis=0, concat_axis=0, tiled=True)  121 us
    unnamed x274, local copies, waits for them, and re-layouts  84.1 us
    all_gather x2, waiting for transfers between devices, line_gather(): lax.all_gather(block, 'row', axis=0, tiled=False, axis_index_groups=LINES)  81 us
    ppermute x3, waiting for transfers between devices, row_gather(): lax.ppermute(line, 'row', plane_pairs(flip))  56.9 us
    pallas_call x4, Pallas kernels, expert_rows(): pl.pallas_call(expert_body, grid_spec=pltpu.PrefetchScalarGridSpec(num_sc...  54.9 us
    ppermute x4, waiting for transfers between devices, row_reduce(): away = lax.ppermute(away.astype(jnp.bfloat16), 'row', plane_pairs(flip))  50 us
    all_to_all x2, waiting for transfers between devices, plane_all(): lax.all_to_all(block, GRID, split_axis=0, concat_axis=0, tiled=True, axis...  29.6 us
    ppermute x6, waiting for transfers between devices, plane_move(): return lax.ppermute(block, 'row', plane_pairs(move))  29 us
  transfers between devices with their start and end apart: 39, of which 29 were waited for; matrix products, arithmetic and copies ran while one was open for 23% of the time, Pallas kernels for 10%

profile of v4, /device:TPU:0, one launch (start us, length us, event | category | flops | bytes accessed | tf_op | source)
XLA Modules:
  0.0 850.8 jit_solution(14422528312280841610)
XLA Ops:
  26.1 15.0 %collective-permute-done.2 = bf16[96,1920]{1,0:T(8,128)(2,1)S(1)} collective-permute-done((bf16[96,1920]{1,0:T(8,128)(2,1)S(1)}, bf16[96,1920]{1,0:T(8,128)(2,1)S(1)}, u32[]{:S(2)}, u32[]{:S(2)}) %collective-permute-start.2) | collective-permute-done | bytes 368672 | tf_op jit(solution)/shard_map/ppermute | solution.py:487
  51.4 11.8 %all-to-all-start = ((bf16[32,96,1152]{2,1,0:T(8,128)(2,1)}), bf16[32,96,1152]{2,1,0:T(8,128)(2,1)}, u32[]{:S(2)}, u32[]{:S(2)}) async-start(bf16[32,96,1152]{2,1,0:T(8,128)(2,1)} %after.14), calls=%async_computation | async-start | bytes 14155776 | tf_op jit(solution)/shard_map/all_to_all | solution.py:477
  68.9 11.7 %collective-permute-done.4 = bf16[4,96,1920]{2,1,0:T(8,128)(2,1)} collective-permute-done((bf16[4,96,1920]{2,1,0:T(8,128)(2,1)S(1)}, bf16[4,96,1920]{2,1,0:T(8,128)(2,1)}, u32[]{:S(2)}, u32[]{:S(2)}) %collective-permute-start.4) | collective-permute-done | bytes 1474592 | tf_op jit(solution)/shard_map/ppermute | solution.py:500
  83.2 42.5 %collective-permute-done.5 = bf16[4,96,1920]{2,1,0:T(8,128)(2,1)} collective-permute-done((bf16[4,96,1920]{2,1,0:T(8,128)(2,1)S(1)}, bf16[4,96,1920]{2,1,0:T(8,128)(2,1)}, u32[]{:S(2)}, u32[]{:S(2)}) %collective-permute-start.5) | collective-permute-done | bytes 1474592 | tf_op jit(solution)/shard_map/ppermute | solution.py:500
  184.4 23.1 %all-gather.5.cloned.1.call-done = bf16[1024,1536]{1,0:T(8,128)(2,1)} async-done(((bf16[256,1536]{1,0:T(8,128)(2,1)}), bf16[1024,1536]{1,0:T(8,128)(2,1)}) %all-gather.5.cloned.1.call-update) | async-done | bytes 3145744 | tf_op jit(solution)/shard_map/all_gather | solution.py:532
  219.6 49.7 %all-to-all-done.refs_1_ = bf16[32,96,1152]{2,1,0:T(8,128)(2,1)} async-done(((bf16[32,96,1152]{2,1,0:T(8,128)(2,1)}), bf16[32,96,1152]{2,1,0:T(8,128)(2,1)}, u32[]{:S(2)}, u32[]{:S(2)}) %all-to-all-start) | async-done | bytes 7077920 | tf_op jit(solution)/shard_map/all_to_all | solution.py:477
  274.0 58.0 %all-gather.7.cloned.1.call-done = bf16[1024,1536]{1,0:T(8,128)(2,1)} async-done(((bf16[256,1536]{1,0:T(8,128)(2,1)}), bf16[1024,1536]{1,0:T(8,128)(2,1)}) %all-gather.7.cloned.1.call-update) | async-done | bytes 3145744 | tf_op jit(solution)/shard_map/all_gather | solution.py:532
  333.0 4.9 collective-permute-done.9.other_ref
  357.9 13.2 %expert_rows.4 = (bf16[384,1536]{1,0:T(8,128)(2,1)S(1)}, bf16[4,2,192,1536]{3,2,1,0:T(8,128)(2,1)S(1)}, bf16[384,1536]{1,0:T(8,128)(2,1)S(1)}, bf16[384,768]{1,0...) custom-call(s32[3]{0:T(128)S(1)} %pad_add_fusion.4.where_ref, ...), custom_call_target="tpu_custom_call" | custom-call | flops 5435817984 | bytes 7667712 | tf_op jit(solution)/shard_map/expert_rows/pallas_call | solution.py:645
  373.6 9.2 %collective-permute-done.12 = bf16[2,4,48,1536]{3,2,1,0:T(8,128)(2,1)S(1)} collective-permute-done((bf16[2,4,48,1536]{3,2,1,0:T(8,128)(2,1)S(1)}, bf16[2,4,48,1536]{3,2,1,0:T(8,128)(2,1)S(1)}, u32[]{:S(2)}, u32[]{:S(2)}) %collective-permute-start.12) | collective-permute-done | bytes 1179680 | tf_op jit(solution)/shard_map/ppermute | solution.py:543
  382.8 13.6 %expert_rows.5 = (bf16[384,1536]{1,0:T(8,128)(2,1)S(1)}, bf16[4,2,192,1536]{3,2,1,0:T(8,128)(2,1)S(1)}, bf16[384,1536]{1,0:T(8,128)(2,1)S(1)}, bf16[384,768]{1,0...) custom-call(s32[3]{0:T(128)S(1)} %pad_add_fusion.4.where_ref, ...), custom_call_target="tpu_custom_call", output_to_operand_aliasing={{1}: (5, {})} | custom-call | flops 5435817984 | bytes 7667712 | tf_op jit(solution)/shard_map/expert_rows/pallas_call | solution.py:645
  401.4 8.6 %collective-permute-done.14 = bf16[2,4,48,1536]{3,2,1,0:T(8,128)(2,1)S(1)} collective-permute-done((bf16[2,4,48,1536]{3,2,1,0:T(8,128)(2,1)S(1)}, bf16[2,4,48,1536]{3,2,1,0:T(8,128)(2,1)S(1)}, u32[]{:S(2)}, u32[]{:S(2)}) %collective-permute-start.14) | collective-permute-done | bytes 1179680 | tf_op jit(solution)/shard_map/ppermute | solution.py:543
  410.0 14.4 %expert_rows.6 = (bf16[384,1536]{1,0:T(8,128)(2,1)}, bf16[4,2,192,1536]{3,2,1,0:T(8,128)(2,1)S(1)}, bf16[384,1536]{1,0:T(8,128)(2,1)S(1)}, bf16[384,768]{1,0:T(8...) custom-call(s32[3]{0:T(128)S(1)} %pad_add_fusion.4.where_ref, ...), custom_call_target="tpu_custom_call", output_to_operand_aliasing={{1}: (5, {})} | custom-call | flops 5435817984 | bytes 7667712 | tf_op jit(solution)/shard_map/expert_rows/pallas_call | solution.py:645
  438.2 13.6 %expert_rows.7 = (bf16[384,1536]{1,0:T(8,128)(2,1)S(1)}, bf16[4,2,192,1536]{3,2,1,0:T(8,128)(2,1)S(1)}, bf16[384,1536]{1,0:T(8,128)(2,1)S(1)}, bf16[384,768]{1,0...) custom-call(s32[3]{0:T(128)S(1)} %pad_add_fusion.4.where_ref, ...), custom_call_target="tpu_custom_call", output_to_operand_aliasing={{1}: (5, {})} | custom-call | flops 5435817984 | bytes 7667712 | tf_op jit(solution)/shard_map/expert_rows/pallas_call | solution.py:645
  468.8 7.8 shard_grad.2
  476.6 9.9 %collective-permute-done.16 = bf16[384,1536]{1,0:T(8,128)(2,1)} collective-permute-done((bf16[384,1536]{1,0:T(8,128)(2,1)S(1)}, bf16[384,1536]{1,0:T(8,128)(2,1)}, u32[]{:S(2)}, u32[]{:S(2)}) %collective-permute-start.16) | collective-permute-done | bytes 1179680 | tf_op jit(solution)/shard_map/ppermute | solution.py:543
  494.8 49.8 %all-to-all-done.2.refs_1_ = bf16[32,96,384]{2,1,0:T(8,128)(2,1)} async-done(((bf16[32,96,384]{2,1,0:T(8,128)(2,1)}), bf16[32,96,384]{2,1,0:T(8,128)(2,1)}, u32[]{:S(2)}, u32[]{:S(2)}) %all-to-all-start.2) | async-done | bytes 2359328 | tf_op jit(solution)/shard_map/all_to_all | solution.py:477
  549.3 5.3 combine_rows.2
  562.3 5.4 add_convert_fusion.1.refs_1_
  573.7 13.1 %shard_grad.3 = bf16[16,2,96,768]{3,2,1,0:T(8,128)(2,1)} custom-call(bf16[384,1536]{1,0:T(8,128)(2,1)S(1)} %bitcast.238, bf16[384,1536]{1,0:T(8,128)(2,1)} %bitcast.241, bf16[384,1536]{1,0:T(8,128)(2,1)} %bitcast.244, bf16[384,1536]{1,0:T(8,128)(2,1)} %after.19.x_ref.refs_3_, bf16[384,768]{1,0:T(8,128)(2,1)S(1)} %copy-done.59, ...), custom_call_target="tpu_custom_call" | custom-call | flops 7247757312 | bytes 14155776 | tf_op jit(solution)/shard_map/shard_grad/pallas_call | solution.py:779
  586.8 29.0 %all-to-all-done.3.refs_0_.refs_1_ = bf16[8,4,48,1536]{3,2,1,0:T(8,128)(2,1)} async-done(((bf16[8,4,48,1536]{3,2,1,0:T(8,128)(2,1)}), bf16[8,4,48,1536]{3,2,1,0:T(8,128)(2,1)}, u32[]{:S(2)}, u32[]{:S(2)}) %all-to-all-start.3) | async-done | bytes 4718624 | tf_op jit(solution)/shard_map/all_to_all | solution.py:555
  616.7 7.0 combine_rows.3
  660.7 6.2 multiply_reduce_fusion
  685.2 6.3 fusion.5
  692.8 5.2 fusion.27
  699.0 8.5 concatenate.154
  725.4 29.4 %collective-permute-done.22 = bf16[4,2,96,896]{3,2,0,1:T(8,128)(2,1)} collective-permute-done((bf16[4,2,96,896]{3,2,0,1:T(8,128)(2,1)}, bf16[4,2,96,896]{3,2,0,1:T(8,128)(2,1)}, u32[]{:S(2)}, u32[]{:S(2)}) %collective-permute-start.22) | collective-permute-done | bytes 1376288 | tf_op jit(solution)/shard_map/ppermute | solution.py:516
  760.3 6.6 collective-permute-done.24
  771.8 11.8 %collective-permute-done.23 = bf16[4,96,896]{2,1,0:T(8,128)(2,1)S(1)} collective-permute-done((bf16[4,96,896]{2,1,0:T(8,128)(2,1)S(1)}, bf16[4,96,896]{2,1,0:T(8,128)(2,1)S(1)}, u32[]{:S(2)}, u32[]{:S(2)}) %collective-permute-start.23) | collective-permute-done | bytes 688160 | tf_op jit(solution)/shard_map/ppermute | solution.py:516
  789.4 10.9 %collective-permute-start.28 = (bf16[96,1920]{1,0:T(8,128)(2,1)}, bf16[96,1920]{1,0:T(8,128)(2,1)}, u32[]{:S(2)}, u32[]{:S(2)}) collective-permute-start(bf16[96,1920]{1,0:T(8,128)(2,1)} %pad_maximum_fusion.18), channel_id=1, source_target_pairs={{0,24},{2,26},{4,28},{6,30},{8,0},{10,2},{12,4},{14,6},{16,8},{18,... | collective-permute-start | bytes 1105928 | tf_op jit(solution)/shard_map/ppermute | solution.py:487
  802.6 21.3 %all-to-all-done.4.refs_0_ = bf16[32,96,768]{2,1,0:T(8,128)(2,1)} async-done(((bf16[32,96,768]{2,1,0:T(8,128)(2,1)}), bf16[32,96,768]{2,1,0:T(8,128)(2,1)}, u32[]{:S(2)}, u32[]{:S(2)}) %all-to-all-start.4) | async-done | bytes 4718624 | tf_op jit(solution)/shard_map/all_to_all | solution.py:477
  829.8 7.4 slice_convert_fusion
  (521 shorter events, 304.4 us)
Async XLA Ops:
  11.5 14.7 %collective-permute-start.1 = (bf16[96,1920]{1,0:T(8,128)(2,1)S(1)}, bf16[96,1920]{1,0:T(8,128)(2,1)S(1)}, u32[]{:S(2)}, u32[]{:S(2)}) collective-permute-start(bf16[96,1920]{1,0:T(8,128)(2,1)S(1)} %concatenate.125), channel_id=1, source_target_pairs={{0,8},{2,10},{4,12},{6,14},{8,16},{10,18},{12,20},{14,22},{16,24},... | collective-permute-start | bytes 1105928 | tf_op jit(solution)/shard_map/ppermute | solution.py:487
  14.6 26.5 %collective-permute-start.2 = (bf16[96,1920]{1,0:T(8,128)(2,1)S(1)}, bf16[96,1920]{1,0:T(8,128)(2,1)S(1)}, u32[]{:S(2)}, u32[]{:S(2)}) collective-permute-start(bf16[96,1920]{1,0:T(8,128)(2,1)S(1)} %concatenate.125), channel_id=1, source_target_pairs={{0,16},{2,18},{4,20},{6,22},{8,24},{10,26},{12,28},{14,30},{16,0},... | collective-permute-start | bytes 1105928 | tf_op jit(solution)/shard_map/ppermute | solution.py:487
  17.2 24.0 %collective-permute-start.3 = (bf16[96,1920]{1,0:T(8,128)(2,1)S(1)}, bf16[96,1920]{1,0:T(8,128)(2,1)S(1)}, u32[]{:S(2)}, u32[]{:S(2)}) collective-permute-start(bf16[96,1920]{1,0:T(8,128)(2,1)S(1)} %concatenate.125), channel_id=1, source_target_pairs={{0,24},{2,26},{4,28},{6,30},{8,0},{10,2},{12,4},{14,6},{16,8},{18,... | collective-permute-start | bytes 1105928 | tf_op jit(solution)/shard_map/ppermute | solution.py:487
  18.5 48.8 %collective-permute-start = (bf16[256,1536]{1,0:T(8,128)(2,1)}, bf16[256,1536]{1,0:T(8,128)(2,1)}, u32[]{:S(2)}, u32[]{:S(2)}) collective-permute-start(bf16[256,1536]{1,0:T(8,128)(2,1)} %param.14), channel_id=1, source_target_pairs={{0,1},{1,0},{2,3},{3,2},{4,5},{5,4},{6,7},{7,6},{8,9},{9,8},{10,11... | collective-permute-start | bytes 2359304 | tf_op jit(solution)/shard_map/ppermute | solution.py:456
  41.4 39.2 %collective-permute-start.4 = (bf16[4,96,1920]{2,1,0:T(8,128)(2,1)S(1)}, bf16[4,96,1920]{2,1,0:T(8,128)(2,1)}, u32[]{:S(2)}, u32[]{:S(2)}) collective-permute-start(bf16[4,96,1920]{2,1,0:T(8,128)(2,1)S(1)} %pad_maximum_fusion.5.refs_1_), channel_id=1, source_target_pairs={{0,2},{2,0},{4,6},{6,4},{8,10},{10,8},{12,14},{14,12},{16,18},{18,... | collective-permute-start | bytes 4423688 | tf_op jit(solution)/shard_map/ppermute | solution.py:500
  42.9 82.7 %collective-permute-start.5 = (bf16[4,96,1920]{2,1,0:T(8,128)(2,1)S(1)}, bf16[4,96,1920]{2,1,0:T(8,128)(2,1)}, u32[]{:S(2)}, u32[]{:S(2)}) collective-permute-start(bf16[4,96,1920]{2,1,0:T(8,128)(2,1)S(1)} %pad_maximum_fusion.5.refs_1_), channel_id=1, source_target_pairs={{0,4},{2,6},{4,0},{6,2},{8,12},{10,14},{12,8},{14,10},{16,20},{18,... | collective-permute-start | bytes 4423688 | tf_op jit(solution)/shard_map/ppermute | solution.py:500
  44.5 86.6 %collective-permute-start.6 = (bf16[4,96,1920]{2,1,0:T(8,128)(2,1)S(1)}, bf16[4,96,1920]{2,1,0:T(8,128)(2,1)}, u32[]{:S(2)}, u32[]{:S(2)}) collective-permute-start(bf16[4,96,1920]{2,1,0:T(8,128)(2,1)S(1)} %pad_maximum_fusion.5.refs_1_), channel_id=1, source_target_pairs={{0,6},{2,4},{4,2},{6,0},{8,14},{10,12},{12,10},{14,8},{16,22},{18,... | collective-permute-start | bytes 4423688 | tf_op jit(solution)/shard_map/ppermute | solution.py:500
  51.4 217.8 %all-to-all-start = ((bf16[32,96,1152]{2,1,0:T(8,128)(2,1)}), bf16[32,96,1152]{2,1,0:T(8,128)(2,1)}, u32[]{:S(2)}, u32[]{:S(2)}) async-start(bf16[32,96,1152]{2,1,0:T(8,128)(2,1)} %after.14), calls=%async_computation | async-start | bytes 14155776 | tf_op jit(solution)/shard_map/all_to_all | solution.py:477
  63.2 144.3 %all-gather.5.cloned.1.call-start = ((), (), s32[]{:S(2)}) async-start(), calls=%async_computation.9 | async-start | bytes 3932160 | tf_op jit(solution)/shard_map/all_gather | solution.py:532
  64.0 268.0 %all-gather.7.cloned.1.call-start = ((), (), s32[]{:S(2)}) async-start(), calls=%async_computation.10 | async-start | bytes 3932160 | tf_op jit(solution)/shard_map/all_gather | solution.py:532
  269.3 63.7 %all-to-all-start.1 = ((bf16[8,4,48,1664]{3,2,1,0:T(8,128)(2,1)}), bf16[8,4,48,1664]{3,2,1,0:T(8,128)(2,1)}, u32[]{:S(2)}, u32[]{:S(2)}) async-start(bf16[8,4,48,1664]{3,2,1,0:T(8,128)(2,1)} %bitcast.230), calls=%async_computation.1 | async-start | bytes 10223616 | tf_op jit(solution)/shard_map/all_to_all | solution.py:555
  353.9 28.9 %collective-permute-start.12 = (bf16[2,4,48,1536]{3,2,1,0:T(8,128)(2,1)S(1)}, bf16[2,4,48,1536]{3,2,1,0:T(8,128)(2,1)S(1)}, u32[]{:S(2)}, u32[]{:S(2)}) collective-permute-start(bf16[2,4,48,1536]{3,2,1,0:T(8,128)(2,1)S(1)} %pad_maximum_fusion.7), channel_id=1, source_target_pairs={{0,2},{2,0},{4,6},{6,4},{8,10},{10,8},{12,14},{14,12},{16,18},{18,... | collective-permute-start | bytes 3538952 | tf_op jit(solution)/shard_map/ppermute | solution.py:543
  355.6 75.7 %collective-permute-start.11 = (bf16[2,4,48,1536]{3,2,1,0:T(8,128)(2,1)S(1)}, bf16[2,4,48,1536]{3,2,1,0:T(8,128)(2,1)S(1)}, u32[]{:S(2)}, u32[]{:S(2)}) collective-permute-start(bf16[2,4,48,1536]{3,2,1,0:T(8,128)(2,1)S(1)} %pad_maximum_fusion.6), channel_id=1, source_target_pairs={{0,6},{2,4},{4,2},{6,0},{8,14},{10,12},{12,10},{14,8},{16,22},{18,... | collective-permute-start | bytes 3538952 | tf_op jit(solution)/shard_map/ppermute | solution.py:543
  357.2 52.8 %collective-permute-start.14 = (bf16[2,4,48,1536]{3,2,1,0:T(8,128)(2,1)S(1)}, bf16[2,4,48,1536]{3,2,1,0:T(8,128)(2,1)S(1)}, u32[]{:S(2)}, u32[]{:S(2)}) collective-permute-start(bf16[2,4,48,1536]{3,2,1,0:T(8,128)(2,1)S(1)} %pad_maximum_fusion.9), channel_id=1, source_target_pairs={{0,4},{2,6},{4,0},{6,2},{8,12},{10,14},{12,8},{14,10},{16,20},{18,... | collective-permute-start | bytes 3538952 | tf_op jit(solution)/shard_map/ppermute | solution.py:543
  400.0 32.6 %collective-permute-start.13 = (bf16[384,1536]{1,0:T(8,128)(2,1)S(1)}, bf16[384,1536]{1,0:T(8,128)(2,1)S(1)}, u32[]{:S(2)}, u32[]{:S(2)}) collective-permute-start(bf16[384,1536]{1,0:T(8,128)(2,1)S(1)} %get-tuple-element.45), channel_id=1, source_target_pairs={{0,2},{2,0},{4,6},{6,4},{8,10},{10,8},{12,14},{14,12},{16,18},{18,... | collective-permute-start | bytes 3538952 | tf_op jit(solution)/shard_map/ppermute | solution.py:543
  430.7 29.9 %collective-permute-start.15 = (bf16[384,1536]{1,0:T(8,128)(2,1)}, bf16[384,1536]{1,0:T(8,128)(2,1)}, u32[]{:S(2)}, u32[]{:S(2)}) collective-permute-start(bf16[384,1536]{1,0:T(8,128)(2,1)} %get-tuple-element.53), channel_id=1, source_target_pairs={{0,4},{2,6},{4,0},{6,2},{8,12},{10,14},{12,8},{14,10},{16,20},{18,... | collective-permute-start | bytes 3538952 | tf_op jit(solution)/shard_map/ppermute | solution.py:543
  458.3 28.2 %collective-permute-start.16 = (bf16[384,1536]{1,0:T(8,128)(2,1)S(1)}, bf16[384,1536]{1,0:T(8,128)(2,1)}, u32[]{:S(2)}, u32[]{:S(2)}) collective-permute-start(bf16[384,1536]{1,0:T(8,128)(2,1)S(1)} %get-tuple-element.58), channel_id=1, source_target_pairs={{0,6},{2,4},{4,2},{6,0},{8,14},{10,12},{12,10},{14,8},{16,22},{18,... | collective-permute-start | bytes 3538952 | tf_op jit(solution)/shard_map/ppermute | solution.py:543
  486.5 58.1 %all-to-all-start.2 = ((bf16[32,96,384]{2,1,0:T(8,128)(2,1)}), bf16[32,96,384]{2,1,0:T(8,128)(2,1)}, u32[]{:S(2)}, u32[]{:S(2)}) async-start(bf16[32,96,384]{2,1,0:T(8,128)(2,1)} %after.21), calls=%async_computation.2 | async-start | bytes 4718592 | tf_op jit(solution)/shard_map/all_to_all | solution.py:477
  556.3 6.0 collective-permute-start.18
  556.5 59.4 %all-to-all-start.3 = ((bf16[8,4,48,1536]{3,2,1,0:T(8,128)(2,1)}), bf16[8,4,48,1536]{3,2,1,0:T(8,128)(2,1)}, u32[]{:S(2)}, u32[]{:S(2)}) async-start(bf16[8,4,48,1536]{3,2,1,0:T(8,128)(2,1)} %after.22), calls=%async_computation.3 | async-start | bytes 9437184 | tf_op jit(solution)/shard_map/all_to_all | solution.py:555
  561.1 74.8 %reduce-scatter.5.cloned.1.call-start = ((), (), s32[]{:S(2)}) async-start(), calls=%async_computation.8 | async-start | bytes 3932160 | tf_op jit(solution)/shard_map/reduce_scatter | solution.py:537
  643.3 10.7 %collective-permute-start.20 = (bf16[256,1536]{1,0:T(8,128)(2,1)}, bf16[256,1536]{1,0:T(8,128)(2,1)}, u32[]{:S(2)}, u32[]{:S(2)}) collective-permute-start(bf16[256,1536]{1,0:T(8,128)(2,1)} %fusion.145), channel_id=1, source_target_pairs={{0,1},{1,0},{2,3},{3,2},{4,5},{5,4},{6,7},{7,6},{8,9},{9,8},{10,11... | collective-permute-start | bytes 2359304 | tf_op jit(solution)/shard_map/ppermute | solution.py:456
  648.5 175.3 %all-to-all-start.4 = ((bf16[32,96,768]{2,1,0:T(8,128)(2,1)}), bf16[32,96,768]{2,1,0:T(8,128)(2,1)}, u32[]{:S(2)}, u32[]{:S(2)}) async-start(bf16[32,96,768]{2,1,0:T(8,128)(2,1)} %after.26), calls=%async_computation.6 | async-start | bytes 9437184 | tf_op jit(solution)/shard_map/all_to_all | solution.py:477
  652.1 172.8 %reduce-scatter.3.cloned.1.call-start = ((), (), s32[]{:S(2)}) async-start(), calls=%async_computation.7 | async-start | bytes 3932160 | tf_op jit(solution)/shard_map/reduce_scatter | solution.py:537
  710.6 44.3 %collective-permute-start.22 = (bf16[4,2,96,896]{3,2,0,1:T(8,128)(2,1)}, bf16[4,2,96,896]{3,2,0,1:T(8,128)(2,1)}, u32[]{:S(2)}, u32[]{:S(2)}) collective-permute-start(bf16[4,2,96,896]{3,2,0,1:T(8,128)(2,1)} %fusion.33), channel_id=1, source_target_pairs={{0,2},{2,0},{4,6},{6,4},{8,10},{10,8},{12,14},{14,12},{16,18},{18,... | collective-permute-start | bytes 4128776 | tf_op jit(solution)/shard_map/ppermute | solution.py:516
  716.8 50.1 %collective-permute-start.24 = (bf16[4,2,96,1024]{3,2,0,1:T(8,128)(2,1)}, bf16[4,2,96,1024]{3,2,0,1:T(8,128)(2,1)}, u32[]{:S(2)}, u32[]{:S(2)}) collective-permute-start(bf16[4,2,96,1024]{3,2,0,1:T(8,128)(2,1)} %fusion.24), channel_id=1, source_target_pairs={{0,4},{2,6},{4,0},{6,2},{8,12},{10,14},{12,8},{14,10},{16,20},{18,... | collective-permute-start | bytes 4718600 | tf_op jit(solution)/shard_map/ppermute | solution.py:516
  720.8 48.4 %collective-permute-start.21 = (f32[256,1536]{1,0:T(8,128)}, f32[256,1536]{1,0:T(8,128)}, u32[]{:S(2)}, u32[]{:S(2)}) collective-permute-start(f32[256,1536]{1,0:T(8,128)} %slice.307), channel_id=1, source_target_pairs={{0,1},{1,0},{2,3},{3,2},{4,5},{5,4},{6,7},{7,6},{8,9},{9,8},{10,11... | collective-permute-start | bytes 4718600 | tf_op jit(solution)/shard_map/ppermute | solution.py:456
  757.5 26.1 %collective-permute-start.23 = (bf16[4,96,896]{2,1,0:T(8,128)(2,1)S(1)}, bf16[4,96,896]{2,1,0:T(8,128)(2,1)S(1)}, u32[]{:S(2)}, u32[]{:S(2)}) collective-permute-start(bf16[4,96,896]{2,1,0:T(8,128)(2,1)S(1)} %fusion.55), channel_id=1, source_target_pairs={{0,4},{2,6},{4,0},{6,2},{8,12},{10,14},{12,8},{14,10},{16,20},{18,... | collective-permute-start | bytes 2064392 | tf_op jit(solution)/shard_map/ppermute | solution.py:516
  769.2 18.0 %collective-permute-start.25 = (bf16[4,96,1024]{2,1,0:T(8,128)(2,1)S(1)}, bf16[4,96,1024]{2,1,0:T(8,128)(2,1)S(1)}, u32[]{:S(2)}, u32[]{:S(2)}) collective-permute-start(bf16[4,96,1024]{2,1,0:T(8,128)(2,1)S(1)} %fusion.52), channel_id=1, source_target_pairs={{0,2},{2,0},{4,6},{6,4},{8,10},{10,8},{12,14},{14,12},{16,18},{18,... | collective-permute-start | bytes 2359304 | tf_op jit(solution)/shard_map/ppermute | solution.py:516
  789.4 47.8 %collective-permute-start.28 = (bf16[96,1920]{1,0:T(8,128)(2,1)}, bf16[96,1920]{1,0:T(8,128)(2,1)}, u32[]{:S(2)}, u32[]{:S(2)}) collective-permute-start(bf16[96,1920]{1,0:T(8,128)(2,1)} %pad_maximum_fusion.18), channel_id=1, source_target_pairs={{0,24},{2,26},{4,28},{6,30},{8,0},{10,2},{12,4},{14,6},{16,8},{18,... | collective-permute-start | bytes 1105928 | tf_op jit(solution)/shard_map/ppermute | solution.py:487
  801.1 38.1 %collective-permute-start.27 = (bf16[96,1920]{1,0:T(8,128)(2,1)}, bf16[96,1920]{1,0:T(8,128)(2,1)}, u32[]{:S(2)}, u32[]{:S(2)}) collective-permute-start(bf16[96,1920]{1,0:T(8,128)(2,1)} %pad_maximum_fusion.17), channel_id=1, source_target_pairs={{0,16},{2,18},{4,20},{6,22},{8,24},{10,26},{12,28},{14,30},{16,0},... | collective-permute-start | bytes 1105928 | tf_op jit(solution)/shard_map/ppermute | solution.py:487
  801.9 37.3 %collective-permute-start.26 = (bf16[96,1920]{1,0:T(8,128)(2,1)}, bf16[96,1920]{1,0:T(8,128)(2,1)}, u32[]{:S(2)}, u32[]{:S(2)}) collective-permute-start(bf16[96,1920]{1,0:T(8,128)(2,1)} %pad_maximum_fusion.16), channel_id=1, source_target_pairs={{0,8},{2,10},{4,12},{6,14},{8,16},{10,18},{12,20},{14,22},{16,24},... | collective-permute-start | bytes 1105928 | tf_op jit(solution)/shard_map/ppermute | solution.py:487
  (131 other events, 1069.2 us)
Sparse Core Ops, SparseCore 0:
  66.2 141.2 all-gather.4
  269.4 62.4 all-gather.6
  567.9 59.5 reduce-scatter.4
  654.9 109.4 reduce-scatter.2

commit v5 on v4

--- a/solution.py
+++ b/solution.py
@@ -941,13 +941,13 @@
     back = [b.reshape(shape) for b in back]
     grad_expert[3] = after(grad_expert[3], back[2])
     down_home = exchange(after(shard_grad(grad_expert, activation, rows), back[3]))
-    far = swap_cores(after(jnp.stack([b[1] for b in back]), down_home))
+    router_grad = sum(
+        lax.dot_general(g, p, tn, preferred_element_type=f32) for g, p in zip(grad_logits, pieces)
+    )
+    router_grad = router_grad[:E].T
+    far = swap_cores(after(jnp.stack([b[1] for b in back]), down_home, router_grad))
     grad_parts = combine(slot_near, jnp.stack([b[0] for b in back]), far)
     grad_normed = line_reduce(grad_parts).astype(f32)
-    router_grad = sum(
-        lax.dot_general(g, p, tn, preferred_element_type=f32) for g, p in zip(grad_logits, pieces)
-    )
-    router_grad = router_grad[:E].T
     mixture = mixture.reshape(mates, LINE, share, MODEL_WIDTH)
     mixture = plane_all(after(mixture, down_home))
     mixture_there = after(mixture, grad_parts)
@@ -1004,7 +1004,7 @@
     output_own, qkv_own = owned[:, :head_cols], owned[:, head_cols + 128 :]
     small_own = owned[:, head_cols : head_cols + 128]
     small_own = small_own + swap_cores(small_own)
-    gate_up_home = after(gate_up_home, *marks)
+    gate_up_home = after(gate_up_home, *marks, block_out, input_grad)
     return (
         block_out,
         input_grad,

time: 860 us -> 845 us (0.983)
  waiting for transfers between devices: 406 us -> 395 us
    all_gather x2, waiting for transfers between devices: 81 us -> 58 us  [line_gather(): lax.all_gather(block, 'row', axis=0, tiled=False, axis_index_groups=LINES)]
    unnamed x274 -> x266, local copies, waits for them, and re-layouts: 84.1 us -> 81.6 us
  transfers between devices with their start and end apart: 39 -> 39, of which waited for: 29 -> 29; matrix products, arithmetic and copies ran while one was open for 23% -> 24% of each run, Pallas kernels for 10% -> 10%
where the time goes in v5:
time: 845 us; the launch traced here: 831 us
  waiting for transfers between devices  395 us (47%)
  local copies, waits for them, and re-layouts  138 us (16%)
  Pallas kernels  94 us (11%)
  other arithmetic  77.6 us (9%)
  starting transfers between devices  57.6 us (7%)
  matrix products  52.3 us (6%)
  between operations  16.7 us (2%)
    all_to_all x3, waiting for transfers between devices, exchange(): return lax.all_to_all(block, GRID, split_axis=0, concat_axis=0, tiled=True)  128 us
    unnamed x266, local copies, waits for them, and re-layouts  81.6 us
    all_gather x2, waiting for transfers between devices, line_gather(): lax.all_gather(block, 'row', axis=0, tiled=False, axis_index_groups=LINES)  58 us
    ppermute x4, waiting for transfers between devices, row_reduce(): away = lax.ppermute(away.astype(jnp.bfloat16), 'row', plane_pairs(flip))  57.7 us
    ppermute x3, waiting for transfers between devices, row_gather(): lax.ppermute(line, 'row', plane_pairs(flip))  55.9 us
    pallas_call x4, Pallas kernels, expert_rows(): pl.pallas_call(expert_body, grid_spec=pltpu.PrefetchScalarGridSpec(num_sc...  54.9 us
    all_to_all x2, waiting for transfers between devices, plane_all(): lax.all_to_all(block, GRID, split_axis=0, concat_axis=0, tiled=True, axis...  30.4 us
    ppermute x6, waiting for transfers between devices, plane_move(): return lax.ppermute(block, 'row', plane_pairs(move))  28.2 us
  transfers between devices with their start and end apart: 39, of which 29 were waited for; matrix products, arithmetic and copies ran while one was open for 24% of the time, Pallas kernels for 10%

profile of v5, /device:TPU:0, one launch (start us, length us, event | category | flops | bytes accessed | tf_op | source)
XLA Modules:
  0.0 830.9 jit_solution(12786049942290480186)
XLA Ops:
  26.2 15.0 %collective-permute-done.2 = bf16[96,1920]{1,0:T(8,128)(2,1)S(1)} collective-permute-done((bf16[96,1920]{1,0:T(8,128)(2,1)S(1)}, bf16[96,1920]{1,0:T(8,128)(2,1)S(1)}, u32[]{:S(2)}, u32[]{:S(2)}) %collective-permute-start.2) | collective-permute-done | bytes 368672 | tf_op jit(solution)/shard_map/ppermute | solution.py:487
  52.0 11.8 %all-to-all-start = ((bf16[32,96,1152]{2,1,0:T(8,128)(2,1)}), bf16[32,96,1152]{2,1,0:T(8,128)(2,1)}, u32[]{:S(2)}, u32[]{:S(2)}) async-start(bf16[32,96,1152]{2,1,0:T(8,128)(2,1)} %after.14), calls=%async_computation | async-start | bytes 14155776 | tf_op jit(solution)/shard_map/all_to_all | solution.py:477
  68.7 8.6 %collective-permute-done.4 = bf16[4,96,1920]{2,1,0:T(8,128)(2,1)} collective-permute-done((bf16[4,96,1920]{2,1,0:T(8,128)(2,1)S(1)}, bf16[4,96,1920]{2,1,0:T(8,128)(2,1)}, u32[]{:S(2)}, u32[]{:S(2)}) %collective-permute-start.4) | collective-permute-done | bytes 1474592 | tf_op jit(solution)/shard_map/ppermute | solution.py:500
  80.0 34.9 %collective-permute-done.5 = bf16[4,96,1920]{2,1,0:T(8,128)(2,1)} collective-permute-done((bf16[4,96,1920]{2,1,0:T(8,128)(2,1)S(1)}, bf16[4,96,1920]{2,1,0:T(8,128)(2,1)}, u32[]{:S(2)}, u32[]{:S(2)}) %collective-permute-start.5) | collective-permute-done | bytes 1474592 | tf_op jit(solution)/shard_map/ppermute | solution.py:500
  117.6 12.3 %collective-permute-done.6 = bf16[4,96,1920]{2,1,0:T(8,128)(2,1)} collective-permute-done((bf16[4,96,1920]{2,1,0:T(8,128)(2,1)S(1)}, bf16[4,96,1920]{2,1,0:T(8,128)(2,1)}, u32[]{:S(2)}, u32[]{:S(2)}) %collective-permute-start.6) | collective-permute-done | bytes 1474592 | tf_op jit(solution)/shard_map/ppermute | solution.py:500
  195.8 71.4 %all-to-all-done.refs_1_ = bf16[32,96,1152]{2,1,0:T(8,128)(2,1)} async-done(((bf16[32,96,1152]{2,1,0:T(8,128)(2,1)}), bf16[32,96,1152]{2,1,0:T(8,128)(2,1)}, u32[]{:S(2)}, u32[]{:S(2)}) %all-to-all-start) | async-done | bytes 7077920 | tf_op jit(solution)/shard_map/all_to_all | solution.py:477
  272.0 57.4 %all-gather.7.cloned.1.call-done = bf16[1024,1536]{1,0:T(8,128)(2,1)} async-done(((bf16[256,1536]{1,0:T(8,128)(2,1)}), bf16[1024,1536]{1,0:T(8,128)(2,1)}) %all-gather.7.cloned.1.call-update) | async-done | bytes 3145744 | tf_op jit(solution)/shard_map/all_gather | solution.py:532
  353.6 13.2 %expert_rows.4 = (bf16[384,1536]{1,0:T(8,128)(2,1)S(1)}, bf16[4,2,192,1536]{3,2,1,0:T(8,128)(2,1)S(1)}, bf16[384,1536]{1,0:T(8,128)(2,1)S(1)}, bf16[384,768]{1,0...) custom-call(s32[3]{0:T(128)S(1)} %pad_add_fusion.4.where_ref, ...), custom_call_target="tpu_custom_call" | custom-call | flops 5435817984 | bytes 7667712 | tf_op jit(solution)/shard_map/expert_rows/pallas_call | solution.py:645
  368.6 9.8 %collective-permute-done.12 = bf16[2,4,48,1536]{3,2,1,0:T(8,128)(2,1)S(1)} collective-permute-done((bf16[2,4,48,1536]{3,2,1,0:T(8,128)(2,1)S(1)}, bf16[2,4,48,1536]{3,2,1,0:T(8,128)(2,1)S(1)}, u32[]{:S(2)}, u32[]{:S(2)}) %collective-permute-start.12) | collective-permute-done | bytes 1179680 | tf_op jit(solution)/shard_map/ppermute | solution.py:543
  378.4 13.6 %expert_rows.5 = (bf16[384,1536]{1,0:T(8,128)(2,1)S(1)}, bf16[4,2,192,1536]{3,2,1,0:T(8,128)(2,1)S(1)}, bf16[384,1536]{1,0:T(8,128)(2,1)S(1)}, bf16[384,768]{1,0...) custom-call(s32[3]{0:T(128)S(1)} %pad_add_fusion.4.where_ref, ...), custom_call_target="tpu_custom_call", output_to_operand_aliasing={{1}: (5, {})} | custom-call | flops 5435817984 | bytes 7667712 | tf_op jit(solution)/shard_map/expert_rows/pallas_call | solution.py:645
  397.1 6.8 collective-permute-done.14
  403.9 14.4 %expert_rows.6 = (bf16[384,1536]{1,0:T(8,128)(2,1)}, bf16[4,2,192,1536]{3,2,1,0:T(8,128)(2,1)S(1)}, bf16[384,1536]{1,0:T(8,128)(2,1)S(1)}, bf16[384,768]{1,0:T(8...) custom-call(s32[3]{0:T(128)S(1)} %pad_add_fusion.4.where_ref, ...), custom_call_target="tpu_custom_call", output_to_operand_aliasing={{1}: (5, {})} | custom-call | flops 5435817984 | bytes 7667712 | tf_op jit(solution)/shard_map/expert_rows/pallas_call | solution.py:645
  433.8 13.6 %expert_rows.7 = (bf16[384,1536]{1,0:T(8,128)(2,1)S(1)}, bf16[4,2,192,1536]{3,2,1,0:T(8,128)(2,1)S(1)}, bf16[384,1536]{1,0:T(8,128)(2,1)S(1)}, bf16[384,768]{1,0...) custom-call(s32[3]{0:T(128)S(1)} %pad_add_fusion.4.where_ref, ...), custom_call_target="tpu_custom_call", output_to_operand_aliasing={{1}: (5, {})} | custom-call | flops 5435817984 | bytes 7667712 | tf_op jit(solution)/shard_map/expert_rows/pallas_call | solution.py:645
  464.4 7.8 shard_grad.2
  472.2 10.0 %collective-permute-done.16 = bf16[384,1536]{1,0:T(8,128)(2,1)} collective-permute-done((bf16[384,1536]{1,0:T(8,128)(2,1)S(1)}, bf16[384,1536]{1,0:T(8,128)(2,1)}, u32[]{:S(2)}, u32[]{:S(2)}) %collective-permute-start.16) | collective-permute-done | bytes 1179680 | tf_op jit(solution)/shard_map/ppermute | solution.py:543
  494.9 45.6 %all-to-all-done.2.refs_1_ = bf16[32,96,384]{2,1,0:T(8,128)(2,1)} async-done(((bf16[32,96,384]{2,1,0:T(8,128)(2,1)}), bf16[32,96,384]{2,1,0:T(8,128)(2,1)}, u32[]{:S(2)}, u32[]{:S(2)}) %all-to-all-start.2) | async-done | bytes 2359328 | tf_op jit(solution)/shard_map/all_to_all | solution.py:477
  545.3 5.3 combine_rows.2
  558.2 5.4 add_convert_fusion.1.refs_1_
  569.6 12.9 %shard_grad.3 = bf16[16,2,96,768]{3,2,1,0:T(8,128)(2,1)} custom-call(bf16[384,1536]{1,0:T(8,128)(2,1)S(1)} %bitcast.238, bf16[384,1536]{1,0:T(8,128)(2,1)} %bitcast.240, bf16[384,1536]{1,0:T(8,128)(2,1)} %bitcast.243, bf16[384,1536]{1,0:T(8,128)(2,1)} %after.19.x_ref.refs_3_, bf16[384,768]{1,0:T(8,128)(2,1)S(1)} %copy-done.57, ...), custom_call_target="tpu_custom_call" | custom-call | flops 7247757312 | bytes 14155776 | tf_op jit(solution)/shard_map/shard_grad/pallas_call | solution.py:779
  582.5 29.2 %all-to-all-done.3.refs_0_.refs_1_ = bf16[8,4,48,1536]{3,2,1,0:T(8,128)(2,1)} async-done(((bf16[8,4,48,1536]{3,2,1,0:T(8,128)(2,1)}), bf16[8,4,48,1536]{3,2,1,0:T(8,128)(2,1)}, u32[]{:S(2)}, u32[]{:S(2)}) %all-to-all-start.3) | async-done | bytes 4718624 | tf_op jit(solution)/shard_map/all_to_all | solution.py:555
  612.6 5.6 combine_rows.3
  618.3 5.6 collective-permute-done.19
  648.3 6.2 multiply_reduce_fusion
  674.0 5.3 fusion.39
  680.8 6.5 fusion.5
  688.5 5.2 fusion.27
  694.7 8.5 %concatenate.154 = f32[4,2,2,96,896]{4,3,0,1,2:T(8,128)} concatenate(f32[4,2,2,96,768]{4,3,0,1,2:T(8,128)} %fusion.27, f32[4,2,2,96,32]{4,3,0,1,2:T(8,128)} %copy.142, f32[4,2,2,96,1]{4,3,0,1,2:T(8,128)} %copy.143, f32[4,2,2,96,1]{4,3,0,1,2:T(8,128)} %copy.144, f32[4,2,2,96,94]{4,3,0,1,2:T(8,128)} %broadcast_in_dim.47), dimensions={4} | concatenate | bytes 11010048 | tf_op jit(solution)/shard_map/concatenate | solution.py:1002
  721.2 31.6 %collective-permute-done.22 = bf16[4,2,96,896]{3,2,0,1:T(8,128)(2,1)} collective-permute-done((bf16[4,2,96,896]{3,2,0,1:T(8,128)(2,1)}, bf16[4,2,96,896]{3,2,0,1:T(8,128)(2,1)}, u32[]{:S(2)}, u32[]{:S(2)}) %collective-permute-start.22) | collective-permute-done | bytes 1376288 | tf_op jit(solution)/shard_map/ppermute | solution.py:516
  755.4 5.9 collective-permute-done.24
  766.3 15.0 %collective-permute-done.23 = bf16[4,96,896]{2,1,0:T(8,128)(2,1)S(1)} collective-permute-done((bf16[4,96,896]{2,1,0:T(8,128)(2,1)S(1)}, bf16[4,96,896]{2,1,0:T(8,128)(2,1)S(1)}, u32[]{:S(2)}, u32[]{:S(2)}) %collective-permute-start.23) | collective-permute-done | bytes 688160 | tf_op jit(solution)/shard_map/ppermute | solution.py:516
  800.8 10.5 %all-to-all-done.4.refs_0_ = bf16[32,96,768]{2,1,0:T(8,128)(2,1)} async-done(((bf16[32,96,768]{2,1,0:T(8,128)(2,1)}), bf16[32,96,768]{2,1,0:T(8,128)(2,1)}, u32[]{:S(2)}, u32[]{:S(2)}) %all-to-all-start.4) | async-done | bytes 4718624 | tf_op jit(solution)/shard_map/all_to_all | solution.py:477
  811.3 7.4 slice_convert_fusion
  (512 shorter events, 301.7 us)
Async XLA Ops:
  7.2 176.5 %all-gather.5.cloned.1.call-start = ((), (), s32[]{:S(2)}) async-start(), calls=%async_computation.9 | async-start | bytes 3932160 | tf_op jit(solution)/shard_map/all_gather | solution.py:532
  11.5 14.7 %collective-permute-start.1 = (bf16[96,1920]{1,0:T(8,128)(2,1)S(1)}, bf16[96,1920]{1,0:T(8,128)(2,1)S(1)}, u32[]{:S(2)}, u32[]{:S(2)}) collective-permute-start(bf16[96,1920]{1,0:T(8,128)(2,1)S(1)} %concatenate.125), channel_id=1, source_target_pairs={{0,8},{2,10},{4,12},{6,14},{8,16},{10,18},{12,20},{14,22},{16,24},... | collective-permute-start | bytes 1105928 | tf_op jit(solution)/shard_map/ppermute | solution.py:487
  14.6 26.5 %collective-permute-start.2 = (bf16[96,1920]{1,0:T(8,128)(2,1)S(1)}, bf16[96,1920]{1,0:T(8,128)(2,1)S(1)}, u32[]{:S(2)}, u32[]{:S(2)}) collective-permute-start(bf16[96,1920]{1,0:T(8,128)(2,1)S(1)} %concatenate.125), channel_id=1, source_target_pairs={{0,16},{2,18},{4,20},{6,22},{8,24},{10,26},{12,28},{14,30},{16,0},... | collective-permute-start | bytes 1105928 | tf_op jit(solution)/shard_map/ppermute | solution.py:487
  17.2 24.0 %collective-permute-start.3 = (bf16[96,1920]{1,0:T(8,128)(2,1)S(1)}, bf16[96,1920]{1,0:T(8,128)(2,1)S(1)}, u32[]{:S(2)}, u32[]{:S(2)}) collective-permute-start(bf16[96,1920]{1,0:T(8,128)(2,1)S(1)} %concatenate.125), channel_id=1, source_target_pairs={{0,24},{2,26},{4,28},{6,30},{8,0},{10,2},{12,4},{14,6},{16,8},{18,... | collective-permute-start | bytes 1105928 | tf_op jit(solution)/shard_map/ppermute | solution.py:487
  18.5 48.6 %collective-permute-start = (bf16[256,1536]{1,0:T(8,128)(2,1)}, bf16[256,1536]{1,0:T(8,128)(2,1)}, u32[]{:S(2)}, u32[]{:S(2)}) collective-permute-start(bf16[256,1536]{1,0:T(8,128)(2,1)} %param.14), channel_id=1, source_target_pairs={{0,1},{1,0},{2,3},{3,2},{4,5},{5,4},{6,7},{7,6},{8,9},{9,8},{10,11... | collective-permute-start | bytes 2359304 | tf_op jit(solution)/shard_map/ppermute | solution.py:456
  41.4 35.9 %collective-permute-start.4 = (bf16[4,96,1920]{2,1,0:T(8,128)(2,1)S(1)}, bf16[4,96,1920]{2,1,0:T(8,128)(2,1)}, u32[]{:S(2)}, u32[]{:S(2)}) collective-permute-start(bf16[4,96,1920]{2,1,0:T(8,128)(2,1)S(1)} %pad_maximum_fusion.5.refs_1_), channel_id=1, source_target_pairs={{0,2},{2,0},{4,6},{6,4},{8,10},{10,8},{12,14},{14,12},{16,18},{18,... | collective-permute-start | bytes 4423688 | tf_op jit(solution)/shard_map/ppermute | solution.py:500
  43.0 72.0 %collective-permute-start.5 = (bf16[4,96,1920]{2,1,0:T(8,128)(2,1)S(1)}, bf16[4,96,1920]{2,1,0:T(8,128)(2,1)}, u32[]{:S(2)}, u32[]{:S(2)}) collective-permute-start(bf16[4,96,1920]{2,1,0:T(8,128)(2,1)S(1)} %pad_maximum_fusion.5.refs_1_), channel_id=1, source_target_pairs={{0,4},{2,6},{4,0},{6,2},{8,12},{10,14},{12,8},{14,10},{16,20},{18,... | collective-permute-start | bytes 4423688 | tf_op jit(solution)/shard_map/ppermute | solution.py:500
  44.5 85.4 %collective-permute-start.6 = (bf16[4,96,1920]{2,1,0:T(8,128)(2,1)S(1)}, bf16[4,96,1920]{2,1,0:T(8,128)(2,1)}, u32[]{:S(2)}, u32[]{:S(2)}) collective-permute-start(bf16[4,96,1920]{2,1,0:T(8,128)(2,1)S(1)} %pad_maximum_fusion.5.refs_1_), channel_id=1, source_target_pairs={{0,6},{2,4},{4,2},{6,0},{8,14},{10,12},{12,10},{14,8},{16,22},{18,... | collective-permute-start | bytes 4423688 | tf_op jit(solution)/shard_map/ppermute | solution.py:500
  52.0 215.2 %all-to-all-start = ((bf16[32,96,1152]{2,1,0:T(8,128)(2,1)}), bf16[32,96,1152]{2,1,0:T(8,128)(2,1)}, u32[]{:S(2)}, u32[]{:S(2)}) async-start(bf16[32,96,1152]{2,1,0:T(8,128)(2,1)} %after.14), calls=%async_computation | async-start | bytes 14155776 | tf_op jit(solution)/shard_map/all_to_all | solution.py:477
  63.8 265.6 %all-gather.7.cloned.1.call-start = ((), (), s32[]{:S(2)}) async-start(), calls=%async_computation.10 | async-start | bytes 3932160 | tf_op jit(solution)/shard_map/all_gather | solution.py:532
  267.3 63.6 %all-to-all-start.1 = ((bf16[8,4,48,1664]{3,2,1,0:T(8,128)(2,1)}), bf16[8,4,48,1664]{3,2,1,0:T(8,128)(2,1)}, u32[]{:S(2)}, u32[]{:S(2)}) async-start(bf16[8,4,48,1664]{3,2,1,0:T(8,128)(2,1)} %bitcast.229), calls=%async_computation.1 | async-start | bytes 10223616 | tf_op jit(solution)/shard_map/all_to_all | solution.py:555
  349.5 28.9 %collective-permute-start.12 = (bf16[2,4,48,1536]{3,2,1,0:T(8,128)(2,1)S(1)}, bf16[2,4,48,1536]{3,2,1,0:T(8,128)(2,1)S(1)}, u32[]{:S(2)}, u32[]{:S(2)}) collective-permute-start(bf16[2,4,48,1536]{3,2,1,0:T(8,128)(2,1)S(1)} %pad_maximum_fusion.7), channel_id=1, source_target_pairs={{0,2},{2,0},{4,6},{6,4},{8,10},{10,8},{12,14},{14,12},{16,18},{18,... | collective-permute-start | bytes 3538952 | tf_op jit(solution)/shard_map/ppermute | solution.py:543
  351.2 52.7 %collective-permute-start.14 = (bf16[2,4,48,1536]{3,2,1,0:T(8,128)(2,1)S(1)}, bf16[2,4,48,1536]{3,2,1,0:T(8,128)(2,1)S(1)}, u32[]{:S(2)}, u32[]{:S(2)}) collective-permute-start(bf16[2,4,48,1536]{3,2,1,0:T(8,128)(2,1)S(1)} %pad_maximum_fusion.9), channel_id=1, source_target_pairs={{0,4},{2,6},{4,0},{6,2},{8,12},{10,14},{12,8},{14,10},{16,20},{18,... | collective-permute-start | bytes 3538952 | tf_op jit(solution)/shard_map/ppermute | solution.py:543
  352.8 73.7 %collective-permute-start.11 = (bf16[2,4,48,1536]{3,2,1,0:T(8,128)(2,1)S(1)}, bf16[2,4,48,1536]{3,2,1,0:T(8,128)(2,1)S(1)}, u32[]{:S(2)}, u32[]{:S(2)}) collective-permute-start(bf16[2,4,48,1536]{3,2,1,0:T(8,128)(2,1)S(1)} %pad_maximum_fusion.6), channel_id=1, source_target_pairs={{0,6},{2,4},{4,2},{6,0},{8,14},{10,12},{12,10},{14,8},{16,22},{18,... | collective-permute-start | bytes 3538952 | tf_op jit(solution)/shard_map/ppermute | solution.py:543
  395.6 32.6 %collective-permute-start.13 = (bf16[384,1536]{1,0:T(8,128)(2,1)S(1)}, bf16[384,1536]{1,0:T(8,128)(2,1)S(1)}, u32[]{:S(2)}, u32[]{:S(2)}) collective-permute-start(bf16[384,1536]{1,0:T(8,128)(2,1)S(1)} %get-tuple-element.45), channel_id=1, source_target_pairs={{0,2},{2,0},{4,6},{6,4},{8,10},{10,8},{12,14},{14,12},{16,18},{18,... | collective-permute-start | bytes 3538952 | tf_op jit(solution)/shard_map/ppermute | solution.py:543
  424.6 31.7 %collective-permute-start.15 = (bf16[384,1536]{1,0:T(8,128)(2,1)}, bf16[384,1536]{1,0:T(8,128)(2,1)}, u32[]{:S(2)}, u32[]{:S(2)}) collective-permute-start(bf16[384,1536]{1,0:T(8,128)(2,1)} %get-tuple-element.53), channel_id=1, source_target_pairs={{0,4},{2,6},{4,0},{6,2},{8,12},{10,14},{12,8},{14,10},{16,20},{18,... | collective-permute-start | bytes 3538952 | tf_op jit(solution)/shard_map/ppermute | solution.py:543
  453.9 28.2 %collective-permute-start.16 = (bf16[384,1536]{1,0:T(8,128)(2,1)S(1)}, bf16[384,1536]{1,0:T(8,128)(2,1)}, u32[]{:S(2)}, u32[]{:S(2)}) collective-permute-start(bf16[384,1536]{1,0:T(8,128)(2,1)S(1)} %get-tuple-element.58), channel_id=1, source_target_pairs={{0,6},{2,4},{4,2},{6,0},{8,14},{10,12},{12,10},{14,8},{16,22},{18,... | collective-permute-start | bytes 3538952 | tf_op jit(solution)/shard_map/ppermute | solution.py:543
  482.1 58.4 %all-to-all-start.2 = ((bf16[32,96,384]{2,1,0:T(8,128)(2,1)}), bf16[32,96,384]{2,1,0:T(8,128)(2,1)}, u32[]{:S(2)}, u32[]{:S(2)}) async-start(bf16[32,96,384]{2,1,0:T(8,128)(2,1)} %after.21), calls=%async_computation.2 | async-start | bytes 4718592 | tf_op jit(solution)/shard_map/all_to_all | solution.py:477
  552.2 6.0 collective-permute-start.18
  552.4 59.4 %all-to-all-start.3 = ((bf16[8,4,48,1536]{3,2,1,0:T(8,128)(2,1)}), bf16[8,4,48,1536]{3,2,1,0:T(8,128)(2,1)}, u32[]{:S(2)}, u32[]{:S(2)}) async-start(bf16[8,4,48,1536]{3,2,1,0:T(8,128)(2,1)} %after.22), calls=%async_computation.3 | async-start | bytes 9437184 | tf_op jit(solution)/shard_map/all_to_all | solution.py:555
  557.0 69.5 %reduce-scatter.5.cloned.1.call-start = ((), (), s32[]{:S(2)}) async-start(), calls=%async_computation.8 | async-start | bytes 3932160 | tf_op jit(solution)/shard_map/reduce_scatter | solution.py:537
  633.8 7.8 collective-permute-start.20
  636.0 175.3 %all-to-all-start.4 = ((bf16[32,96,768]{2,1,0:T(8,128)(2,1)}), bf16[32,96,768]{2,1,0:T(8,128)(2,1)}, u32[]{:S(2)}, u32[]{:S(2)}) async-start(bf16[32,96,768]{2,1,0:T(8,128)(2,1)} %after.26), calls=%async_computation.6 | async-start | bytes 9437184 | tf_op jit(solution)/shard_map/all_to_all | solution.py:477
  639.6 156.3 %reduce-scatter.3.cloned.1.call-start = ((), (), s32[]{:S(2)}) async-start(), calls=%async_computation.7 | async-start | bytes 3932160 | tf_op jit(solution)/shard_map/reduce_scatter | solution.py:537
  706.4 46.4 %collective-permute-start.22 = (bf16[4,2,96,896]{3,2,0,1:T(8,128)(2,1)}, bf16[4,2,96,896]{3,2,0,1:T(8,128)(2,1)}, u32[]{:S(2)}, u32[]{:S(2)}) collective-permute-start(bf16[4,2,96,896]{3,2,0,1:T(8,128)(2,1)} %fusion.33), channel_id=1, source_target_pairs={{0,2},{2,0},{4,6},{6,4},{8,10},{10,8},{12,14},{14,12},{16,18},{18,... | collective-permute-start | bytes 4128776 | tf_op jit(solution)/shard_map/ppermute | solution.py:516
  712.6 48.8 %collective-permute-start.24 = (bf16[4,2,96,1024]{3,2,0,1:T(8,128)(2,1)}, bf16[4,2,96,1024]{3,2,0,1:T(8,128)(2,1)}, u32[]{:S(2)}, u32[]{:S(2)}) collective-permute-start(bf16[4,2,96,1024]{3,2,0,1:T(8,128)(2,1)} %fusion.24), channel_id=1, source_target_pairs={{0,4},{2,6},{4,0},{6,2},{8,12},{10,14},{12,8},{14,10},{16,20},{18,... | collective-permute-start | bytes 4718600 | tf_op jit(solution)/shard_map/ppermute | solution.py:516
  716.6 47.1 %collective-permute-start.21 = (f32[256,1536]{1,0:T(8,128)}, f32[256,1536]{1,0:T(8,128)}, u32[]{:S(2)}, u32[]{:S(2)}) collective-permute-start(f32[256,1536]{1,0:T(8,128)} %slice.311), channel_id=1, source_target_pairs={{0,1},{1,0},{2,3},{3,2},{4,5},{5,4},{6,7},{7,6},{8,9},{9,8},{10,11... | collective-permute-start | bytes 4718600 | tf_op jit(solution)/shard_map/ppermute | solution.py:456
  755.4 25.9 %collective-permute-start.23 = (bf16[4,96,896]{2,1,0:T(8,128)(2,1)S(1)}, bf16[4,96,896]{2,1,0:T(8,128)(2,1)S(1)}, u32[]{:S(2)}, u32[]{:S(2)}) collective-permute-start(bf16[4,96,896]{2,1,0:T(8,128)(2,1)S(1)} %fusion.55), channel_id=1, source_target_pairs={{0,4},{2,6},{4,0},{6,2},{8,12},{10,14},{12,8},{14,10},{16,20},{18,... | collective-permute-start | bytes 2064392 | tf_op jit(solution)/shard_map/ppermute | solution.py:516
  763.7 24.1 %collective-permute-start.25 = (bf16[4,96,1024]{2,1,0:T(8,128)(2,1)S(1)}, bf16[4,96,1024]{2,1,0:T(8,128)(2,1)S(1)}, u32[]{:S(2)}, u32[]{:S(2)}) collective-permute-start(bf16[4,96,1024]{2,1,0:T(8,128)(2,1)S(1)} %fusion.52), channel_id=1, source_target_pairs={{0,2},{2,0},{4,6},{6,4},{8,10},{10,8},{12,14},{14,12},{16,18},{18,... | collective-permute-start | bytes 2359304 | tf_op jit(solution)/shard_map/ppermute | solution.py:516
  789.0 29.7 %collective-permute-start.26 = (bf16[96,1920]{1,0:T(8,128)(2,1)}, bf16[96,1920]{1,0:T(8,128)(2,1)}, u32[]{:S(2)}, u32[]{:S(2)}) collective-permute-start(bf16[96,1920]{1,0:T(8,128)(2,1)} %pad_maximum_fusion.16), channel_id=1, source_target_pairs={{0,8},{2,10},{4,12},{6,14},{8,16},{10,18},{12,20},{14,22},{16,24},... | collective-permute-start | bytes 1105928 | tf_op jit(solution)/shard_map/ppermute | solution.py:487
  789.8 29.4 %collective-permute-start.27 = (bf16[96,1920]{1,0:T(8,128)(2,1)}, bf16[96,1920]{1,0:T(8,128)(2,1)}, u32[]{:S(2)}, u32[]{:S(2)}) collective-permute-start(bf16[96,1920]{1,0:T(8,128)(2,1)} %pad_maximum_fusion.17), channel_id=1, source_target_pairs={{0,16},{2,18},{4,20},{6,22},{8,24},{10,26},{12,28},{14,30},{16,0},... | collective-permute-start | bytes 1105928 | tf_op jit(solution)/shard_map/ppermute | solution.py:487
  795.4 23.9 %collective-permute-start.28 = (bf16[96,1920]{1,0:T(8,128)(2,1)}, bf16[96,1920]{1,0:T(8,128)(2,1)}, u32[]{:S(2)}, u32[]{:S(2)}) collective-permute-start(bf16[96,1920]{1,0:T(8,128)(2,1)} %pad_maximum_fusion.18), channel_id=1, source_target_pairs={{0,24},{2,26},{4,28},{6,30},{8,0},{10,2},{12,4},{14,6},{16,8},{18,... | collective-permute-start | bytes 1105928 | tf_op jit(solution)/shard_map/ppermute | solution.py:487
  (127 other events, 1151.3 us)
Sparse Core Ops, SparseCore 0:
  45.6 138.0 all-gather.4
  267.4 61.8 all-gather.6
  563.8 59.5 reduce-scatter.4
  642.5 109.4 reduce-scatter.2

commit v6 on v5

--- a/solution.py
+++ b/solution.py
@@ -940,7 +940,7 @@
     shape = (2, LINE, share, MODEL_WIDTH)
     back = [b.reshape(shape) for b in back]
     grad_expert[3] = after(grad_expert[3], back[2])
-    down_home = exchange(after(shard_grad(grad_expert, activation, rows), back[3]))
+    down_home = exchange(shard_grad(grad_expert, activation, rows))
     router_grad = sum(
         lax.dot_general(g, p, tn, preferred_element_type=f32) for g, p in zip(grad_logits, pieces)
     )

time: 845 us -> 839 us (level)
    all_to_all x3, waiting for transfers between devices: 128 us -> 82.2 us  [exchange(): return lax.all_to_all(block, GRID, split_axis=0, concat_axis=0, tiled=True)]
    ppermute x6, waiting for transfers between devices: 28.2 us -> 67.2 us  [plane_move(): return lax.ppermute(block, 'row', plane_pairs(move))]
    unnamed x266 -> x270, local copies, waits for them, and re-layouts: 81.6 us -> 82.3 us
  transfers between devices with their start and end apart: 39 -> 39, of which waited for: 29 -> 28; matrix products, arithmetic and copies ran while one was open for 24% -> 24% of each run, Pallas kernels for 10% -> 9%
where the time goes in v6:
time: 839 us; the launch traced here: 825 us
  waiting for transfers between devices  388 us (46%)
  local copies, waits for them, and re-layouts  137 us (16%)
  Pallas kernels  94.2 us (11%)
  other arithmetic  77.4 us (9%)
  starting transfers between devices  58.9 us (7%)
  matrix products  52.1 us (6%)
  between operations  16.7 us (2%)
    unnamed x270, local copies, waits for them, and re-layouts  82.3 us
    all_to_all x3, waiting for transfers between devices, exchange(): return lax.all_to_all(block, GRID, split_axis=0, concat_axis=0, tiled=True)  82.2 us
    ppermute x6, waiting for transfers between devices, plane_move(): return lax.ppermute(block, 'row', plane_pairs(move))  67.2 us
    all_gather x2, waiting for transfers between devices, line_gather(): lax.all_gather(block, 'row', axis=0, tiled=False, axis_index_groups=LINES)  58 us
    ppermute x4, waiting for transfers between devices, row_reduce(): away = lax.ppermute(away.astype(jnp.bfloat16), 'row', plane_pairs(flip))  57.8 us
    ppermute x3, waiting for transfers between devices, row_gather(): lax.ppermute(line, 'row', plane_pairs(flip))  55.9 us
    pallas_call x4, Pallas kernels, expert_rows(): pl.pallas_call(expert_body, grid_spec=pltpu.PrefetchScalarGridSpec(num_sc...  54.8 us
    all_to_all x2, waiting for transfers between devices, plane_all(): lax.all_to_all(block, GRID, split_axis=0, concat_axis=0, tiled=True, axis...  30.3 us
  transfers between devices with their start and end apart: 39, of which 28 were waited for; matrix products, arithmetic and copies ran while one was open for 24% of the time, Pallas kernels for 9%

profile of v6, /device:TPU:0, one launch (start us, length us, event | category | flops | bytes accessed | tf_op | source)
XLA Modules:
  0.0 825.0 jit_solution(3055731086362811586)
XLA Ops:
  26.2 15.0 %collective-permute-done.2 = bf16[96,1920]{1,0:T(8,128)(2,1)S(1)} collective-permute-done((bf16[96,1920]{1,0:T(8,128)(2,1)S(1)}, bf16[96,1920]{1,0:T(8,128)(2,1)S(1)}, u32[]{:S(2)}, u32[]{:S(2)}) %collective-permute-start.2) | collective-permute-done | bytes 368672 | tf_op jit(solution)/shard_map/ppermute | solution.py:487
  52.0 11.8 %all-to-all-start = ((bf16[32,96,1152]{2,1,0:T(8,128)(2,1)}), bf16[32,96,1152]{2,1,0:T(8,128)(2,1)}, u32[]{:S(2)}, u32[]{:S(2)}) async-start(bf16[32,96,1152]{2,1,0:T(8,128)(2,1)} %after.13), calls=%async_computation | async-start | bytes 14155776 | tf_op jit(solution)/shard_map/all_to_all | solution.py:477
  68.7 8.7 %collective-permute-done.4 = bf16[4,96,1920]{2,1,0:T(8,128)(2,1)} collective-permute-done((bf16[4,96,1920]{2,1,0:T(8,128)(2,1)S(1)}, bf16[4,96,1920]{2,1,0:T(8,128)(2,1)}, u32[]{:S(2)}, u32[]{:S(2)}) %collective-permute-start.4) | collective-permute-done | bytes 1474592 | tf_op jit(solution)/shard_map/ppermute | solution.py:500
  80.0 34.9 %collective-permute-done.5 = bf16[4,96,1920]{2,1,0:T(8,128)(2,1)} collective-permute-done((bf16[4,96,1920]{2,1,0:T(8,128)(2,1)S(1)}, bf16[4,96,1920]{2,1,0:T(8,128)(2,1)}, u32[]{:S(2)}, u32[]{:S(2)}) %collective-permute-start.5) | collective-permute-done | bytes 1474592 | tf_op jit(solution)/shard_map/ppermute | solution.py:500
  117.5 12.3 %collective-permute-done.6 = bf16[4,96,1920]{2,1,0:T(8,128)(2,1)} collective-permute-done((bf16[4,96,1920]{2,1,0:T(8,128)(2,1)S(1)}, bf16[4,96,1920]{2,1,0:T(8,128)(2,1)}, u32[]{:S(2)}, u32[]{:S(2)}) %collective-permute-start.6) | collective-permute-done | bytes 1474592 | tf_op jit(solution)/shard_map/ppermute | solution.py:500
  195.8 71.4 %all-to-all-done.refs_1_ = bf16[32,96,1152]{2,1,0:T(8,128)(2,1)} async-done(((bf16[32,96,1152]{2,1,0:T(8,128)(2,1)}), bf16[32,96,1152]{2,1,0:T(8,128)(2,1)}, u32[]{:S(2)}, u32[]{:S(2)}) %all-to-all-start) | async-done | bytes 7077920 | tf_op jit(solution)/shard_map/all_to_all | solution.py:477
  272.0 57.4 %all-gather.7.cloned.1.call-done = bf16[1024,1536]{1,0:T(8,128)(2,1)} async-done(((bf16[256,1536]{1,0:T(8,128)(2,1)}), bf16[1024,1536]{1,0:T(8,128)(2,1)}) %all-gather.7.cloned.1.call-update) | async-done | bytes 3145744 | tf_op jit(solution)/shard_map/all_gather | solution.py:532
  353.6 13.2 %expert_rows.4 = (bf16[384,1536]{1,0:T(8,128)(2,1)S(1)}, bf16[4,2,192,1536]{3,2,1,0:T(8,128)(2,1)S(1)}, bf16[384,1536]{1,0:T(8,128)(2,1)S(1)}, bf16[384,768]{1,0...) custom-call(s32[3]{0:T(128)S(1)} %pad_add_fusion.4.where_ref, ...), custom_call_target="tpu_custom_call" | custom-call | flops 5435817984 | bytes 7667712 | tf_op jit(solution)/shard_map/expert_rows/pallas_call | solution.py:645
  368.6 9.8 %collective-permute-done.12 = bf16[2,4,48,1536]{3,2,1,0:T(8,128)(2,1)S(1)} collective-permute-done((bf16[2,4,48,1536]{3,2,1,0:T(8,128)(2,1)S(1)}, bf16[2,4,48,1536]{3,2,1,0:T(8,128)(2,1)S(1)}, u32[]{:S(2)}, u32[]{:S(2)}) %collective-permute-start.12) | collective-permute-done | bytes 1179680 | tf_op jit(solution)/shard_map/ppermute | solution.py:543
  378.4 13.6 %expert_rows.5 = (bf16[384,1536]{1,0:T(8,128)(2,1)S(1)}, bf16[4,2,192,1536]{3,2,1,0:T(8,128)(2,1)S(1)}, bf16[384,1536]{1,0:T(8,128)(2,1)S(1)}, bf16[384,768]{1,0...) custom-call(s32[3]{0:T(128)S(1)} %pad_add_fusion.4.where_ref, ...), custom_call_target="tpu_custom_call", output_to_operand_aliasing={{1}: (5, {})} | custom-call | flops 5435817984 | bytes 7667712 | tf_op jit(solution)/shard_map/expert_rows/pallas_call | solution.py:645
  397.0 6.8 collective-permute-done.14
  403.9 14.4 %expert_rows.6 = (bf16[384,1536]{1,0:T(8,128)(2,1)}, bf16[4,2,192,1536]{3,2,1,0:T(8,128)(2,1)S(1)}, bf16[384,1536]{1,0:T(8,128)(2,1)S(1)}, bf16[384,768]{1,0:T(8...) custom-call(s32[3]{0:T(128)S(1)} %pad_add_fusion.4.where_ref, ...), custom_call_target="tpu_custom_call", output_to_operand_aliasing={{1}: (5, {})} | custom-call | flops 5435817984 | bytes 7667712 | tf_op jit(solution)/shard_map/expert_rows/pallas_call | solution.py:645
  433.8 13.6 %expert_rows.7 = (bf16[384,1536]{1,0:T(8,128)(2,1)S(1)}, bf16[4,2,192,1536]{3,2,1,0:T(8,128)(2,1)S(1)}, bf16[384,1536]{1,0:T(8,128)(2,1)S(1)}, bf16[384,768]{1,0...) custom-call(s32[3]{0:T(128)S(1)} %pad_add_fusion.4.where_ref, ...), custom_call_target="tpu_custom_call", output_to_operand_aliasing={{1}: (5, {})} | custom-call | flops 5435817984 | bytes 7667712 | tf_op jit(solution)/shard_map/expert_rows/pallas_call | solution.py:645
  463.0 7.8 shard_grad.2
  483.3 48.8 %collective-permute-done.16 = bf16[384,1536]{1,0:T(8,128)(2,1)S(1)} collective-permute-done((bf16[384,1536]{1,0:T(8,128)(2,1)S(1)}, bf16[384,1536]{1,0:T(8,128)(2,1)S(1)}, u32[]{:S(2)}, u32[]{:S(2)}) %collective-permute-start.16) | collective-permute-done | bytes 1179680 | tf_op jit(solution)/shard_map/ppermute | solution.py:543
  538.7 5.3 combine_rows.2
  551.7 5.4 add_convert_fusion.1.refs_1_
  562.9 13.2 %shard_grad.3 = bf16[16,2,96,768]{3,2,1,0:T(8,128)(2,1)} custom-call(bf16[384,1536]{1,0:T(8,128)(2,1)S(1)} %bitcast.237, bf16[384,1536]{1,0:T(8,128)(2,1)} %bitcast.239, bf16[384,1536]{1,0:T(8,128)(2,1)} %bitcast.242, bf16[384,1536]{1,0:T(8,128)(2,1)} %after.18.x_ref.refs_3_, bf16[384,768]{1,0:T(8,128)(2,1)S(1)} %copy-done.59, ...), custom_call_target="tpu_custom_call" | custom-call | flops 7247757312 | bytes 14155776 | tf_op jit(solution)/shard_map/shard_grad/pallas_call | solution.py:779
  576.1 29.1 %all-to-all-done.3.refs_0_.refs_1_ = bf16[8,4,48,1536]{3,2,1,0:T(8,128)(2,1)} async-done(((bf16[8,4,48,1536]{3,2,1,0:T(8,128)(2,1)}), bf16[8,4,48,1536]{3,2,1,0:T(8,128)(2,1)}, u32[]{:S(2)}, u32[]{:S(2)}) %all-to-all-start.3) | async-done | bytes 4718624 | tf_op jit(solution)/shard_map/all_to_all | solution.py:555
  606.0 5.6 combine_rows.3
  611.7 5.6 collective-permute-done.19
  642.2 6.2 multiply_reduce_fusion
  667.6 5.3 fusion.39
  674.4 6.4 fusion.5
  682.1 5.2 fusion.27
  688.3 8.4 %concatenate.154 = f32[4,2,2,96,896]{4,3,0,1,2:T(8,128)} concatenate(f32[4,2,2,96,768]{4,3,0,1,2:T(8,128)} %fusion.27, f32[4,2,2,96,32]{4,3,0,1,2:T(8,128)} %copy.141, f32[4,2,2,96,1]{4,3,0,1,2:T(8,128)} %copy.142, f32[4,2,2,96,1]{4,3,0,1,2:T(8,128)} %copy.143, f32[4,2,2,96,94]{4,3,0,1,2:T(8,128)} %broadcast_in_dim.47), dimensions={4} | concatenate | bytes 11010048 | tf_op jit(solution)/shard_map/concatenate | solution.py:1002
  714.8 31.6 %collective-permute-done.22 = bf16[4,2,96,896]{3,2,0,1:T(8,128)(2,1)} collective-permute-done((bf16[4,2,96,896]{3,2,0,1:T(8,128)(2,1)}, bf16[4,2,96,896]{3,2,0,1:T(8,128)(2,1)}, u32[]{:S(2)}, u32[]{:S(2)}) %collective-permute-start.22) | collective-permute-done | bytes 1376288 | tf_op jit(solution)/shard_map/ppermute | solution.py:516
  749.0 6.0 collective-permute-done.24
  760.0 12.5 %collective-permute-done.23 = bf16[4,96,896]{2,1,0:T(8,128)(2,1)S(1)} collective-permute-done((bf16[4,96,896]{2,1,0:T(8,128)(2,1)S(1)}, bf16[4,96,896]{2,1,0:T(8,128)(2,1)S(1)}, u32[]{:S(2)}, u32[]{:S(2)}) %collective-permute-start.23) | collective-permute-done | bytes 688160 | tf_op jit(solution)/shard_map/ppermute | solution.py:516
  773.8 7.8 collective-permute-done.25
  794.6 10.8 %all-to-all-done.4.refs_0_ = bf16[32,96,768]{2,1,0:T(8,128)(2,1)} async-done(((bf16[32,96,768]{2,1,0:T(8,128)(2,1)}), bf16[32,96,768]{2,1,0:T(8,128)(2,1)}, u32[]{:S(2)}, u32[]{:S(2)}) %all-to-all-start.4) | async-done | bytes 4718624 | tf_op jit(solution)/shard_map/all_to_all | solution.py:477
  805.4 7.4 slice_convert_fusion
  (515 shorter events, 296.9 us)
Async XLA Ops:
  7.2 176.5 %all-gather.5.cloned.1.call-start = ((), (), s32[]{:S(2)}) async-start(), calls=%async_computation.9 | async-start | bytes 3932160 | tf_op jit(solution)/shard_map/all_gather | solution.py:532
  11.5 14.7 %collective-permute-start.1 = (bf16[96,1920]{1,0:T(8,128)(2,1)S(1)}, bf16[96,1920]{1,0:T(8,128)(2,1)S(1)}, u32[]{:S(2)}, u32[]{:S(2)}) collective-permute-start(bf16[96,1920]{1,0:T(8,128)(2,1)S(1)} %concatenate.125), channel_id=1, source_target_pairs={{0,8},{2,10},{4,12},{6,14},{8,16},{10,18},{12,20},{14,22},{16,24},... | collective-permute-start | bytes 1105928 | tf_op jit(solution)/shard_map/ppermute | solution.py:487
  14.6 26.5 %collective-permute-start.2 = (bf16[96,1920]{1,0:T(8,128)(2,1)S(1)}, bf16[96,1920]{1,0:T(8,128)(2,1)S(1)}, u32[]{:S(2)}, u32[]{:S(2)}) collective-permute-start(bf16[96,1920]{1,0:T(8,128)(2,1)S(1)} %concatenate.125), channel_id=1, source_target_pairs={{0,16},{2,18},{4,20},{6,22},{8,24},{10,26},{12,28},{14,30},{16,0},... | collective-permute-start | bytes 1105928 | tf_op jit(solution)/shard_map/ppermute | solution.py:487
  17.2 24.0 %collective-permute-start.3 = (bf16[96,1920]{1,0:T(8,128)(2,1)S(1)}, bf16[96,1920]{1,0:T(8,128)(2,1)S(1)}, u32[]{:S(2)}, u32[]{:S(2)}) collective-permute-start(bf16[96,1920]{1,0:T(8,128)(2,1)S(1)} %concatenate.125), channel_id=1, source_target_pairs={{0,24},{2,26},{4,28},{6,30},{8,0},{10,2},{12,4},{14,6},{16,8},{18,... | collective-permute-start | bytes 1105928 | tf_op jit(solution)/shard_map/ppermute | solution.py:487
  18.5 48.6 %collective-permute-start = (bf16[256,1536]{1,0:T(8,128)(2,1)}, bf16[256,1536]{1,0:T(8,128)(2,1)}, u32[]{:S(2)}, u32[]{:S(2)}) collective-permute-start(bf16[256,1536]{1,0:T(8,128)(2,1)} %param.14), channel_id=1, source_target_pairs={{0,1},{1,0},{2,3},{3,2},{4,5},{5,4},{6,7},{7,6},{8,9},{9,8},{10,11... | collective-permute-start | bytes 2359304 | tf_op jit(solution)/shard_map/ppermute | solution.py:456
  41.4 35.9 %collective-permute-start.4 = (bf16[4,96,1920]{2,1,0:T(8,128)(2,1)S(1)}, bf16[4,96,1920]{2,1,0:T(8,128)(2,1)}, u32[]{:S(2)}, u32[]{:S(2)}) collective-permute-start(bf16[4,96,1920]{2,1,0:T(8,128)(2,1)S(1)} %pad_maximum_fusion.5.refs_1_), channel_id=1, source_target_pairs={{0,2},{2,0},{4,6},{6,4},{8,10},{10,8},{12,14},{14,12},{16,18},{18,... | collective-permute-start | bytes 4423688 | tf_op jit(solution)/shard_map/ppermute | solution.py:500
  43.0 72.0 %collective-permute-start.5 = (bf16[4,96,1920]{2,1,0:T(8,128)(2,1)S(1)}, bf16[4,96,1920]{2,1,0:T(8,128)(2,1)}, u32[]{:S(2)}, u32[]{:S(2)}) collective-permute-start(bf16[4,96,1920]{2,1,0:T(8,128)(2,1)S(1)} %pad_maximum_fusion.5.refs_1_), channel_id=1, source_target_pairs={{0,4},{2,6},{4,0},{6,2},{8,12},{10,14},{12,8},{14,10},{16,20},{18,... | collective-permute-start | bytes 4423688 | tf_op jit(solution)/shard_map/ppermute | solution.py:500
  44.5 85.4 %collective-permute-start.6 = (bf16[4,96,1920]{2,1,0:T(8,128)(2,1)S(1)}, bf16[4,96,1920]{2,1,0:T(8,128)(2,1)}, u32[]{:S(2)}, u32[]{:S(2)}) collective-permute-start(bf16[4,96,1920]{2,1,0:T(8,128)(2,1)S(1)} %pad_maximum_fusion.5.refs_1_), channel_id=1, source_target_pairs={{0,6},{2,4},{4,2},{6,0},{8,14},{10,12},{12,10},{14,8},{16,22},{18,... | collective-permute-start | bytes 4423688 | tf_op jit(solution)/shard_map/ppermute | solution.py:500
  52.0 215.3 %all-to-all-start = ((bf16[32,96,1152]{2,1,0:T(8,128)(2,1)}), bf16[32,96,1152]{2,1,0:T(8,128)(2,1)}, u32[]{:S(2)}, u32[]{:S(2)}) async-start(bf16[32,96,1152]{2,1,0:T(8,128)(2,1)} %after.13), calls=%async_computation | async-start | bytes 14155776 | tf_op jit(solution)/shard_map/all_to_all | solution.py:477
  63.8 265.6 %all-gather.7.cloned.1.call-start = ((), (), s32[]{:S(2)}) async-start(), calls=%async_computation.10 | async-start | bytes 3932160 | tf_op jit(solution)/shard_map/all_gather | solution.py:532
  267.3 63.6 %all-to-all-start.1 = ((bf16[8,4,48,1664]{3,2,1,0:T(8,128)(2,1)}), bf16[8,4,48,1664]{3,2,1,0:T(8,128)(2,1)}, u32[]{:S(2)}, u32[]{:S(2)}) async-start(bf16[8,4,48,1664]{3,2,1,0:T(8,128)(2,1)} %bitcast.228), calls=%async_computation.1 | async-start | bytes 10223616 | tf_op jit(solution)/shard_map/all_to_all | solution.py:555
  349.5 28.9 %collective-permute-start.12 = (bf16[2,4,48,1536]{3,2,1,0:T(8,128)(2,1)S(1)}, bf16[2,4,48,1536]{3,2,1,0:T(8,128)(2,1)S(1)}, u32[]{:S(2)}, u32[]{:S(2)}) collective-permute-start(bf16[2,4,48,1536]{3,2,1,0:T(8,128)(2,1)S(1)} %pad_maximum_fusion.7), channel_id=1, source_target_pairs={{0,2},{2,0},{4,6},{6,4},{8,10},{10,8},{12,14},{14,12},{16,18},{18,... | collective-permute-start | bytes 3538952 | tf_op jit(solution)/shard_map/ppermute | solution.py:543
  351.2 52.7 %collective-permute-start.14 = (bf16[2,4,48,1536]{3,2,1,0:T(8,128)(2,1)S(1)}, bf16[2,4,48,1536]{3,2,1,0:T(8,128)(2,1)S(1)}, u32[]{:S(2)}, u32[]{:S(2)}) collective-permute-start(bf16[2,4,48,1536]{3,2,1,0:T(8,128)(2,1)S(1)} %pad_maximum_fusion.9), channel_id=1, source_target_pairs={{0,4},{2,6},{4,0},{6,2},{8,12},{10,14},{12,8},{14,10},{16,20},{18,... | collective-permute-start | bytes 3538952 | tf_op jit(solution)/shard_map/ppermute | solution.py:543
  352.8 73.7 %collective-permute-start.11 = (bf16[2,4,48,1536]{3,2,1,0:T(8,128)(2,1)S(1)}, bf16[2,4,48,1536]{3,2,1,0:T(8,128)(2,1)S(1)}, u32[]{:S(2)}, u32[]{:S(2)}) collective-permute-start(bf16[2,4,48,1536]{3,2,1,0:T(8,128)(2,1)S(1)} %pad_maximum_fusion.6), channel_id=1, source_target_pairs={{0,6},{2,4},{4,2},{6,0},{8,14},{10,12},{12,10},{14,8},{16,22},{18,... | collective-permute-start | bytes 3538952 | tf_op jit(solution)/shard_map/ppermute | solution.py:543
  395.6 32.6 %collective-permute-start.13 = (bf16[384,1536]{1,0:T(8,128)(2,1)S(1)}, bf16[384,1536]{1,0:T(8,128)(2,1)S(1)}, u32[]{:S(2)}, u32[]{:S(2)}) collective-permute-start(bf16[384,1536]{1,0:T(8,128)(2,1)S(1)} %get-tuple-element.45), channel_id=1, source_target_pairs={{0,2},{2,0},{4,6},{6,4},{8,10},{10,8},{12,14},{14,12},{16,18},{18,... | collective-permute-start | bytes 3538952 | tf_op jit(solution)/shard_map/ppermute | solution.py:543
  424.6 30.3 %collective-permute-start.15 = (bf16[384,1536]{1,0:T(8,128)(2,1)}, bf16[384,1536]{1,0:T(8,128)(2,1)}, u32[]{:S(2)}, u32[]{:S(2)}) collective-permute-start(bf16[384,1536]{1,0:T(8,128)(2,1)} %get-tuple-element.53), channel_id=1, source_target_pairs={{0,4},{2,6},{4,0},{6,2},{8,12},{10,14},{12,8},{14,10},{16,20},{18,... | collective-permute-start | bytes 3538952 | tf_op jit(solution)/shard_map/ppermute | solution.py:543
  470.8 63.1 %all-to-all-start.2 = ((bf16[32,96,384]{2,1,0:T(8,128)(2,1)}), bf16[32,96,384]{2,1,0:T(8,128)(2,1)}, u32[]{:S(2)}, u32[]{:S(2)}) async-start(bf16[32,96,384]{2,1,0:T(8,128)(2,1)} %bitcast.264), calls=%async_computation.2 | async-start | bytes 4718592 | tf_op jit(solution)/shard_map/all_to_all | solution.py:477
  477.4 54.7 %collective-permute-start.16 = (bf16[384,1536]{1,0:T(8,128)(2,1)S(1)}, bf16[384,1536]{1,0:T(8,128)(2,1)S(1)}, u32[]{:S(2)}, u32[]{:S(2)}) collective-permute-start(bf16[384,1536]{1,0:T(8,128)(2,1)S(1)} %copy-done.31), channel_id=1, source_target_pairs={{0,6},{2,4},{4,2},{6,0},{8,14},{10,12},{12,10},{14,8},{16,22},{18,... | collective-permute-start | bytes 3538952 | tf_op jit(solution)/shard_map/ppermute | solution.py:543
  545.7 6.0 collective-permute-start.18
  545.8 59.4 %all-to-all-start.3 = ((bf16[8,4,48,1536]{3,2,1,0:T(8,128)(2,1)}), bf16[8,4,48,1536]{3,2,1,0:T(8,128)(2,1)}, u32[]{:S(2)}, u32[]{:S(2)}) async-start(bf16[8,4,48,1536]{3,2,1,0:T(8,128)(2,1)} %after.20), calls=%async_computation.3 | async-start | bytes 9437184 | tf_op jit(solution)/shard_map/all_to_all | solution.py:555
  550.4 69.4 %reduce-scatter.5.cloned.1.call-start = ((), (), s32[]{:S(2)}) async-start(), calls=%async_computation.8 | async-start | bytes 3932160 | tf_op jit(solution)/shard_map/reduce_scatter | solution.py:537
  627.2 8.2 collective-permute-start.20
  629.5 175.9 %all-to-all-start.4 = ((bf16[32,96,768]{2,1,0:T(8,128)(2,1)}), bf16[32,96,768]{2,1,0:T(8,128)(2,1)}, u32[]{:S(2)}, u32[]{:S(2)}) async-start(bf16[32,96,768]{2,1,0:T(8,128)(2,1)} %after.24), calls=%async_computation.6 | async-start | bytes 9437184 | tf_op jit(solution)/shard_map/all_to_all | solution.py:477
  633.6 156.2 %reduce-scatter.3.cloned.1.call-start = ((), (), s32[]{:S(2)}) async-start(), calls=%async_computation.7 | async-start | bytes 3932160 | tf_op jit(solution)/shard_map/reduce_scatter | solution.py:537
  699.9 46.5 %collective-permute-start.22 = (bf16[4,2,96,896]{3,2,0,1:T(8,128)(2,1)}, bf16[4,2,96,896]{3,2,0,1:T(8,128)(2,1)}, u32[]{:S(2)}, u32[]{:S(2)}) collective-permute-start(bf16[4,2,96,896]{3,2,0,1:T(8,128)(2,1)} %fusion.33), channel_id=1, source_target_pairs={{0,2},{2,0},{4,6},{6,4},{8,10},{10,8},{12,14},{14,12},{16,18},{18,... | collective-permute-start | bytes 4128776 | tf_op jit(solution)/shard_map/ppermute | solution.py:516
  706.2 48.9 %collective-permute-start.24 = (bf16[4,2,96,1024]{3,2,0,1:T(8,128)(2,1)}, bf16[4,2,96,1024]{3,2,0,1:T(8,128)(2,1)}, u32[]{:S(2)}, u32[]{:S(2)}) collective-permute-start(bf16[4,2,96,1024]{3,2,0,1:T(8,128)(2,1)} %fusion.24), channel_id=1, source_target_pairs={{0,4},{2,6},{4,0},{6,2},{8,12},{10,14},{12,8},{14,10},{16,20},{18,... | collective-permute-start | bytes 4718600 | tf_op jit(solution)/shard_map/ppermute | solution.py:516
  710.2 47.2 %collective-permute-start.21 = (f32[256,1536]{1,0:T(8,128)}, f32[256,1536]{1,0:T(8,128)}, u32[]{:S(2)}, u32[]{:S(2)}) collective-permute-start(f32[256,1536]{1,0:T(8,128)} %slice.311), channel_id=1, source_target_pairs={{0,1},{1,0},{2,3},{3,2},{4,5},{5,4},{6,7},{7,6},{8,9},{9,8},{10,11... | collective-permute-start | bytes 4718600 | tf_op jit(solution)/shard_map/ppermute | solution.py:456
  749.0 23.5 %collective-permute-start.23 = (bf16[4,96,896]{2,1,0:T(8,128)(2,1)S(1)}, bf16[4,96,896]{2,1,0:T(8,128)(2,1)S(1)}, u32[]{:S(2)}, u32[]{:S(2)}) collective-permute-start(bf16[4,96,896]{2,1,0:T(8,128)(2,1)S(1)} %fusion.55), channel_id=1, source_target_pairs={{0,4},{2,6},{4,0},{6,2},{8,12},{10,14},{12,8},{14,10},{16,20},{18,... | collective-permute-start | bytes 2064392 | tf_op jit(solution)/shard_map/ppermute | solution.py:516
  757.3 24.2 %collective-permute-start.25 = (bf16[4,96,1024]{2,1,0:T(8,128)(2,1)S(1)}, bf16[4,96,1024]{2,1,0:T(8,128)(2,1)S(1)}, u32[]{:S(2)}, u32[]{:S(2)}) collective-permute-start(bf16[4,96,1024]{2,1,0:T(8,128)(2,1)S(1)} %fusion.52), channel_id=1, source_target_pairs={{0,2},{2,0},{4,6},{6,4},{8,10},{10,8},{12,14},{14,12},{16,18},{18,... | collective-permute-start | bytes 2359304 | tf_op jit(solution)/shard_map/ppermute | solution.py:516
  782.8 30.0 %collective-permute-start.26 = (bf16[96,1920]{1,0:T(8,128)(2,1)}, bf16[96,1920]{1,0:T(8,128)(2,1)}, u32[]{:S(2)}, u32[]{:S(2)}) collective-permute-start(bf16[96,1920]{1,0:T(8,128)(2,1)} %pad_maximum_fusion.16), channel_id=1, source_target_pairs={{0,8},{2,10},{4,12},{6,14},{8,16},{10,18},{12,20},{14,22},{16,24},... | collective-permute-start | bytes 1105928 | tf_op jit(solution)/shard_map/ppermute | solution.py:487
  783.6 29.7 %collective-permute-start.27 = (bf16[96,1920]{1,0:T(8,128)(2,1)}, bf16[96,1920]{1,0:T(8,128)(2,1)}, u32[]{:S(2)}, u32[]{:S(2)}) collective-permute-start(bf16[96,1920]{1,0:T(8,128)(2,1)} %pad_maximum_fusion.17), channel_id=1, source_target_pairs={{0,16},{2,18},{4,20},{6,22},{8,24},{10,26},{12,28},{14,30},{16,0},... | collective-permute-start | bytes 1105928 | tf_op jit(solution)/shard_map/ppermute | solution.py:487
  788.9 24.3 %collective-permute-start.28 = (bf16[96,1920]{1,0:T(8,128)(2,1)}, bf16[96,1920]{1,0:T(8,128)(2,1)}, u32[]{:S(2)}, u32[]{:S(2)}) collective-permute-start(bf16[96,1920]{1,0:T(8,128)(2,1)} %pad_maximum_fusion.18), channel_id=1, source_target_pairs={{0,24},{2,26},{4,28},{6,30},{8,0},{10,2},{12,4},{14,6},{16,8},{18,... | collective-permute-start | bytes 1105928 | tf_op jit(solution)/shard_map/ppermute | solution.py:487
  (129 other events, 1164.8 us)
Sparse Core Ops, SparseCore 0:
  45.6 138.0 all-gather.4
  267.4 61.8 all-gather.6
  557.2 60.5 reduce-scatter.4
  636.4 109.4 reduce-scatter.2
